TPU v7x, 32 devices: a whole 2x2x4 slice. The times are simulated.
32 devices in a mesh: ha: 4 (over z), wa: 4 (over y, x), head: 2 (over core).
Axes of the slice: x: 2, y: 2, z: 4, core: 2. Of those that a mesh axis runs over, the one named last changes fastest.
Arguments:
- queries: bfloat16 [64, 64, 3072], P('ha', 'wa', 'head'), may hold values from -5 to 5
- keys_values: bfloat16 [64, 64, 2, 3072], P('ha', 'wa', None, 'head'), may hold values from -5 to 5
- ref_cache: bfloat16 [8, 128, 2, 3072], P('wa', None, None, 'head'), may hold values from -5 to 5
- ref_ids: int32 [4, 4, 2], P('ha'), may hold values from 0 to 7, as said below
- flags: int32 [64, 64], P('ha', 'wa'), may hold values from 0 to 1, as said below
- proj_weight: bfloat16 [3072, 3072], P('head'), may hold values from -0.15625 to 0.15625
Outputs:
- projected: bfloat16 [64, 64, 3072], P('ha', 'wa', 'head')
Inputs may be any that keep to these rules, and one draw needn't show every extreme that they name: `ref_ids`: the 2 ids of one tile give 2 different values of id // 2. `flags`: A tile of 16 x 16 tokens holds at most 64 flagged tokens, and some tile holds exactly 64.
All inputs are finite; a program needn't handle non-finite values.
Results may differ from a plain program's by a relative error of at most 0.0063.
Values may be sent and summed in bfloat16 or wider, within the bound.
No kernel may reach another device: no remote copies, remote signals or barrier semaphores. Data moves between devices by JAX's collectives and lax.ppermute only.
A program may use at most 128 MiB of HBM per device.

v0:
```python
import jax
import jax.numpy as jnp
from jax import lax
from jax.sharding import PartitionSpec as P

HD = 128
RADIUS = 16


def extended(cells, sides, width):
    for axis, dim in sides:
        count = lax.axis_size(axis)
        ends = count - 1
        head = lax.slice_in_dim(cells, 0, width, axis=dim)
        tail = lax.slice_in_dim(cells, cells.shape[dim] - width, cells.shape[dim], axis=dim)
        cells = jnp.concatenate(
            [
                lax.ppermute(tail, axis, [(i, (i + 1) % count) for i in range(ends)]),
                cells,
                lax.ppermute(head, axis, [((i + 1) % count, i) for i in range(ends)]),
            ],
            axis=dim,
        )
    return cells


def on_device(queries, keys_values, ref_cache, ref_ids, flags, proj_weight):
    tile_rows, tile_cols, channels = queries.shape
    head_count = channels // HD
    padded_rows = tile_rows + 2 * RADIUS
    padded_cols = tile_cols + 2 * RADIUS
    token_count = tile_rows * tile_cols
    score_scale = HD ** (-0.5)
    padded = extended(keys_values, (("ha", 0), ("wa", 1)), RADIUS)
    row_place = lax.axis_index("ha") * tile_rows - RADIUS + jnp.arange(padded_rows, dtype=jnp.int32)
    col_place = lax.axis_index("wa") * tile_cols - RADIUS + jnp.arange(padded_cols, dtype=jnp.int32)
    row_inside = (row_place >= 0) & (row_place < tile_rows * lax.axis_size("ha"))
    col_inside = (col_place >= 0) & (col_place < tile_cols * lax.axis_size("wa"))
    inside = row_inside[:, None] & col_inside[None, :]
    query_row = jnp.arange(tile_rows)[:, None, None, None]
    query_col = jnp.arange(tile_cols)[None, :, None, None]
    key_row = jnp.arange(padded_rows)[None, None, :, None]
    key_col = jnp.arange(padded_cols)[None, None, None, :]
    window = (jnp.abs(key_row - RADIUS - query_row) <= RADIUS) & (
        jnp.abs(key_col - RADIUS - query_col) <= RADIUS
    )
    window = (window & inside[None, None]).reshape(token_count, padded_rows * padded_cols)
    key_flat = padded[:, :, 0].reshape(padded_rows * padded_cols, channels)
    value_flat = padded[:, :, 1].reshape(padded_rows * padded_cols, channels)
    query_flat = queries.reshape(token_count, channels)
    flagged = flags.reshape(token_count) == 1
    wanted = ref_ids[0]
    my_blocks = lax.dynamic_index_in_dim(wanted, lax.axis_index("wa"), 0, keepdims=False)
    per_owner = ref_cache.shape[0]
    target = lax.axis_index("wa") * per_owner + jnp.arange(per_owner, dtype=jnp.int32)
    request_count = jnp.sum((wanted[:, :, None] == target[None, None, :]).astype(jnp.int32), axis=1)
    outgoing = jnp.einsum(
        "wr,rtkc->wtkc",
        request_count.astype(jnp.bfloat16),
        ref_cache,
        preferred_element_type=jnp.float32,
    ).astype(jnp.bfloat16)
    arrived = lax.all_to_all(outgoing, "wa", split_axis=0, concat_axis=0, tiled=True)
    picked = jnp.take(arrived, my_blocks // per_owner, axis=0)
    ref_keys = picked[:, :, 0].reshape(-1, channels)
    ref_values = picked[:, :, 1].reshape(-1, channels)
    head_outputs = []
    for head_index in range(head_count):
        first = head_index * HD
        head_query = query_flat[:, first : first + HD]
        scores = (
            jnp.einsum(
                "qc,kc->qk",
                head_query,
                key_flat[:, first : first + HD],
                preferred_element_type=jnp.float32,
            )
            * score_scale
        )
        scores = jnp.where(window, scores, -jnp.inf)
        row_max = jnp.max(scores, axis=1)
        ref_scores = (
            jnp.einsum(
                "qc,kc->qk",
                head_query,
                ref_keys[:, first : first + HD],
                preferred_element_type=jnp.float32,
            )
            * score_scale
        )
        ref_scores = jnp.where(flagged[:, None], ref_scores, -jnp.inf)
        row_max = jnp.maximum(row_max, jnp.max(ref_scores, axis=1))
        ref_probs = jnp.exp(ref_scores - row_max[:, None])
        ref_total = jnp.sum(ref_probs, axis=1)
        ref_part = jnp.dot(
            ref_probs.astype(jnp.bfloat16),
            ref_values[:, first : first + HD],
            preferred_element_type=jnp.float32,
        )
        probs = jnp.exp(scores - row_max[:, None])
        denominator = jnp.sum(probs, axis=1) + ref_total
        numerator = (
            jnp.dot(
                probs.astype(jnp.bfloat16),
                value_flat[:, first : first + HD],
                preferred_element_type=jnp.float32,
            )
            + ref_part
        )
        head_outputs.append(numerator / denominator[:, None])
    attended = jnp.concatenate(head_outputs, axis=1).astype(jnp.bfloat16)
    partial_term = jnp.dot(attended, proj_weight, preferred_element_type=jnp.float32).reshape(
        tile_rows, tile_cols, -1
    )
    return lax.psum_scatter(
        partial_term.astype(jnp.bfloat16), "head", scatter_dimension=2, tiled=True
    )


def solution(mesh):
    return jax.shard_map(
        on_device,
        mesh=mesh,
        in_specs=(
            P("ha", "wa", "head"),
            P("ha", "wa", None, "head"),
            P("wa", None, None, "head"),
            P("ha", None, None),
            P("ha", "wa"),
            P("head", None),
        ),
        out_specs=P("ha", "wa", "head"),
        check_vma=False,
    )
```

profile of v0, /device:TPU:0, one launch (start us, length us, event | category | flops | bytes accessed | tf_op | source)
XLA Modules:
  0.0 318.6 jit_solution(5779033536588266587)
XLA Ops:
  6.5 1.8 copy.25
  8.3 6.1 %collective-permute-start = (bf16[16,16,2,1536]{3,1,0,2:T(8,128)(2,1)S(1)}, bf16[16,16,2,1536]{3,1,0,2:T(8,128)(2,1)}, u32[]{:S(2)}, u32[]{:S(2)}) collective-permute-start(bf16[16,16,2,1536]{3,1,0,2:T(8,128)(2,1)S(1)} %copy.25), channel_id=1, source_target_pairs={{0,8},{8,16},{16,24},{1,9},{9,17},{17,25},{2,10},{10,18},{18,26},{... | collective-permute-start | bytes 4718600 | tf_op jit(solution)/shard_map/ppermute | solution.py:18
  14.4 1.3 collective-permute-start.1
  15.8 2.5 convolution_convert_fusion.1
  18.3 4.1 %copy.29 = bf16[4,128,2,1536]{3,2,1,0:T(2,128)(2,1)} copy(bf16[4,128,2,1536]{3,0,2,1:T(4,128)(2,1)S(1)} %convolution_convert_fusion.1) | data formatting | bytes 6291456 | tf_op jit(solution)/shard_map/convert_element_type | solution.py:62
  22.4 4.6 %all-to-all-start = ((bf16[4,128,2,1536]{3,2,1,0:T(2,128)(2,1)}), bf16[4,128,2,1536]{3,2,1,0:T(2,128)(2,1)}, u32[]{:S(2)}, u32[]{:S(2)}) async-start(bf16[4,128,2,1536]{3,2,1,0:T(2,128)(2,1)} %copy.29), calls=%async_computation | async-start | bytes 6291456 | tf_op jit(solution)/shard_map/all_to_all | solution.py:63
  27.1 0.8 broadcast_and_fusion
  27.9 19.0 %collective-permute-done = bf16[16,16,2,1536]{3,1,0,2:T(8,128)(2,1)} collective-permute-done((bf16[16,16,2,1536]{3,1,0,2:T(8,128)(2,1)S(1)}, bf16[16,16,2,1536]{3,1,0,2:T(8,128)(2,1)}, u32[]{:S(2)}, u32[]{:S(2)}) %collective-permute-start) | collective-permute-done | bytes 1572896 | tf_op jit(solution)/shard_map/ppermute | solution.py:18
  46.9 2.7 constant_dynamic-update-slice_fusion.2
  49.6 1.5 constant_dynamic-update-slice_fusion.1
  51.0 1.2 collective-permute-done.1
  52.3 2.7 constant_dynamic-update-slice_fusion
  54.9 1.3 collective-permute-start.3
  56.2 6.7 %collective-permute-start.2 = (bf16[48,16,2,1536]{3,1,0,2:T(8,128)(2,1)}, bf16[48,16,2,1536]{3,1,0,2:T(8,128)(2,1)}, u32[]{:S(2)}, u32[]{:S(2)}) collective-permute-start(bf16[48,16,2,1536]{3,1,0,2:T(8,128)(2,1)} %constant_dynamic-update-slice_fusion), channel_id=1, source_target_pairs={{0,2},{2,4},{4,6},{1,3},{3,5},{5,7},{8,10},{10,12},{12,14},{9,11},... | collective-permute-start | bytes 14155784 | tf_op jit(solution)/shard_map/ppermute | solution.py:18
  63.2 3.0 and.98
  66.2 0.7 copy.24
  67.3 4.1 %copy.30 = bf16[4,128,2,1536]{3,1,2,0:T(8,128)(2,1)} copy(bf16[4,128,2,1536]{3,2,1,0:T(2,128)(2,1)} %all-to-all-done) | data formatting | bytes 6291456 | tf_op jit(solution)/shard_map/all_to_all | solution.py:63
  71.3 2.5 gather_fusion
  74.2 1.0 copy-done.3
  75.7 0.2 fusion.384
  76.6 0.2 fusion.392
  77.9 87.8 %collective-permute-done.3 = bf16[48,16,2,1536]{3,1,0,2:T(8,128)(2,1)} collective-permute-done((bf16[48,16,2,1536]{3,1,0,2:T(8,128)(2,1)}, bf16[48,16,2,1536]{3,1,0,2:T(8,128)(2,1)}, u32[]{:S(2)}, u32[]{:S(2)}) %collective-permute-start.3) | collective-permute-done | bytes 4718624 | tf_op jit(solution)/shard_map/ppermute | solution.py:20
  165.7 7.2 %pad_maximum_fusion = bf16[48,48,2,1536]{3,1,0,2:T(8,128)(2,1)S(1)} fusion(bf16[48,16,2,1536]{3,1,0,2:T(8,128)(2,1)} %collective-permute-done.3, bf16[48,16,2,1536]{3,1,0,2:T(8,128)(2,1)} %constant_dynamic-update-slice_fusion, bf16[48,16,2,1536]{3,1,0,2:T(8,128)(2,1)} %collective-permute-done.2), kind=kLoop, calls=%fused_computation.1 | loop fusion | flops 42467328 | bytes 28311552 | tf_op jit(solution)/shard_map/concatenate | solution.py:16
  172.9 1.3 fusion.377
  174.2 0.7 fusion.379
  174.8 0.7 fusion.381
  176.1 0.7 fusion.383
  177.1 0.7 fusion.385
  178.1 0.7 fusion.387
  179.0 0.7 fusion.389
  180.0 0.7 fusion.391
  181.0 0.7 fusion.393
  181.9 0.7 fusion.395
  182.9 0.7 fusion.397
  183.9 0.7 fusion.399
  184.8 0.7 fusion.401
  185.8 0.4 fusion.24
  186.2 0.4 fusion.26
  186.6 0.4 fusion.28
  187.0 0.4 fusion.30
  187.4 0.4 fusion.32
  187.8 0.4 fusion.34
  188.2 0.6 fusion.36
  188.8 0.4 fusion.38
  189.2 0.4 fusion.40
  189.6 0.4 fusion.42
  190.0 0.4 fusion.44
  190.3 0.4 fusion.46
  190.9 0.5 fusion.238
  191.4 0.5 fusion.232
  192.0 0.5 fusion.226
  192.5 0.5 fusion.220
  193.0 0.5 fusion.214
  193.6 0.5 fusion.208
  194.1 0.5 fusion.202
  194.7 0.5 fusion.196
  195.3 0.5 fusion.190
  195.8 0.5 fusion.184
  196.4 0.5 fusion.178
  196.9 0.5 fusion.172
  197.5 0.3 slice-done.1
  197.7 0.2 slice-done.2
  198.0 3.8 %convolution_convert_fusion = bf16[256,3072]{1,0:T(8,128)(2,1)} fusion(bf16[256,1536]{0,1:T(8,128)(2,1)S(1)} %fusion.172, bf16[1536,3072]{1,0:T(8,128)(2,1)S(1)} %bitcast.103), kind=kOutput, calls=%fused_computation.38 | convolution fusion | flops 2416705536 | bytes 11796480 | tf_op jit(solution)/shard_map/dot_general | solution.py:112
  201.8 109.9 %reduce-scatter.2.cloned.1.call-done = bf16[16,16,1536]{2,1,0:T(8,128)(2,1)} async-done(((bf16[16,16,3072]{2,1,0:T(8,128)(2,1)}), bf16[16,16,1536]{2,1,0:T(8,128)(2,1)}) %reduce-scatter.2.cloned.1.call-update) | async-done | bytes 786448 | tf_op jit(solution)/shard_map/reduce_scatter | solution.py:115
  (97 shorter events, 6.9 us)
Async XLA Ops:
  6.5 9.3 %copy-start = (bf16[2,128,2,1536]{3,2,1,0:T(2,128)(2,1)S(1)}, bf16[2,128,2,1536]{3,2,1,0:T(2,128)(2,1)}, u32[]{:S(2)}) copy-start(bf16[2,128,2,1536]{3,2,1,0:T(2,128)(2,1)} %param.8) | copy-start | bytes 4718596
  6.5 9.2 %copy-start.5 = (s32[1,4,2]{1,2,0:T(2,128)S(1)}, s32[1,4,2]{1,2,0:T(2,128)}, u32[]{:S(2)}) copy-start(s32[1,4,2]{1,2,0:T(2,128)} %param.9) | copy-start | bytes 100
  8.3 38.6 %collective-permute-start = (bf16[16,16,2,1536]{3,1,0,2:T(8,128)(2,1)S(1)}, bf16[16,16,2,1536]{3,1,0,2:T(8,128)(2,1)}, u32[]{:S(2)}, u32[]{:S(2)}) collective-permute-start(bf16[16,16,2,1536]{3,1,0,2:T(8,128)(2,1)S(1)} %copy.25), channel_id=1, source_target_pairs={{0,8},{8,16},{16,24},{1,9},{9,17},{17,25},{2,10},{10,18},{18,26},{... | collective-permute-start | bytes 4718600 | tf_op jit(solution)/shard_map/ppermute | solution.py:18
  14.4 37.8 %collective-permute-start.1 = (bf16[16,16,2,1536]{3,1,0,2:T(8,128)(2,1)S(1)}, bf16[16,16,2,1536]{3,1,0,2:T(8,128)(2,1)}, u32[]{:S(2)}, u32[]{:S(2)}) collective-permute-start(bf16[16,16,2,1536]{3,1,0,2:T(8,128)(2,1)S(1)} %copy.25), channel_id=1, source_target_pairs={{8,0},{16,8},{24,16},{9,1},{17,9},{25,17},{10,2},{18,10},{26,18},{... | collective-permute-start | bytes 4718600 | tf_op jit(solution)/shard_map/ppermute | solution.py:20
  22.4 44.9 %all-to-all-start = ((bf16[4,128,2,1536]{3,2,1,0:T(2,128)(2,1)}), bf16[4,128,2,1536]{3,2,1,0:T(2,128)(2,1)}, u32[]{:S(2)}, u32[]{:S(2)}) async-start(bf16[4,128,2,1536]{3,2,1,0:T(2,128)(2,1)} %copy.29), calls=%async_computation | async-start | bytes 6291456 | tf_op jit(solution)/shard_map/all_to_all | solution.py:63
  27.0 284.7 %reduce-scatter.2.cloned.1.call-start = ((), (), s32[]{:S(2)}) async-start(), calls=%async_computation.2 | async-start | bytes 2359296 | tf_op jit(solution)/shard_map/reduce_scatter | solution.py:115
  27.1 22.5 %copy-start.2 = (bf16[16,16,2,1536]{3,2,1,0:T(2,128)(2,1)S(1)}, bf16[16,16,2,1536]{3,2,1,0:T(2,128)(2,1)}, u32[]{:S(2)}) copy-start(bf16[16,16,2,1536]{3,2,1,0:T(2,128)(2,1)} %param.7) | copy-start | bytes 4718596
  51.0 11.9 %copy-start.4 = (s32[16,16]{1,0:T(8,128)S(1)}, s32[16,16]{1,0:T(8,128)}, u32[]{:S(2)}) copy-start(s32[16,16]{1,0:T(8,128)} %param.10) | copy-start | bytes 3076
  54.9 110.8 %collective-permute-start.3 = (bf16[48,16,2,1536]{3,1,0,2:T(8,128)(2,1)}, bf16[48,16,2,1536]{3,1,0,2:T(8,128)(2,1)}, u32[]{:S(2)}, u32[]{:S(2)}) collective-permute-start(bf16[48,16,2,1536]{3,1,0,2:T(8,128)(2,1)} %constant_dynamic-update-slice_fusion), channel_id=1, source_target_pairs={{2,0},{4,2},{6,4},{3,1},{5,3},{7,5},{10,8},{12,10},{14,12},{11,9},... | collective-permute-start | bytes 14155784 | tf_op jit(solution)/shard_map/ppermute | solution.py:20
  56.2 109.5 %collective-permute-start.2 = (bf16[48,16,2,1536]{3,1,0,2:T(8,128)(2,1)}, bf16[48,16,2,1536]{3,1,0,2:T(8,128)(2,1)}, u32[]{:S(2)}, u32[]{:S(2)}) collective-permute-start(bf16[48,16,2,1536]{3,1,0,2:T(8,128)(2,1)} %constant_dynamic-update-slice_fusion), channel_id=1, source_target_pairs={{0,2},{2,4},{4,6},{1,3},{3,5},{5,7},{8,10},{10,12},{12,14},{9,11},... | collective-permute-start | bytes 14155784 | tf_op jit(solution)/shard_map/ppermute | solution.py:18
  74.1 1.1 copy-start.3
  194.1 3.3 %slice-start = ((s8[9437184]{0:T(1024)(128)(4,1)}), s8[4194304]{0:T(1024)(128)(4,1)S(1)}, s32[]{:S(2)}) async-start(s8[9437184]{0:T(1024)(128)(4,1)} %bitcast.102), calls=%async_computation.3 | async-start | bytes 8388608
  194.7 3.0 slice-start.1
  195.8 2.2 slice-start.2
  198.0 113.8 %copy-start.1 = (bf16[2,128,2,1536]{3,2,1,0:T(2,128)(2,1)S(1)}, bf16[2,128,2,1536]{3,2,1,0:T(2,128)(2,1)}, u32[]{:S(2)}) copy-start(bf16[2,128,2,1536]{3,2,1,0:T(2,128)(2,1)} %param.8) | copy-start | bytes 4718596
Sparse Core Ops, SparseCore 0:
  201.9 109.7 reduce-scatter.1
where the time goes:
time: 319 us
  waiting for transfers between devices  218 us (68%)
  local copies, waits for them, and re-layouts  26.4 us (8%)
  matrix products  25.9 us (8%)
  starting transfers between devices  20 us (6%)
  other arithmetic  14.2 us (4%)
  between operations  14 us (4%)
    reduce_scatter x1, waiting for transfers between devices, on_device(): lax.psum_scatter(partial_term.astype(jnp.bfloat16), 'head', scatter_dimen...  110 us
    ppermute x2, waiting for transfers between devices, extended(): lax.ppermute(head, axis, [((i + 1) % count, i) for i in range(ends)])  89.1 us
    ppermute x2, waiting for transfers between devices, extended(): lax.ppermute(tail, axis, [(i, (i + 1) % count) for i in range(ends)])  19 us
    ppermute x2, starting transfers between devices, extended(): lax.ppermute(tail, axis, [(i, (i + 1) % count) for i in range(ends)])  12.8 us
    dot_general x12, matrix products, on_device(): jnp.einsum('qc,kc->qk', head_query, key_flat[:, first:first + HD], prefer...  7.93 us
    unnamed x21, local copies, waits for them, and re-layouts  7.48 us
    concatenate x1, other arithmetic, extended(): jnp.concatenate([lax.ppermute(tail, axis, [(i, (i + 1) % count) for i in...  7.17 us
    dot_general x12, matrix products, on_device(): jnp.dot(probs.astype(jnp.bfloat16), value_flat[:, first:first + HD], pref...  6.47 us
  transfers between devices with their start and end apart: 6, of which 4 were waited for; matrix products, arithmetic and copies ran while one was open for 9% of the time, Pallas kernels for 0%

commit v1 on v0

--- a/solution.py
+++ b/solution.py
@@ -1,10 +1,16 @@
+import functools
+import math
+
 import jax
 import jax.numpy as jnp
 from jax import lax
+from jax.experimental import pallas as pl
+from jax.experimental.pallas import tpu as pltpu
 from jax.sharding import PartitionSpec as P
 
 HD = 128
 RADIUS = 16
+FAR = -131072.0
 
 
 def extended(cells, sides, width):
@@ -24,7 +30,7 @@
     return cells
 
 
-def on_device(queries, keys_values, ref_cache, ref_ids, flags, proj_weight):
+def by_tile(queries, keys_values, ref_cache, ref_ids, flags, proj_weight):
     tile_rows, tile_cols, channels = queries.shape
     head_count = channels // HD
     padded_rows = tile_rows + 2 * RADIUS
@@ -117,6 +123,164 @@
     )
 
 
+def attend_kernel(per_owner, ids_ref, q_ref, qf_ref, own_ref, up_ref, down_ref, ref_ref, kf_ref, o_ref, s_ref):
+    tiles, token_count, _ = q_ref.shape
+    block_tokens = ref_ref.shape[2] // per_owner
+    chosen_count = ids_ref.shape[1]
+    factor = HD ** (-0.5) * math.log2(math.e)
+    ones = jnp.ones((token_count, HD), jnp.bfloat16)
+    ones_block = jnp.ones((block_tokens, HD), jnp.bfloat16)
+    for w in range(tiles):
+        q_wide = jnp.concatenate([q_ref[w], qf_ref[w]], axis=1)
+        window = []
+        for other in range(max(w - 1, 0), min(w + 2, tiles)):
+            for r, source in enumerate((up_ref, own_ref, down_ref)):
+                window.append((source, other, r, other - w + 1))
+        at = 0
+        best = None
+        spans = []
+
+        def scored(keys, features, at, best):
+            wide = jnp.concatenate([keys, features], axis=1)
+            s = lax.dot_general(
+                q_wide, wide, (((1,), (1,)), ((), ())), preferred_element_type=jnp.float32
+            )
+            width = s.shape[1]
+            s_ref[:, at : at + width] = s
+            for part in range(0, width, HD):
+                piece = s[:, part : part + HD]
+                best = piece if best is None else jnp.maximum(best, piece)
+            return at + width, best
+
+        for source, other, r, c in window:
+            at, best = scored(source[other, 0], kf_ref[r, c], at, best)
+        picks = []
+        for n in range(chosen_count):
+            chosen = ids_ref[w, n]
+            owner = lax.div(chosen, per_owner)
+            start = pl.multiple_of(lax.rem(chosen, per_owner) * block_tokens, block_tokens)
+            picks.append((owner, start))
+            at, best = scored(
+                ref_ref[owner, 0, pl.ds(start, block_tokens)], kf_ref[3, 0, :block_tokens], at, best
+            )
+        row_max = jnp.max(best, axis=1, keepdims=True)
+        at = 0
+        total = jnp.zeros((token_count, 2 * HD), jnp.float32)
+
+        def weighed(values, at, total):
+            width = values.shape[0]
+            probs = jnp.exp2((s_ref[:, at : at + width] - row_max) * factor)
+            total = total + jnp.dot(
+                probs.astype(jnp.bfloat16), values, preferred_element_type=jnp.float32
+            )
+            return at + width, total
+
+        for source, other, r, c in window:
+            at, total = weighed(jnp.concatenate([source[other, 1], ones], axis=1), at, total)
+        for owner, start in picks:
+            at, total = weighed(
+                jnp.concatenate([ref_ref[owner, 1, pl.ds(start, block_tokens)], ones_block], axis=1),
+                at,
+                total,
+            )
+        o_ref[w] = (total[:, :HD] / total[:, HD:]).astype(jnp.bfloat16)
+
+
+def attend(per_owner, ids, q, q_features, own, up, down, ref, k_features):
+    tiles, token_count, _ = q.shape
+    key_count = 9 * token_count + ids.shape[1] * (ref.shape[2] // per_owner)
+    vmem = pl.BlockSpec(memory_space=pltpu.VMEM)
+    return pl.pallas_call(
+        functools.partial(attend_kernel, per_owner),
+        out_shape=jax.ShapeDtypeStruct(q.shape, jnp.bfloat16),
+        in_specs=[pl.BlockSpec(memory_space=pltpu.SMEM)] + [vmem] * 7,
+        out_specs=vmem,
+        scratch_shapes=[pltpu.VMEM((token_count, key_count), jnp.float32)],
+        compiler_params=pltpu.CompilerParams(vmem_limit_bytes=40 << 20),
+        name="attend",
+    )(ids, q, q_features, own, up, down, ref, k_features)
+
+
+def features(tile_rows, tile_cols, flags):
+    token_count = tile_rows * tile_cols
+    lane = lax.broadcasted_iota(jnp.int32, (token_count, HD), 1)
+    token = lax.broadcasted_iota(jnp.int32, (token_count, HD), 0)
+    row, col = token // tile_cols, token % tile_cols
+    row_lane = lane
+    col_lane = lane - tile_rows
+    is_row = lane < tile_rows
+    is_col = (lane >= tile_rows) & (lane < tile_rows + tile_cols)
+    is_flag = lane == tile_rows + tile_cols
+    hot = (is_row & (row_lane == row)) | (is_col & (col_lane == col))
+    q_features = jnp.where(
+        is_flag[None], (1 - flags)[:, :, None], hot.astype(jnp.int32)[None]
+    ).astype(jnp.bfloat16)
+    place = lax.axis_index("ha")
+    last = lax.axis_size("ha") - 1
+    row_far = [
+        is_row & ((row < row_lane) | (place == 0)),
+        jnp.zeros_like(is_row),
+        is_row & ((row > row_lane) | (place == last)),
+    ]
+    col_far = [is_col & (col < col_lane), jnp.zeros_like(is_col), is_col & (col > col_lane)]
+    zero = jnp.zeros_like(is_row)
+    table = [[row_far[r] | col_far[c] for c in range(3)] for r in range(3)] + [[is_flag, zero, zero]]
+    k_features = jnp.where(jnp.array(0) == 0, jnp.stack([jnp.stack(t) for t in table]), False)
+    return q_features, jnp.where(k_features, FAR, 0.0).astype(jnp.bfloat16)
+
+
+def by_head(queries, keys_values, ref_cache, ref_ids, flags, proj_weight):
+    tile_rows, tile_cols, channels = queries.shape
+    tiles = lax.axis_size("wa")
+    token_count = tile_rows * tile_cols
+    share = channels // HD // tiles
+    per_owner, block_tokens = ref_cache.shape[:2]
+    heights = lax.axis_size("ha")
+    kv = keys_values.reshape(token_count, 2, tiles, share, HD)
+    qs = queries.reshape(token_count, tiles, share, HD)
+    rc = ref_cache.reshape(per_owner * block_tokens, 2, tiles, share, HD)
+
+    def swap(x):
+        return lax.all_to_all(x, "wa", split_axis=0, concat_axis=0, tiled=True)
+
+    down_pairs = [(i, i + 1) for i in range(heights - 1)]
+    up_pairs = [(i + 1, i) for i in range(heights - 1)]
+    all_flags = lax.all_gather(flags.reshape(token_count), "wa", axis=0)
+    q_features, k_features = features(tile_rows, tile_cols, all_flags)
+    outs = []
+    for n in range(share):
+        own = swap(kv[:, :, :, n].transpose(2, 1, 0, 3))
+        up = lax.ppermute(own, "ha", down_pairs)
+        down = lax.ppermute(own, "ha", up_pairs)
+        q = swap(qs[:, :, n].transpose(1, 0, 2))
+        ref = swap(rc[:, :, :, n].transpose(2, 1, 0, 3))
+        out = attend(per_owner, ref_ids[0], q, q_features, own, up, down, ref, k_features)
+        outs.append(swap(out))
+    attended = jnp.stack(outs, axis=1).transpose(2, 0, 1, 3).reshape(token_count, channels)
+    half = proj_weight.shape[1] // 2
+    mine = lax.axis_index("head")
+    theirs = 1 - mine
+
+    def partial(which):
+        columns = lax.dynamic_slice_in_dim(proj_weight, which * half, half, 1)
+        return jnp.dot(attended, columns, preferred_element_type=jnp.float32).astype(jnp.bfloat16)
+
+    arrived = lax.ppermute(partial(theirs), "head", [(0, 1), (1, 0)])
+    total = partial(mine).astype(jnp.float32) + arrived.astype(jnp.float32)
+    return total.astype(jnp.bfloat16).reshape(tile_rows, tile_cols, half)
+
+
+def on_device(queries, *others):
+    head_count = queries.shape[2] // HD
+    fits = (
+        head_count % lax.axis_size("wa") == 0
+        and lax.axis_size("head") == 2
+        and queries.shape[0] == RADIUS
+        and queries.shape[1] == RADIUS
+    )
+    return (by_head if fits else by_tile)(queries, *others)
+
+
 def solution(mesh):
     return jax.shard_map(
         on_device,

time: 319 us -> 170 us (0.53)
  waiting for transfers between devices: 218 us -> 26.4 us
  starting transfers between devices: 20 us -> 66.6 us
  matrix products: 25.9 us -> 8.36 us
  Pallas kernels: 0 us -> 15.9 us
  between operations: 14 us -> 0.47 us
  local copies, waits for them, and re-layouts: 26.4 us -> 37.8 us
  other arithmetic: 14.2 us -> 4.11 us
  blocking collectives: 0 us -> 8.52 us
    reduce_scatter x1 -> x0, waiting for transfers between devices: 110 us -> none  [on_device(): lax.psum_scatter(partial_term.astype(jnp.bfloat16), 'head', scatter_dimen...]
    ppermute x4 -> x7, waiting for transfers between devices: 108 us -> 2.28 us  [the longest x1 2.27 us: by_head(): arrived = lax.ppermute(partial(theirs), 'head', [(0, 1), (1, 0)])]
    all_to_all x1 -> x12, starting transfers between devices: 4.63 us -> 48.3 us  [swap(): return lax.all_to_all(x, 'wa', split_axis=0, concat_axis=0, tiled=True)]
    all_to_all x1 -> x12, waiting for transfers between devices: 0.01 us -> 24.1 us  [swap(): return lax.all_to_all(x, 'wa', split_axis=0, concat_axis=0, tiled=True)]
    dot_general x50 -> x2, matrix products: 25.9 us -> 8.36 us  [partial(): jnp.dot(attended, columns, preferred_element_type=jnp.float32)]
    pallas_call x0 -> x3, Pallas kernels: none -> 15.9 us  [attend(): pl.pallas_call(functools.partial(attend_kernel, per_owner), out_shape=jax...]
    reshape x0 -> x3, local copies, waits for them, and re-layouts: none -> 13.1 us  [the longest x1 5.18 us: by_head(): kv = keys_values.reshape(token_count, 2, tiles, share, HD)]
    unnamed x21 -> x53, local copies, waits for them, and re-layouts: 7.48 us -> 16.2 us
  transfers between devices with their start and end apart: 6 -> 19, of which waited for: 4 -> 6; matrix products, arithmetic and copies ran while one was open for 9% -> 19% of each run, Pallas kernels for 0% -> 9%
where the time goes in v1:
time: 170 us; the launch traced here: 168 us
  starting transfers between devices  66.6 us (39%)
  local copies, waits for them, and re-layouts  37.8 us (22%)
  waiting for transfers between devices  26.4 us (16%)
  Pallas kernels  15.9 us (9%)
  blocking collectives  8.52 us (5%)
  matrix products  8.36 us (5%)
  other arithmetic  4.11 us (2%)
    all_to_all x12, starting transfers between devices, swap(): return lax.all_to_all(x, 'wa', split_axis=0, concat_axis=0, tiled=True)  48.3 us
    all_to_all x12, waiting for transfers between devices, swap(): return lax.all_to_all(x, 'wa', split_axis=0, concat_axis=0, tiled=True)  24.1 us
    unnamed x53, local copies, waits for them, and re-layouts  16.2 us
    pallas_call x3, Pallas kernels, attend(): pl.pallas_call(functools.partial(attend_kernel, per_owner), out_shape=jax...  15.9 us
    ppermute x3, starting transfers between devices, by_head(): up = lax.ppermute(own, 'ha', down_pairs)  14.2 us
    all_gather x1, blocking collectives, by_head(): all_flags = lax.all_gather(flags.reshape(token_count), 'wa', axis=0)  8.52 us
    dot_general x2, matrix products, partial(): jnp.dot(attended, columns, preferred_element_type=jnp.float32)  8.36 us
    reshape x1, local copies, waits for them, and re-layouts, by_head(): kv = keys_values.reshape(token_count, 2, tiles, share, HD)  5.18 us
  transfers between devices with their start and end apart: 19, of which 6 were waited for; matrix products, arithmetic and copies ran while one was open for 19% of the time, Pallas kernels for 9%

profile of v1, /device:TPU:0, one launch (start us, length us, event | category | flops | bytes accessed | tf_op | source)
XLA Modules:
  0.0 168.2 jit_solution(2463096142803296999)
XLA Ops:
  0.0 2.7 %reshape.1191 = bf16[256,4,3,128]{3,2,1,0:T(4,128)(2,1)S(1)} reshape(bf16[16,16,1536]{2,1,0:T(8,128)(2,1)} %param.6) | data formatting | bytes 1572864 | tf_op jit(solution)/shard_map/reshape | solution.py:240
  2.7 1.1 fusion.35
  3.9 0.7 copy.74
  4.6 5.2 %all-to-all-start = ((bf16[4,256,128]{2,1,0:T(8,128)(2,1)}), bf16[4,256,128]{2,1,0:T(8,128)(2,1)S(1)}, u32[]{:S(2)}, u32[]{:S(2)}) async-start(bf16[4,256,128]{2,1,0:T(8,128)(2,1)} %bitcast.65), calls=%async_computation | async-start | bytes 524288 | tf_op jit(solution)/shard_map/all_to_all | solution.py:244
  9.8 0.7 copy.73
  10.5 4.6 %all-to-all-done.q_ref = bf16[4,256,128]{2,1,0:T(8,128)(2,1)S(1)} async-done(((bf16[4,256,128]{2,1,0:T(8,128)(2,1)}), bf16[4,256,128]{2,1,0:T(8,128)(2,1)S(1)}, u32[]{:S(2)}, u32[]{:S(2)}) %all-to-all-start) | async-done | bytes 262176 | tf_op jit(solution)/shard_map/all_to_all | solution.py:244
  15.1 0.7 copy-done.2
  15.9 3.4 %all-to-all-start.4 = ((bf16[4,256,128]{2,1,0:T(8,128)(2,1)}), bf16[4,256,128]{2,1,0:T(8,128)(2,1)S(1)}, u32[]{:S(2)}, u32[]{:S(2)}) async-start(bf16[4,256,128]{2,1,0:T(8,128)(2,1)} %bitcast.64), calls=%async_computation.4 | async-start | bytes 524288 | tf_op jit(solution)/shard_map/all_to_all | solution.py:244
  19.3 5.2 %reshape.1201 = bf16[256,2,4,3,128]{4,3,2,1,0:T(4,128)(2,1)S(1)} reshape(bf16[16,16,2,1536]{3,2,1,0:T(2,128)(2,1)} %param.7) | data formatting | bytes 3145728 | tf_op jit(solution)/shard_map/reshape | solution.py:239
  24.5 0.7 copy.72
  25.2 4.2 %all-to-all-start.8 = ((bf16[4,256,128]{2,1,0:T(8,128)(2,1)}), bf16[4,256,128]{2,1,0:T(8,128)(2,1)S(1)}, u32[]{:S(2)}, u32[]{:S(2)}) async-start(bf16[4,256,128]{2,1,0:T(8,128)(2,1)} %bitcast.63), calls=%async_computation.8 | async-start | bytes 524288 | tf_op jit(solution)/shard_map/all_to_all | solution.py:244
  29.4 3.2 %fusion.34 = (bf16[256,2,4,1,128]{4,3,2,1,0:T(2,128)(2,1)S(1)}, bf16[256,2,4,1,128]{4,3,2,1,0:T(2,128)(2,1)}, bf16[256,2,4,1,128]{4,3,2,1,0:T(2,128)(2,1)}) fusion(bf16[256,2,4,3,128]{4,3,2,1,0:T(4,128)(2,1)S(1)} %reshape.1201), kind=kLoop, calls=%fused_computation.61 | loop fusion | bytes 3145728 | tf_op jit(solution)/shard_map/slice | solution.py:252
  32.5 1.0 copy.71
  33.5 5.2 %reshape.1202 = bf16[256,2,4,3,128]{4,3,2,1,0:T(4,128)(2,1)S(1)} reshape(bf16[2,128,2,1536]{3,2,1,0:T(2,128)(2,1)} %param.8) | data formatting | bytes 3145728 | tf_op jit(solution)/shard_map/reshape | solution.py:241
  38.7 4.2 %all-to-all-start.1 = ((bf16[4,2,256,128]{3,2,1,0:T(8,128)(2,1)}), bf16[4,2,256,128]{3,2,1,0:T(8,128)(2,1)S(1)}, u32[]{:S(2)}, u32[]{:S(2)}) async-start(bf16[4,2,256,128]{3,2,1,0:T(8,128)(2,1)} %bitcast.62), calls=%async_computation.1 | async-start | bytes 1048576 | tf_op jit(solution)/shard_map/all_to_all | solution.py:244
  42.9 3.2 %fusion.33 = (bf16[256,2,4,1,128]{4,3,2,1,0:T(2,128)(2,1)S(1)}, bf16[256,2,4,1,128]{4,3,2,1,0:T(2,128)(2,1)}, bf16[256,2,4,1,128]{4,3,2,1,0:T(2,128)(2,1)}) fusion(bf16[256,2,4,3,128]{4,3,2,1,0:T(4,128)(2,1)S(1)} %reshape.1202), kind=kLoop, calls=%fused_computation.60 | loop fusion | bytes 3145728 | tf_op jit(solution)/shard_map/slice | solution.py:256
  46.1 1.0 copy.70
  47.1 2.4 %all-to-all-done.1.own_ref = bf16[4,2,256,128]{3,2,1,0:T(8,128)(2,1)S(1)} async-done(((bf16[4,2,256,128]{3,2,1,0:T(8,128)(2,1)}), bf16[4,2,256,128]{3,2,1,0:T(8,128)(2,1)S(1)}, u32[]{:S(2)}, u32[]{:S(2)}) %all-to-all-start.1) | async-done | bytes 524320 | tf_op jit(solution)/shard_map/all_to_all | solution.py:244
  49.5 3.5 %all-to-all-start.2 = ((bf16[4,2,256,128]{3,2,1,0:T(8,128)(2,1)}), bf16[4,2,256,128]{3,2,1,0:T(8,128)(2,1)S(1)}, u32[]{:S(2)}, u32[]{:S(2)}) async-start(bf16[4,2,256,128]{3,2,1,0:T(8,128)(2,1)} %bitcast.61), calls=%async_computation.2 | async-start | bytes 1048576 | tf_op jit(solution)/shard_map/all_to_all | solution.py:244
  53.0 1.0 copy.69
  54.1 5.5 %all-to-all-done.2.ref_ref = bf16[4,2,256,128]{3,2,1,0:T(8,128)(2,1)S(1)} async-done(((bf16[4,2,256,128]{3,2,1,0:T(8,128)(2,1)}), bf16[4,2,256,128]{3,2,1,0:T(8,128)(2,1)S(1)}, u32[]{:S(2)}, u32[]{:S(2)}) %all-to-all-start.2) | async-done | bytes 524320 | tf_op jit(solution)/shard_map/all_to_all | solution.py:244
  59.5 3.5 %all-to-all-start.5 = ((bf16[4,2,256,128]{3,2,1,0:T(8,128)(2,1)}), bf16[4,2,256,128]{3,2,1,0:T(8,128)(2,1)S(1)}, u32[]{:S(2)}, u32[]{:S(2)}) async-start(bf16[4,2,256,128]{3,2,1,0:T(8,128)(2,1)} %bitcast.70), calls=%async_computation.5 | async-start | bytes 1048576 | tf_op jit(solution)/shard_map/all_to_all | solution.py:244
  63.0 0.1 reshape.1196
  63.1 2.2 %copy.68 = bf16[256,2,4,1,128]{4,0,1,2,3:T(8,128)(2,1)} copy(bf16[256,2,4,1,128]{4,3,2,1,0:T(2,128)(2,1)} %get-tuple-element.6) | data formatting | bytes 1048576
  65.3 8.5 %all-gather = s32[4,1,256]{2,1,0:T(1,128)S(1)} all-gather(s32[1,1,256]{2,1,0:T(1,128)S(1)} %reshape.1196), channel_id=1, replica_groups=mesh['ha'=4,'wa'=4,'head'=2] {'wa'}, dimensions={0}, use_global_device_ids=true | all-gather | bytes 5120 | tf_op jit(solution)/shard_map/all_gather | solution.py:248
  73.9 0.3 fusion.15
  74.2 0.2 copy-done.11
  74.5 3.5 %all-to-all-start.6 = ((bf16[4,2,256,128]{3,2,1,0:T(8,128)(2,1)}), bf16[4,2,256,128]{3,2,1,0:T(8,128)(2,1)S(1)}, u32[]{:S(2)}, u32[]{:S(2)}) async-start(bf16[4,2,256,128]{3,2,1,0:T(8,128)(2,1)} %bitcast.69), calls=%async_computation.6 | async-start | bytes 1048576 | tf_op jit(solution)/shard_map/all_to_all | solution.py:244
  78.0 1.0 copy.67
  79.0 0.2 select_convert_fusion.1.qf_ref
  79.2 6.2 %all-to-all-done.6.ref_ref = bf16[4,2,256,128]{3,2,1,0:T(8,128)(2,1)S(1)} async-done(((bf16[4,2,256,128]{3,2,1,0:T(8,128)(2,1)}), bf16[4,2,256,128]{3,2,1,0:T(8,128)(2,1)S(1)}, u32[]{:S(2)}, u32[]{:S(2)}) %all-to-all-start.6) | async-done | bytes 524320 | tf_op jit(solution)/shard_map/all_to_all | solution.py:244
  85.4 4.3 %all-to-all-start.9 = ((bf16[4,2,256,128]{3,2,1,0:T(8,128)(2,1)}), bf16[4,2,256,128]{3,2,1,0:T(8,128)(2,1)}, u32[]{:S(2)}, u32[]{:S(2)}) async-start(bf16[4,2,256,128]{3,2,1,0:T(8,128)(2,1)} %bitcast.68), calls=%async_computation.9 | async-start | bytes 1048576 | tf_op jit(solution)/shard_map/all_to_all | solution.py:244
  89.7 1.0 fusion.32
  90.7 3.5 %collective-permute-start = (bf16[4,2,256,128]{3,2,1,0:T(8,128)(2,1)S(1)}, bf16[4,2,256,128]{3,2,1,0:T(8,128)(2,1)S(1)}, u32[]{:S(2)}, u32[]{:S(2)}) collective-permute-start(bf16[4,2,256,128]{3,2,1,0:T(8,128)(2,1)S(1)} %all-to-all-done.1.own_ref), channel_id=1, source_target_pairs={{0,8},{8,16},{16,24},{1,9},{9,17},{17,25},{2,10},{10,18},{18,26},{... | collective-permute-start | bytes 1572872 | tf_op jit(solution)/shard_map/ppermute | solution.py:253
  94.2 0.7 broadcast_in_dim.42
  94.9 1.3 collective-permute-start.1
  96.2 0.6 add_bitcast_fusion
  96.9 2.2 %copy.66 = bf16[256,2,4,1,128]{4,0,1,2,3:T(8,128)(2,1)} copy(bf16[256,2,4,1,128]{4,3,2,1,0:T(2,128)(2,1)} %get-tuple-element.7) | data formatting | bytes 1048576
  99.1 4.1 %all-to-all-start.10 = ((bf16[4,2,256,128]{3,2,1,0:T(8,128)(2,1)}), bf16[4,2,256,128]{3,2,1,0:T(8,128)(2,1)}, u32[]{:S(2)}, u32[]{:S(2)}) async-start(bf16[4,2,256,128]{3,2,1,0:T(8,128)(2,1)} %bitcast.67), calls=%async_computation.10 | async-start | bytes 1048576 | tf_op jit(solution)/shard_map/all_to_all | solution.py:244
  103.2 0.6 add_bitcast_fusion.2
  103.9 0.1 copy.32.ids_ref
  104.0 5.3 %collective-permute-start.2 = (bf16[4,2,256,128]{3,2,1,0:T(8,128)(2,1)S(1)}, bf16[4,2,256,128]{3,2,1,0:T(8,128)(2,1)}, u32[]{:S(2)}, u32[]{:S(2)}) collective-permute-start(bf16[4,2,256,128]{3,2,1,0:T(8,128)(2,1)S(1)} %all-to-all-done.5.own_ref), channel_id=1, source_target_pairs={{0,8},{8,16},{16,24},{1,9},{9,17},{17,25},{2,10},{10,18},{18,26},{... | collective-permute-start | bytes 1572872 | tf_op jit(solution)/shard_map/ppermute | solution.py:253
  109.4 1.3 collective-permute-start.3
  110.7 0.1 add_bitcast_fusion.1
  110.8 5.4 %collective-permute-start.4 = (bf16[4,2,256,128]{3,2,1,0:T(8,128)(2,1)}, bf16[4,2,256,128]{3,2,1,0:T(8,128)(2,1)}, u32[]{:S(2)}, u32[]{:S(2)}) collective-permute-start(bf16[4,2,256,128]{3,2,1,0:T(8,128)(2,1)} %all-to-all-done.9.own_ref), channel_id=1, source_target_pairs={{0,8},{8,16},{16,24},{1,9},{9,17},{17,25},{2,10},{10,18},{18,26},{... | collective-permute-start | bytes 1572872 | tf_op jit(solution)/shard_map/ppermute | solution.py:253
  116.1 0.8 copy-done.5
  116.9 1.5 collective-permute-start.5
  118.4 1.2 select_convert_fusion.kf_ref
  119.6 0.9 copy-done.3
  120.5 1.0 copy-done.6
  121.6 4.6 %attend.3 = bf16[4,256,128]{2,1,0:T(8,128)(2,1)S(1)} custom-call(s32[4,2]{1,0:T(4,128)S(1)} %copy.32.ids_ref, bf16[4,256,128]{2,1,0:T(8,128)(2,1)S(1)} %copy-done.3, bf16[4,256,128]{2,1,0:T(8,128)(2,1)S(1)} %select_convert_fusion.1.qf_ref, bf16[4,2,256,128]{3,2,1,0:T(8,128)(2,1)S(1)} %all-to-all-done.1.own_ref, bf16[4,2,256,128]{3,2,1,0:T(8,128)(2,1)S(1)} %copy-done.6, ...), custom_call_target="tpu_custom_call" | custom-call | tf_op jit(solution)/shard_map/attend/pallas_call | solution.py:193
  126.2 0.7 copy-done.4
  126.9 4.2 %all-to-all-start.3 = ((bf16[4,256,128]{2,1,0:T(8,128)(2,1)}), bf16[4,256,128]{2,1,0:T(8,128)(2,1)S(1)}, u32[]{:S(2)}, u32[]{:S(2)}) async-start(bf16[4,256,128]{2,1,0:T(8,128)(2,1)} %copy-done.4), calls=%async_computation.3 | async-start | bytes 524288 | tf_op jit(solution)/shard_map/all_to_all | solution.py:244
  131.1 0.9 copy-done.1
  132.0 5.5 %attend.4 = bf16[4,256,128]{2,1,0:T(8,128)(2,1)} custom-call(s32[4,2]{1,0:T(4,128)S(1)} %copy.32.ids_ref, bf16[4,256,128]{2,1,0:T(8,128)(2,1)S(1)} %copy-done.1, bf16[4,256,128]{2,1,0:T(8,128)(2,1)S(1)} %select_convert_fusion.1.qf_ref, bf16[4,2,256,128]{3,2,1,0:T(8,128)(2,1)S(1)} %all-to-all-done.5.own_ref, ...), custom_call_target="tpu_custom_call" | custom-call | tf_op jit(solution)/shard_map/attend/pallas_call | solution.py:193
  137.5 4.2 %all-to-all-start.7 = ((bf16[4,256,128]{2,1,0:T(8,128)(2,1)}), bf16[4,256,128]{2,1,0:T(8,128)(2,1)S(1)}, u32[]{:S(2)}, u32[]{:S(2)}) async-start(bf16[4,256,128]{2,1,0:T(8,128)(2,1)} %attend.4), calls=%async_computation.7 | async-start | bytes 524288 | tf_op jit(solution)/shard_map/all_to_all | solution.py:244
  141.7 5.8 %attend.5 = bf16[4,256,128]{2,1,0:T(8,128)(2,1)} custom-call(s32[4,2]{1,0:T(4,128)S(1)} %copy.32.ids_ref, bf16[4,256,128]{2,1,0:T(8,128)(2,1)S(1)} %all-to-all-done.8.q_ref, bf16[4,256,128]{2,1,0:T(8,128)(2,1)S(1)} %select_convert_fusion.1.qf_ref, bf16[4,2,256,128]{3,2,1,0:T(8,128)(2,1)} %all-to-all-done.9.own_ref, ...), custom_call_target="tpu_custom_call" | custom-call | tf_op jit(solution)/shard_map/attend/pallas_call | solution.py:193
  147.5 4.2 %all-to-all-start.11 = ((bf16[4,256,128]{2,1,0:T(8,128)(2,1)}), bf16[4,256,128]{2,1,0:T(8,128)(2,1)S(1)}, u32[]{:S(2)}, u32[]{:S(2)}) async-start(bf16[4,256,128]{2,1,0:T(8,128)(2,1)} %attend.5), calls=%async_computation.11 | async-start | bytes 524288 | tf_op jit(solution)/shard_map/all_to_all | solution.py:244
  151.7 5.4 %all-to-all-done.11 = bf16[4,256,128]{2,1,0:T(8,128)(2,1)S(1)} async-done(((bf16[4,256,128]{2,1,0:T(8,128)(2,1)}), bf16[4,256,128]{2,1,0:T(8,128)(2,1)S(1)}, u32[]{:S(2)}, u32[]{:S(2)}) %all-to-all-start.11) | async-done | bytes 262176 | tf_op jit(solution)/shard_map/all_to_all | solution.py:244
  157.1 0.1 maximum_bitcast_fusion
  157.2 0.3 copy.41
  157.5 3.7 %fusion.10 = bf16[256,1536]{1,0:T(8,128)(2,1)S(1)} fusion(bf16[256,1536]{0,1:T(8,128)(2,1)S(1)} %bitcast.74, bf16[1536,3072]{1,0:T(8,128)(2,1)} %param.11, s32[]{:T(128)S(6)} %select_n.113), kind=kOutput, calls=%fused_computation.6 | convolution fusion | flops 1208352768 | bytes 6291460 | tf_op jit(solution)/shard_map/dot_general | solution.py:266
  161.3 2.3 %collective-permute-done.6 = bf16[256,1536]{1,0:T(8,128)(2,1)S(1)} collective-permute-done((bf16[256,1536]{1,0:T(8,128)(2,1)S(1)}, bf16[256,1536]{1,0:T(8,128)(2,1)S(1)}, u32[]{:S(2)}, u32[]{:S(2)}) %collective-permute-start.6) | collective-permute-done | bytes 786464 | tf_op jit(solution)/shard_map/ppermute | solution.py:268
  163.6 4.6 %add_convert_fusion = bf16[256,1536]{1,0:T(8,128)(2,1)} fusion(bf16[256,1536]{1,0:T(8,128)(2,1)S(1)} %collective-permute-done.6, bf16[256,1536]{0,1:T(8,128)(2,1)S(1)} %bitcast.75, bf16[1536,3072]{1,0:T(8,128)(2,1)} %param.11, s32[]{:T(128)S(6)} %select_n.112), kind=kOutput, calls=%fused_computation.7 | convolution fusion | flops 1209925632 | bytes 7077892 | tf_op jit(solution)/shard_map/dot_general | solution.py:266
  (59 shorter events, 0.3 us)
Async XLA Ops:
  4.6 10.5 %all-to-all-start = ((bf16[4,256,128]{2,1,0:T(8,128)(2,1)}), bf16[4,256,128]{2,1,0:T(8,128)(2,1)S(1)}, u32[]{:S(2)}, u32[]{:S(2)}) async-start(bf16[4,256,128]{2,1,0:T(8,128)(2,1)} %bitcast.65), calls=%async_computation | async-start | bytes 524288 | tf_op jit(solution)/shard_map/all_to_all | solution.py:244
  15.1 0.7 copy-start.2
  15.9 9.4 %all-to-all-start.4 = ((bf16[4,256,128]{2,1,0:T(8,128)(2,1)}), bf16[4,256,128]{2,1,0:T(8,128)(2,1)S(1)}, u32[]{:S(2)}, u32[]{:S(2)}) async-start(bf16[4,256,128]{2,1,0:T(8,128)(2,1)} %bitcast.64), calls=%async_computation.4 | async-start | bytes 524288 | tf_op jit(solution)/shard_map/all_to_all | solution.py:244
  25.2 7.3 %copy-start = (bf16[4,256,128]{2,1,0:T(8,128)(2,1)}, bf16[4,256,128]{2,1,0:T(8,128)(2,1)S(1)}, u32[]{:S(2)}) copy-start(bf16[4,256,128]{2,1,0:T(8,128)(2,1)S(1)} %all-to-all-done.4.q_ref) | copy-start | bytes 786436
  25.2 13.5 %all-to-all-start.8 = ((bf16[4,256,128]{2,1,0:T(8,128)(2,1)}), bf16[4,256,128]{2,1,0:T(8,128)(2,1)S(1)}, u32[]{:S(2)}, u32[]{:S(2)}) async-start(bf16[4,256,128]{2,1,0:T(8,128)(2,1)} %bitcast.63), calls=%async_computation.8 | async-start | bytes 524288 | tf_op jit(solution)/shard_map/all_to_all | solution.py:244
  38.7 10.8 %all-to-all-start.1 = ((bf16[4,2,256,128]{3,2,1,0:T(8,128)(2,1)}), bf16[4,2,256,128]{3,2,1,0:T(8,128)(2,1)S(1)}, u32[]{:S(2)}, u32[]{:S(2)}) async-start(bf16[4,2,256,128]{3,2,1,0:T(8,128)(2,1)} %bitcast.62), calls=%async_computation.1 | async-start | bytes 1048576 | tf_op jit(solution)/shard_map/all_to_all | solution.py:244
  46.1 6.9 %copy-start.8 = (bf16[256,2,4,1,128]{4,3,2,1,0:T(2,128)(2,1)S(1)}, bf16[256,2,4,1,128]{4,3,2,1,0:T(2,128)(2,1)}, u32[]{:S(2)}) copy-start(bf16[256,2,4,1,128]{4,3,2,1,0:T(2,128)(2,1)} %get-tuple-element.9) | copy-start | bytes 1572868
  47.1 15.9 %copy-start.13 = (s32[16,16]{1,0:T(8,128)S(1)}, s32[16,16]{1,0:T(8,128)}, u32[]{:S(2)}) copy-start(s32[16,16]{1,0:T(8,128)} %param.10) | copy-start | bytes 3076
  49.5 10.0 %all-to-all-start.2 = ((bf16[4,2,256,128]{3,2,1,0:T(8,128)(2,1)}), bf16[4,2,256,128]{3,2,1,0:T(8,128)(2,1)S(1)}, u32[]{:S(2)}, u32[]{:S(2)}) async-start(bf16[4,2,256,128]{3,2,1,0:T(8,128)(2,1)} %bitcast.61), calls=%async_computation.2 | async-start | bytes 1048576 | tf_op jit(solution)/shard_map/all_to_all | solution.py:244
  54.0 24.0 %copy-start.7 = (bf16[256,2,4,1,128]{4,3,2,1,0:T(2,128)(2,1)S(1)}, bf16[256,2,4,1,128]{4,3,2,1,0:T(2,128)(2,1)}, u32[]{:S(2)}) copy-start(bf16[256,2,4,1,128]{4,3,2,1,0:T(2,128)(2,1)} %get-tuple-element.10) | copy-start | bytes 1572868
  54.0 20.2 %copy-start.14 = (pred[256]{0:T(512)(128)(4,1)}, pred[256]{0:T(512)(128)(4,1)S(1)}, u32[]{:S(2)}) copy-start(pred[256]{0:T(512)(128)(4,1)S(1)} %get-tuple-element.24) | copy-start | bytes 772
  54.0 20.2 %copy-start.15 = (pred[256]{0:T(512)(128)(4,1)}, pred[256]{0:T(512)(128)(4,1)S(1)}, u32[]{:S(2)}) copy-start(pred[256]{0:T(512)(128)(4,1)S(1)} %get-tuple-element.25) | copy-start | bytes 772
  54.0 20.1 %copy-start.16 = (pred[128]{0:T(512)(128)(4,1)}, pred[128]{0:T(512)(128)(4,1)S(1)}, u32[]{:S(2)}) copy-start(pred[128]{0:T(512)(128)(4,1)S(1)} %get-tuple-element.26) | copy-start | bytes 388
  54.0 20.1 %copy-start.17 = (pred[128]{0:T(512)(128)(4,1)}, pred[128]{0:T(512)(128)(4,1)S(1)}, u32[]{:S(2)}) copy-start(pred[128]{0:T(512)(128)(4,1)S(1)} %get-tuple-element.27) | copy-start | bytes 388
  59.5 14.6 %all-to-all-start.5 = ((bf16[4,2,256,128]{3,2,1,0:T(8,128)(2,1)}), bf16[4,2,256,128]{3,2,1,0:T(8,128)(2,1)S(1)}, u32[]{:S(2)}, u32[]{:S(2)}) async-start(bf16[4,2,256,128]{3,2,1,0:T(8,128)(2,1)} %bitcast.70), calls=%async_computation.5 | async-start | bytes 1048576 | tf_op jit(solution)/shard_map/all_to_all | solution.py:244
  63.0 11.2 %copy-start.18 = (s32[128]{0:T(128)}, s32[128]{0:T(128)S(1)}, u32[]{:S(2)}) copy-start(s32[128]{0:T(128)S(1)} %iota_add_fusion) | copy-start | bytes 1540
  73.9 0.5 copy-start.11
  73.9 0.6 copy-start.9
  74.5 11.0 %all-to-all-start.6 = ((bf16[4,2,256,128]{3,2,1,0:T(8,128)(2,1)}), bf16[4,2,256,128]{3,2,1,0:T(8,128)(2,1)S(1)}, u32[]{:S(2)}, u32[]{:S(2)}) async-start(bf16[4,2,256,128]{3,2,1,0:T(8,128)(2,1)} %bitcast.69), calls=%async_computation.6 | async-start | bytes 1048576 | tf_op jit(solution)/shard_map/all_to_all | solution.py:244
  77.9 11.8 %copy-start.10 = (s32[256]{0:T(256)S(1)}, s32[256]{0:T(256)}, u32[]{:S(2)}) copy-start(s32[256]{0:T(256)} %copy-done.9) | copy-start | bytes 3076
  78.0 11.8 %copy-start.12 = (s32[256]{0:T(256)S(1)}, s32[256]{0:T(256)}, u32[]{:S(2)}) copy-start(s32[256]{0:T(256)} %copy-done.11) | copy-start | bytes 3076
  79.0 10.7 %copy-start.19 = (pred[128]{0:T(512)(128)(4,1)}, pred[128]{0:T(512)(128)(4,1)S(1)}, u32[]{:S(2)}) copy-start(pred[128]{0:T(512)(128)(4,1)S(1)} %iota_compare_fusion.1) | copy-start | bytes 388
  85.4 18.5 %copy-start.20 = (s32[1,4,2]{1,2,0:T(2,128)S(1)}, s32[1,4,2]{1,2,0:T(2,128)}, u32[]{:S(2)}) copy-start(s32[1,4,2]{1,2,0:T(2,128)} %param.9) | copy-start | bytes 100
  85.4 13.7 %all-to-all-start.9 = ((bf16[4,2,256,128]{3,2,1,0:T(8,128)(2,1)}), bf16[4,2,256,128]{3,2,1,0:T(8,128)(2,1)}, u32[]{:S(2)}, u32[]{:S(2)}) async-start(bf16[4,2,256,128]{3,2,1,0:T(8,128)(2,1)} %bitcast.68), calls=%async_computation.9 | async-start | bytes 1048576 | tf_op jit(solution)/shard_map/all_to_all | solution.py:244
  90.7 25.4 %collective-permute-start = (bf16[4,2,256,128]{3,2,1,0:T(8,128)(2,1)S(1)}, bf16[4,2,256,128]{3,2,1,0:T(8,128)(2,1)S(1)}, u32[]{:S(2)}, u32[]{:S(2)}) collective-permute-start(bf16[4,2,256,128]{3,2,1,0:T(8,128)(2,1)S(1)} %all-to-all-done.1.own_ref), channel_id=1, source_target_pairs={{0,8},{8,16},{16,24},{1,9},{9,17},{17,25},{2,10},{10,18},{18,26},{... | collective-permute-start | bytes 1572872 | tf_op jit(solution)/shard_map/ppermute | solution.py:253
  94.9 24.7 %collective-permute-start.1 = (bf16[4,2,256,128]{3,2,1,0:T(8,128)(2,1)S(1)}, bf16[4,2,256,128]{3,2,1,0:T(8,128)(2,1)}, u32[]{:S(2)}, u32[]{:S(2)}) collective-permute-start(bf16[4,2,256,128]{3,2,1,0:T(8,128)(2,1)S(1)} %all-to-all-done.1.own_ref), channel_id=1, source_target_pairs={{8,0},{16,8},{24,16},{9,1},{17,9},{25,17},{10,2},{18,10},{26,18},{... | collective-permute-start | bytes 1572872 | tf_op jit(solution)/shard_map/ppermute | solution.py:254
  99.1 27.8 %all-to-all-start.10 = ((bf16[4,2,256,128]{3,2,1,0:T(8,128)(2,1)}), bf16[4,2,256,128]{3,2,1,0:T(8,128)(2,1)}, u32[]{:S(2)}, u32[]{:S(2)}) async-start(bf16[4,2,256,128]{3,2,1,0:T(8,128)(2,1)} %bitcast.67), calls=%async_computation.10 | async-start | bytes 1048576 | tf_op jit(solution)/shard_map/all_to_all | solution.py:244
  104.0 27.0 %collective-permute-start.2 = (bf16[4,2,256,128]{3,2,1,0:T(8,128)(2,1)S(1)}, bf16[4,2,256,128]{3,2,1,0:T(8,128)(2,1)}, u32[]{:S(2)}, u32[]{:S(2)}) collective-permute-start(bf16[4,2,256,128]{3,2,1,0:T(8,128)(2,1)S(1)} %all-to-all-done.5.own_ref), channel_id=1, source_target_pairs={{0,8},{8,16},{16,24},{1,9},{9,17},{17,25},{2,10},{10,18},{18,26},{... | collective-permute-start | bytes 1572872 | tf_op jit(solution)/shard_map/ppermute | solution.py:253
  109.4 21.7 %collective-permute-start.3 = (bf16[4,2,256,128]{3,2,1,0:T(8,128)(2,1)S(1)}, bf16[4,2,256,128]{3,2,1,0:T(8,128)(2,1)}, u32[]{:S(2)}, u32[]{:S(2)}) collective-permute-start(bf16[4,2,256,128]{3,2,1,0:T(8,128)(2,1)S(1)} %all-to-all-done.5.own_ref), channel_id=1, source_target_pairs={{8,0},{16,8},{24,16},{9,1},{17,9},{25,17},{10,2},{18,10},{26,18},{... | collective-permute-start | bytes 1572872 | tf_op jit(solution)/shard_map/ppermute | solution.py:254
  110.8 31.0 %collective-permute-start.4 = (bf16[4,2,256,128]{3,2,1,0:T(8,128)(2,1)}, bf16[4,2,256,128]{3,2,1,0:T(8,128)(2,1)}, u32[]{:S(2)}, u32[]{:S(2)}) collective-permute-start(bf16[4,2,256,128]{3,2,1,0:T(8,128)(2,1)} %all-to-all-done.9.own_ref), channel_id=1, source_target_pairs={{0,8},{8,16},{16,24},{1,9},{9,17},{17,25},{2,10},{10,18},{18,26},{... | collective-permute-start | bytes 1572872 | tf_op jit(solution)/shard_map/ppermute | solution.py:253
  116.1 0.8 copy-start.5
  116.9 24.8 %collective-permute-start.5 = (bf16[4,2,256,128]{3,2,1,0:T(8,128)(2,1)}, bf16[4,2,256,128]{3,2,1,0:T(8,128)(2,1)}, u32[]{:S(2)}, u32[]{:S(2)}) collective-permute-start(bf16[4,2,256,128]{3,2,1,0:T(8,128)(2,1)} %all-to-all-done.9.own_ref), channel_id=1, source_target_pairs={{8,0},{16,8},{24,16},{9,1},{17,9},{25,17},{10,2},{18,10},{26,18},{... | collective-permute-start | bytes 1572872 | tf_op jit(solution)/shard_map/ppermute | solution.py:254
  119.6 1.0 copy-start.3
  120.5 1.0 copy-start.6
  126.2 0.7 copy-start.4
  126.9 10.6 %all-to-all-start.3 = ((bf16[4,256,128]{2,1,0:T(8,128)(2,1)}), bf16[4,256,128]{2,1,0:T(8,128)(2,1)S(1)}, u32[]{:S(2)}, u32[]{:S(2)}) async-start(bf16[4,256,128]{2,1,0:T(8,128)(2,1)} %copy-done.4), calls=%async_computation.3 | async-start | bytes 524288 | tf_op jit(solution)/shard_map/all_to_all | solution.py:244
  131.1 1.0 copy-start.1
  137.5 10.0 %all-to-all-start.7 = ((bf16[4,256,128]{2,1,0:T(8,128)(2,1)}), bf16[4,256,128]{2,1,0:T(8,128)(2,1)S(1)}, u32[]{:S(2)}, u32[]{:S(2)}) async-start(bf16[4,256,128]{2,1,0:T(8,128)(2,1)} %attend.4), calls=%async_computation.7 | async-start | bytes 524288 | tf_op jit(solution)/shard_map/all_to_all | solution.py:244
  147.5 9.6 %all-to-all-start.11 = ((bf16[4,256,128]{2,1,0:T(8,128)(2,1)}), bf16[4,256,128]{2,1,0:T(8,128)(2,1)S(1)}, u32[]{:S(2)}, u32[]{:S(2)}) async-start(bf16[4,256,128]{2,1,0:T(8,128)(2,1)} %attend.5), calls=%async_computation.11 | async-start | bytes 524288 | tf_op jit(solution)/shard_map/all_to_all | solution.py:244
  161.2 2.4 %collective-permute-start.6 = (bf16[256,1536]{1,0:T(8,128)(2,1)S(1)}, bf16[256,1536]{1,0:T(8,128)(2,1)S(1)}, u32[]{:S(2)}, u32[]{:S(2)}) collective-permute-start(bf16[256,1536]{1,0:T(8,128)(2,1)S(1)} %fusion.10), channel_id=1, source_target_pairs={{0,1},{1,0},{2,3},{3,2},{4,5},{5,4},{6,7},{7,6},{8,9},{9,8},{10,11... | collective-permute-start | bytes 2359304 | tf_op jit(solution)/shard_map/ppermute | solution.py:268

commit v2 on v0

--- a/solution.py
+++ b/solution.py
@@ -1,10 +1,16 @@
+import functools
+import math
+
 import jax
 import jax.numpy as jnp
 from jax import lax
+from jax.experimental import pallas as pl
+from jax.experimental.pallas import tpu as pltpu
 from jax.sharding import PartitionSpec as P
 
 HD = 128
 RADIUS = 16
+FAR = -131072.0
 
 
 def extended(cells, sides, width):
@@ -24,7 +30,7 @@
     return cells
 
 
-def on_device(queries, keys_values, ref_cache, ref_ids, flags, proj_weight):
+def by_tile(queries, keys_values, ref_cache, ref_ids, flags, proj_weight):
     tile_rows, tile_cols, channels = queries.shape
     head_count = channels // HD
     padded_rows = tile_rows + 2 * RADIUS
@@ -117,6 +123,455 @@
     )
 
 
+VMEM = pl.BlockSpec(memory_space=pltpu.VMEM)
+SMEM = pl.BlockSpec(memory_space=pltpu.SMEM)
+ANY = pl.BlockSpec(memory_space=pl.ANY)
+
+
+def copied(pairs, sem):
+    copies = [
+        pltpu.make_async_copy(source, target, sem.at[n]) for n, (source, target) in enumerate(pairs)
+    ]
+    for copy in copies:
+        copy.start()
+    for copy in copies:
+        copy.wait()
+
+
+def attend_kernel(per_owner, tiles, count, me_ref, ids_ref, *refs):
+    come, (qf_ref, own_ref, a_ref, b_ref, kf_ref) = refs[:tiles], refs[tiles : tiles + 5]
+    o_refs, scratch = refs[tiles + 5 : 2 * tiles + 5], refs[2 * tiles + 5 :]
+    s_ref, qr_ref, out_ref = scratch
+    token_count = qf_ref.shape[1]
+    head_rows = qr_ref.shape[1] // count
+    block_tokens = (head_rows - token_count) // 2 // per_owner
+    chosen_count = ids_ref.shape[1]
+    factor = HD ** (-0.5) * math.log2(math.e)
+    ones = jnp.ones((token_count, HD), jnp.bfloat16)
+    ones_block = jnp.ones((block_tokens, HD), jnp.bfloat16)
+    for k in range(tiles):
+        qr_ref[me_ref[0] ^ k] = come[k][: qr_ref.shape[1]]
+    for head in range(count):
+        query_at = head * head_rows
+        key_at = query_at + token_count
+        value_at = key_at + per_owner * block_tokens
+        for w in range(tiles):
+            queries = qr_ref[w, query_at : query_at + token_count]
+            q_wide = jnp.concatenate([queries, qf_ref[w]], axis=1)
+            window = []
+            for other in range(max(w - 1, 0), min(w + 2, tiles)):
+                for r, source in enumerate((a_ref, own_ref, b_ref)):
+                    window.append((source, other, r, other - w + 1))
+            at = 0
+            best = None
+
+            def scored(keys, features, at, best):
+                wide = jnp.concatenate([keys, features], axis=1)
+                s = lax.dot_general(
+                    q_wide, wide, (((1,), (1,)), ((), ())), preferred_element_type=jnp.float32
+                )
+                width = s.shape[1]
+                s_ref[:, at : at + width] = s
+                for part in range(0, width, HD):
+                    piece = s[:, part : part + HD]
+                    best = piece if best is None else jnp.maximum(best, piece)
+                return at + width, best
+
+            for source, other, r, c in window:
+                at, best = scored(source[other, 2 * head], kf_ref[r, c], at, best)
+            picks = []
+            for n in range(chosen_count):
+                chosen = ids_ref[w, n]
+                owner = lax.div(chosen, per_owner)
+                start = pl.multiple_of(lax.rem(chosen, per_owner) * block_tokens, block_tokens)
+                picks.append((owner, start))
+                at, best = scored(
+                    qr_ref[owner, pl.ds(key_at + start, block_tokens)],
+                    kf_ref[3, 0, :block_tokens],
+                    at,
+                    best,
+                )
+            row_max = jnp.max(best, axis=1, keepdims=True)
+            at = 0
+            total = jnp.zeros((token_count, 2 * HD), jnp.float32)
+
+            def weighed(values, at, total):
+                width = values.shape[0]
+                probs = jnp.exp2((s_ref[:, at : at + width] - row_max) * factor)
+                total = total + jnp.dot(
+                    probs.astype(jnp.bfloat16), values, preferred_element_type=jnp.float32
+                )
+                return at + width, total
+
+            for source, other, r, c in window:
+                values = source[other, 2 * head + 1]
+                at, total = weighed(jnp.concatenate([values, ones], axis=1), at, total)
+            for owner, start in picks:
+                values = qr_ref[owner, pl.ds(value_at + start, block_tokens)]
+                at, total = weighed(jnp.concatenate([values, ones_block], axis=1), at, total)
+            out_ref[w, head * token_count : (head + 1) * token_count] = (
+                total[:, :HD] / total[:, HD:]
+            ).astype(jnp.bfloat16)
+    for k in range(tiles):
+        o_refs[k][...] = out_ref[me_ref[0] ^ k]
+
+
+def attend(per_owner, me, ids, qr, q_features, own, first, second, k_features):
+    tiles, token_count, _ = q_features.shape
+    count = own.shape[1] // 2
+    key_count = (9 + ids.shape[1]) * token_count
+    rows = qr[0].shape[0] // 128 * 128
+    return pl.pallas_call(
+        functools.partial(attend_kernel, per_owner, tiles, count),
+        out_shape=[jax.ShapeDtypeStruct((count * token_count, HD), jnp.bfloat16)] * tiles,
+        in_specs=[SMEM] * 2 + [VMEM] * (tiles + 5),
+        out_specs=[VMEM] * tiles,
+        scratch_shapes=[
+            pltpu.VMEM((token_count, key_count), jnp.float32),
+            pltpu.VMEM((tiles, rows, HD), jnp.bfloat16),
+            pltpu.VMEM((tiles, count * token_count, HD), jnp.bfloat16),
+        ],
+        compiler_params=pltpu.CompilerParams(vmem_limit_bytes=10 << 20),
+        cost_estimate=pl.CostEstimate(
+            flops=count * tiles * 4 * token_count * key_count * HD,
+            transcendentals=count * tiles * token_count * key_count,
+            bytes_accessed=3 * own.size * 2,
+        ),
+        name="attend",
+    )(me, ids, *in_vmem(*qr, q_features, own, first, second, k_features))
+
+
+def grid_lanes(tile_rows, tile_cols):
+    token_count = tile_rows * tile_cols
+    lane = lax.broadcasted_iota(jnp.int32, (token_count, HD), 1)
+    token = lax.broadcasted_iota(jnp.int32, (token_count, HD), 0)
+    row, col = lax.div(token, tile_cols), lax.rem(token, tile_cols)
+    is_row = lane < tile_rows
+    is_col = (lane >= tile_rows) & (lane < tile_rows + tile_cols)
+    is_flag = lane == tile_rows + tile_cols
+    return lane, row, col, is_row, is_col, is_flag
+
+
+def query_features_kernel(tile_rows, tile_cols, me_ref, *refs):
+    *come, o_ref = refs
+    lane, row, col, is_row, is_col, is_flag = grid_lanes(tile_rows, tile_cols)
+    hot = ((is_row & (lane == row)) | (is_col & (lane - tile_rows == col))).astype(jnp.float32)
+    token = row * tile_cols + col
+    for k, ref in enumerate(come):
+        flags = ref[...].astype(jnp.float32)
+        flag = jnp.zeros(hot.shape, jnp.float32)
+        for part in range(tile_rows * tile_cols // HD):
+            flag += jnp.where(token - part * HD == lane, flags[part : part + 1], 0.0)
+        column = jnp.sum(flag, axis=1, keepdims=True)
+        o_ref[me_ref[0] ^ k] = jnp.where(is_flag, 1.0 - column, hot).astype(jnp.bfloat16)
+
+
+def query_features(tile_rows, tile_cols, me, come):
+    tiles = len(come)
+    last = come[0].shape[0] // 16 - 1
+    return pl.pallas_call(
+        functools.partial(query_features_kernel, tile_rows, tile_cols),
+        grid=(1,),
+        out_shape=jax.ShapeDtypeStruct((tiles, tile_rows * tile_cols, HD), jnp.bfloat16),
+        in_specs=[SMEM] + [pl.BlockSpec((16, HD), lambda i: (last, 0))] * tiles,
+        out_specs=VMEM,
+        compiler_params=pltpu.CompilerParams(vmem_limit_bytes=4 << 20),
+        name="query_features",
+    )(me, *come)
+
+
+def key_features_kernel(tile_rows, tile_cols, side_ref, o_ref):
+    lane, row, col, is_row, is_col, is_flag = grid_lanes(tile_rows, tile_cols)
+    far_rows = []
+    for slot in range(2):
+        toward, there = side_ref[slot, 0], side_ref[slot, 1]
+        beyond = (row - lane) * toward > 0
+        far_rows.append(jnp.where(is_row & (beyond | (there == 0)), FAR, 0.0))
+    near = jnp.zeros_like(far_rows[0])
+    far_rows = [far_rows[0], near, far_rows[1]]
+    far_cols = [
+        jnp.where(is_col & (col < lane - tile_rows), FAR, 0.0),
+        near,
+        jnp.where(is_col & (col > lane - tile_rows), FAR, 0.0),
+    ]
+    for r in range(3):
+        for c in range(3):
+            o_ref[r, c] = (far_rows[r] + far_cols[c]).astype(jnp.bfloat16)
+    for c in range(3):
+        o_ref[3, c] = jnp.where(is_flag, FAR, 0.0).astype(jnp.bfloat16)
+
+
+def key_features(tile_rows, tile_cols, sides):
+    return pl.pallas_call(
+        functools.partial(key_features_kernel, tile_rows, tile_cols),
+        out_shape=jax.ShapeDtypeStruct((4, 3, tile_rows * tile_cols, HD), jnp.bfloat16),
+        in_specs=[SMEM],
+        out_specs=VMEM,
+        compiler_params=pltpu.CompilerParams(vmem_limit_bytes=4 << 20),
+        name="key_features",
+    )(sides)
+
+
+def pack_kv_kernel(tiles, share, heads, me_ref, x_ref, *refs):
+    *o_refs, sem = refs
+    pairs = []
+    for k, o_ref in enumerate(o_refs):
+        for n, head in enumerate(heads):
+            first = pl.multiple_of(((me_ref[0] ^ k) * share + head) * HD, HD)
+            pairs.append((x_ref.at[:, :, pl.ds(first, HD)], o_ref.at[2 * n : 2 * n + 2]))
+    copied(pairs, sem)
+
+
+def pack_kv(me, x, heads, tiles, share):
+    shape = jax.ShapeDtypeStruct((2 * len(heads), x.shape[1], HD), x.dtype)
+    return pl.pallas_call(
+        functools.partial(pack_kv_kernel, tiles, share, heads),
+        out_shape=[shape] * tiles,
+        in_specs=[SMEM, ANY],
+        out_specs=[VMEM] * tiles,
+        scratch_shapes=[pltpu.SemaphoreType.DMA((tiles * len(heads),))],
+        compiler_params=pltpu.CompilerParams(vmem_limit_bytes=8 << 20),
+        name="pack_kv",
+    )(me, x)
+
+
+def order_kernel(me_ref, *refs):
+    *come, o_ref, sem = refs
+    copied([(ref, o_ref.at[me_ref[0] ^ k]) for k, ref in enumerate(come)], sem)
+
+
+def order(me, come):
+    tiles = len(come)
+    return pl.pallas_call(
+        order_kernel,
+        out_shape=jax.ShapeDtypeStruct((tiles, *come[0].shape), come[0].dtype),
+        in_specs=[SMEM] + [ANY] * tiles,
+        out_specs=VMEM,
+        scratch_shapes=[pltpu.SemaphoreType.DMA((tiles,))],
+        compiler_params=pltpu.CompilerParams(vmem_limit_bytes=6 << 20),
+        name="order",
+    )(me, *come)
+
+
+def pack_qr_kernel(tiles, share, chunks, me_ref, q_ref, r_ref, f_ref, *refs):
+    *o_refs, sem = refs
+    token_count = q_ref.shape[0]
+    block_tokens = r_ref.shape[1]
+    pairs = []
+    for c, heads in enumerate(chunks):
+        for k in range(tiles):
+            o_ref = o_refs[c * tiles + k]
+            at = 0
+            for head in heads:
+                lanes = pl.ds(pl.multiple_of(((me_ref[0] ^ k) * share + head) * HD, HD), HD)
+                pairs.append((q_ref.at[:, lanes], o_ref.at[at : at + token_count]))
+                at += token_count
+                for part in range(2):
+                    pairs.append((r_ref.at[part, :, lanes], o_ref.at[at : at + block_tokens]))
+                    at += block_tokens
+            if f_ref.shape[0] + at == o_ref.shape[0]:
+                pairs.append((f_ref, o_ref.at[at : at + f_ref.shape[0]]))
+    copied(pairs, sem)
+
+
+def pack_qr(me, q, r, f, chunks, tiles, share):
+    rows = q.shape[0] + 2 * r.shape[1]
+    shapes = [
+        jax.ShapeDtypeStruct((rows * len(heads) + (f.shape[0] if heads[0] == 0 else 0), HD), q.dtype)
+        for c, heads in enumerate(chunks)
+        for k in range(tiles)
+    ]
+    flat = pl.pallas_call(
+        functools.partial(pack_qr_kernel, tiles, share, chunks),
+        out_shape=shapes,
+        in_specs=[SMEM] + [ANY] * 3,
+        out_specs=[VMEM] * len(shapes),
+        scratch_shapes=[pltpu.SemaphoreType.DMA((tiles * (3 * share + 1),))],
+        compiler_params=pltpu.CompilerParams(vmem_limit_bytes=8 << 20),
+        name="pack_qr",
+    )(me, q, r, f)
+    return [flat[n * tiles : (n + 1) * tiles] for n in range(len(chunks))]
+
+
+def fetch_rows(tiles, share, chunk, me_ref, w_hbm, w_ref, sem, columns):
+    depth = len(chunk) * HD
+    copies = []
+    for k in range(tiles):
+        first = pl.multiple_of(((me_ref[0] ^ k) * share + chunk[0]) * HD, HD)
+        copies.append(
+            pltpu.make_async_copy(
+                w_hbm.at[pl.ds(first, depth), columns], w_ref.at[k], sem.at[k]
+            )
+        )
+        copies[-1].start()
+    return copies
+
+
+def side_by_side(ref, count):
+    token_count = ref.shape[0] // count
+    return jnp.concatenate(
+        [ref[n * token_count : (n + 1) * token_count] for n in range(count)], axis=1
+    )
+
+
+def project_early_kernel(tiles, share, chunk, me_ref, w_hbm, *refs):
+    *heads, o_ref, w_ref, sem = refs
+    width = o_ref.shape[2]
+    copies = fetch_rows(tiles, share, chunk, me_ref, w_hbm, w_ref, sem, slice(None))
+    for k in range(tiles):
+        copies[k].wait()
+        x = side_by_side(heads[k], len(chunk))
+        for half in range(2):
+            part = jnp.dot(
+                x, w_ref[k, :, half * width : (half + 1) * width], preferred_element_type=jnp.float32
+            )
+            o_ref[half] = part if k == 0 else o_ref[half] + part
+
+
+def project_early(me, weight, heads, chunk, share):
+    tiles = len(heads)
+    token_count = heads[0].shape[0] // len(chunk)
+    width = weight.shape[1]
+    return pl.pallas_call(
+        functools.partial(project_early_kernel, tiles, share, chunk),
+        out_shape=jax.ShapeDtypeStruct((2, token_count, width // 2), jnp.float32),
+        in_specs=[SMEM, ANY] + [VMEM] * tiles,
+        out_specs=VMEM,
+        scratch_shapes=[
+            pltpu.VMEM((tiles, len(chunk) * HD, width), jnp.bfloat16),
+            pltpu.SemaphoreType.DMA((tiles,)),
+        ],
+        compiler_params=pltpu.CompilerParams(vmem_limit_bytes=14 << 20),
+        name="project_early",
+    )(me, pltpu.with_memory_space_constraint(weight, pltpu.HBM), *heads)
+
+
+def project_kernel(tiles, share, chunk, me_ref, which_ref, w_hbm, early_ref, *refs):
+    *heads, o_ref, w_ref, sem = refs
+    width = o_ref.shape[1]
+    columns = pl.ds(pl.multiple_of(which_ref[0] * width, HD), width)
+    copies = fetch_rows(tiles, share, chunk, me_ref, w_hbm, w_ref, sem, columns)
+    total = early_ref[which_ref[0]]
+    for copy in copies:
+        copy.wait()
+    for k in range(tiles):
+        x = side_by_side(heads[k], len(chunk))
+        total = total + jnp.dot(x, w_ref[k], preferred_element_type=jnp.float32)
+    o_ref[...] = total.astype(o_ref.dtype)
+
+
+def project(me, which, weight, early, heads, chunk, share):
+    tiles = len(heads)
+    _, token_count, width = early.shape
+    return pl.pallas_call(
+        functools.partial(project_kernel, tiles, share, chunk),
+        out_shape=jax.ShapeDtypeStruct((token_count, width), jnp.bfloat16),
+        in_specs=[SMEM] * 2 + [ANY] + [VMEM] * (1 + tiles),
+        out_specs=VMEM,
+        scratch_shapes=[
+            pltpu.VMEM((tiles, len(chunk) * HD, width), jnp.bfloat16),
+            pltpu.SemaphoreType.DMA((tiles,)),
+        ],
+        compiler_params=pltpu.CompilerParams(vmem_limit_bytes=10 << 20),
+        name="project",
+    )(me, which.reshape(1), pltpu.with_memory_space_constraint(weight, pltpu.HBM), early, *heads)
+
+
+def in_vmem(*arrays):
+    return [pltpu.with_memory_space_constraint(x, pltpu.VMEM) for x in arrays]
+
+
+def after(x, *others):
+    return lax.optimization_barrier((x, *others))[0]
+
+
+def by_head(queries, keys_values, ref_cache, ref_ids, flags, proj_weight):
+    tile_rows, tile_cols, channels = queries.shape
+    tiles = lax.axis_size("wa")
+    token_count = tile_rows * tile_cols
+    share = channels // HD // tiles
+    chunks = [list(range(share - 1)), [share - 1]]
+    per_owner = ref_cache.shape[0]
+    heights = lax.axis_size("ha")
+    kv = keys_values.reshape(token_count, 2, channels).transpose(1, 0, 2)
+
+    def swap(come):
+        return [
+            x if k == 0 else lax.ppermute(x, "wa", [(i, i ^ k) for i in range(tiles)])
+            for k, x in enumerate(come)
+        ]
+
+    even = [(i, i + 1) for i in range(0, heights - 1, 2)]
+    odd = [(i, i + 1) for i in range(1, heights - 1, 2)]
+    both_ways = [[(b, a) for a, b in pairs] + pairs for pairs in (even, odd)]
+
+    def neighbours(x):
+        return [lax.ppermute(x, "ha", pairs) for pairs in both_ways]
+
+    place = lax.axis_index("ha")
+    toward = 1 - 2 * (place % 2)
+    sides = jnp.stack(
+        [
+            jnp.stack([way, ((place + way >= 0) & (place + way < heights)).astype(jnp.int32)])
+            for way in (toward, -toward)
+        ]
+    )
+    me = lax.axis_index("wa").reshape(1)
+    packed = [pack_kv(me, kv, chunks[0], tiles, share)]
+    for chunk in chunks[1:]:
+        packed.append(pack_kv(me, after(kv, *packed[-1]), chunk, tiles, share))
+    come = [swap(packed[0])]
+    for pieces in packed[1:]:
+        come.append(swap([after(x, *come[-1][1:]) for x in pieces]))
+    own = [order(me, lax.optimization_barrier((*come[0], *packed[-1]))[:tiles])]
+    around = [neighbours(own[0])]
+    late_q, late_r = lax.optimization_barrier((queries, ref_cache, packed[-1][1]))[:2]
+    late_r = late_r.reshape(-1, 2, channels).transpose(1, 0, 2)
+    flag_rows = jnp.pad(flags.reshape(-1, HD), ((0, 16 - token_count // HD), (0, 0)))
+    late_q = late_q.reshape(token_count, channels)
+    flag_rows = flag_rows.astype(jnp.bfloat16)
+    qr = pack_qr(me, late_q, late_r, flag_rows, chunks[:1], tiles, share)
+    later = lax.optimization_barrier((late_q, late_r, flag_rows, come[-1][1]))[:3]
+    qr += pack_qr(me, *later, chunks[1:], tiles, share)
+    k_features = key_features(tile_rows, tile_cols, sides)
+    for pieces in come[1:]:
+        own.append(order(me, lax.optimization_barrier((*pieces, qr[0][1], k_features))[:tiles]))
+        around.append(neighbours(after(own[-1], *around[-1])))
+    arrived = []
+    for n, pieces in enumerate(qr):
+        gates = come[-1][1:] if n == 0 else arrived[-1][1:]
+        arrived.append(swap([after(x, *gates) for x in pieces]))
+    q_features = query_features(tile_rows, tile_cols, me, arrived[0])
+    heads = [
+        swap(
+            attend(
+                per_owner, me, ref_ids[0], arrived[n], q_features, own[n], *around[n], k_features
+            )
+        )
+        for n in range(len(chunks))
+    ]
+    early = project_early(me, proj_weight, heads[0], chunks[0], share)
+    mine = lax.axis_index("head")
+    theirs = project(me, 1 - mine, proj_weight, early, heads[1], chunks[1], share)
+    got = lax.ppermute(theirs, "head", [(0, 1), (1, 0)])
+    own_part = project(me, mine, proj_weight, early, heads[1], chunks[1], share)
+    total = own_part.astype(jnp.float32) + got.astype(jnp.float32)
+    return total.astype(jnp.bfloat16).reshape(tile_rows, tile_cols, -1)
+
+
+def on_device(queries, *others):
+    head_count = queries.shape[2] // HD
+    fits = (
+        head_count % lax.axis_size("wa") == 0
+        and lax.axis_size("wa") & (lax.axis_size("wa") - 1) == 0
+        and head_count // lax.axis_size("wa") > 1
+        and lax.axis_size("head") == 2
+        and queries.shape[0] == RADIUS
+        and queries.shape[1] == RADIUS
+    )
+    return (by_head if fits else by_tile)(queries, *others)
+
+
 def solution(mesh):
     return jax.shard_map(
         on_device,

time: 319 us -> 87.1 us (0.27)
  waiting for transfers between devices: 218 us -> 19.2 us
  Pallas kernels: 0 us -> 29.3 us
  matrix products: 25.9 us -> 0 us
  local copies, waits for them, and re-layouts: 26.4 us -> 5.17 us
  between operations: 14 us -> 0.25 us
  other arithmetic: 14.2 us -> 1.16 us
  starting transfers between devices: 20 us -> 31.7 us
    reduce_scatter x1 -> x0, waiting for transfers between devices: 110 us -> none  [on_device(): lax.psum_scatter(partial_term.astype(jnp.bfloat16), 'head', scatter_dimen...]
    ppermute x4 -> x23, waiting for transfers between devices: 108 us -> 19.2 us  [the longest x18 12.7 us: swap(): lax.ppermute(x, 'wa', [(i, i ^ k) for i in range(tiles)])]
    pallas_call x0 -> x13, Pallas kernels: none -> 29.3 us  [the longest x2 13.6 us: attend(): pl.pallas_call(functools.partial(attend_kernel, per_owner, tiles, count),...]
    dot_general x50 -> x0, matrix products: 25.9 us -> none  [the longest x12 7.93 us: on_device(): jnp.einsum('qc,kc->qk', head_query, key_flat[:, first:first + HD], prefer...]
    ppermute x4 -> x23, starting transfers between devices: 15.4 us -> 31.7 us  [the longest x18 22.1 us: swap(): lax.ppermute(x, 'wa', [(i, i ^ k) for i in range(tiles)])]
    concatenate x1 -> x0, other arithmetic: 7.17 us -> none  [extended(): jnp.concatenate([lax.ppermute(tail, axis, [(i, (i + 1) % count) for i in...]
    reduce_sum x25 -> x0, other arithmetic: 5.88 us -> none  [the longest x12 4.93 us: on_device(): denominator = jnp.sum(probs, axis=1) + ref_total]
    all_to_all x1 -> x0, starting transfers between devices: 4.63 us -> none  [on_device(): lax.all_to_all(outgoing, 'wa', split_axis=0, concat_axis=0, tiled=True)]
  transfers between devices with their start and end apart: 6 -> 23, of which waited for: 4 -> 6; matrix products, arithmetic and copies ran while one was open for 9% -> 2% of each run, Pallas kernels for 0% -> 31%
where the time goes in v2:
time: 87.1 us; the launch traced here: 86.7 us
  starting transfers between devices  31.7 us (36%)
  Pallas kernels  29.3 us (34%)
  waiting for transfers between devices  19.2 us (22%)
  local copies, waits for them, and re-layouts  5.17 us (6%)
  other arithmetic  1.16 us (1%)
    ppermute x18, starting transfers between devices, swap(): lax.ppermute(x, 'wa', [(i, i ^ k) for i in range(tiles)])  22.1 us
    pallas_call x2, Pallas kernels, attend(): pl.pallas_call(functools.partial(attend_kernel, per_owner, tiles, count),...  13.6 us
    ppermute x18, waiting for transfers between devices, swap(): lax.ppermute(x, 'wa', [(i, i ^ k) for i in range(tiles)])  12.7 us
    ppermute x4, starting transfers between devices, neighbours(): return [lax.ppermute(x, 'ha', pairs) for pairs in both_ways]  9.47 us
    ppermute x4, waiting for transfers between devices, neighbours(): return [lax.ppermute(x, 'ha', pairs) for pairs in both_ways]  6.48 us
    pallas_call x2, Pallas kernels, project(): pl.pallas_call(functools.partial(project_kernel, tiles, share, chunk), ou...  4.75 us
    pallas_call x1, Pallas kernels, project_early(): pl.pallas_call(functools.partial(project_early_kernel, tiles, share, chun...  3.83 us
    unnamed x15, local copies, waits for them, and re-layouts  3.32 us
  transfers between devices with their start and end apart: 23, of which 6 were waited for; matrix products, arithmetic and copies ran while one was open for 2% of the time, Pallas kernels for 31%

profile of v2, /device:TPU:0, one launch (start us, length us, event | category | flops | bytes accessed | tf_op | source)
XLA Modules:
  0.0 86.7 jit_solution(6046668737714559026)
XLA Ops:
  0.0 1.7 %copy.7 = bf16[16,16,2,1536]{3,1,0,2:T(8,128)(2,1)S(1)} copy(bf16[16,16,2,1536]{3,2,1,0:T(2,128)(2,1)} %param.7) | data formatting | bytes 3145728 | tf_op args[1]
  1.7 0.3 pack_kv.2
  2.0 3.0 %collective-permute-start = (bf16[4,256,128]{2,1,0:T(8,128)(2,1)S(1)}, bf16[4,256,128]{2,1,0:T(8,128)(2,1)S(1)}, u32[]{:S(2)}, u32[]{:S(2)}) collective-permute-start(bf16[4,256,128]{2,1,0:T(8,128)(2,1)S(1)} %get-tuple-element.57), channel_id=1, source_target_pairs={{0,2},{2,0},{4,6},{6,4},{1,3},{3,1},{5,7},{7,5},{8,10},{10,8},{12,... | collective-permute-start | bytes 786440 | tf_op jit(solution)/shard_map/ppermute | solution.py:500
  5.0 1.5 %collective-permute-start.1 = (bf16[4,256,128]{2,1,0:T(8,128)(2,1)S(1)}, bf16[4,256,128]{2,1,0:T(8,128)(2,1)S(1)}, u32[]{:S(2)}, u32[]{:S(2)}) collective-permute-start(bf16[4,256,128]{2,1,0:T(8,128)(2,1)S(1)} %get-tuple-element.58), channel_id=1, source_target_pairs={{0,4},{2,6},{4,0},{6,2},{1,5},{3,7},{5,1},{7,3},{8,12},{10,14},{12... | collective-permute-start | bytes 786440 | tf_op jit(solution)/shard_map/ppermute | solution.py:500
  6.5 0.0 collective-permute-start.2
  6.5 0.9 %pack_kv.3 = (bf16[2,256,128]{2,1,0:T(8,128)(2,1)S(1)}, bf16[2,256,128]{2,1,0:T(8,128)(2,1)}, bf16[2,256,128]{2,1,0:T(8,128)(2,1)}, bf16[2,256,128]{2,1,0:T(8,128)(2,1)}) custom-call(s32[1]{0:T(128)} %bitcast.me_ref, bf16[2,256,1536]{2,1,0:T(8,128)(2,1)S(1)} %bitcast.21), custom_call_target="tpu_custom_call" | custom-call | tf_op jit(solution)/shard_map/pack_kv/pallas_call | solution.py:327
  7.4 4.7 %collective-permute-done.refs_1_ = bf16[4,256,128]{2,1,0:T(8,128)(2,1)S(1)} collective-permute-done((bf16[4,256,128]{2,1,0:T(8,128)(2,1)S(1)}, bf16[4,256,128]{2,1,0:T(8,128)(2,1)S(1)}, u32[]{:S(2)}, u32[]{:S(2)}) %collective-permute-start) | collective-permute-done | bytes 262176 | tf_op jit(solution)/shard_map/ppermute | solution.py:500
  12.1 6.2 %collective-permute-done.1.refs_2_ = bf16[4,256,128]{2,1,0:T(8,128)(2,1)S(1)} collective-permute-done((bf16[4,256,128]{2,1,0:T(8,128)(2,1)S(1)}, bf16[4,256,128]{2,1,0:T(8,128)(2,1)S(1)}, u32[]{:S(2)}, u32[]{:S(2)}) %collective-permute-start.1) | collective-permute-done | bytes 262176 | tf_op jit(solution)/shard_map/ppermute | solution.py:500
  18.4 0.0 collective-permute-done.2.refs_3_
  18.4 0.1 order.2.refs_5_
  18.5 1.6 %collective-permute-start.10 = (bf16[4,4,256,128]{3,2,1,0:T(8,128)(2,1)S(1)}, bf16[4,4,256,128]{3,2,1,0:T(8,128)(2,1)}, u32[]{:S(2)}, u32[]{:S(2)}) collective-permute-start(bf16[4,4,256,128]{3,2,1,0:T(8,128)(2,1)S(1)} %order.2.refs_5_), channel_id=1, source_target_pairs={{16,8},{8,16},{17,9},{9,17},{18,10},{10,18},{19,11},{11,19},{20,12... | collective-permute-start | bytes 3145736 | tf_op jit(solution)/shard_map/ppermute | solution.py:509
  20.1 3.5 %collective-permute-start.9 = (bf16[4,4,256,128]{3,2,1,0:T(8,128)(2,1)S(1)}, bf16[4,4,256,128]{3,2,1,0:T(8,128)(2,1)}, u32[]{:S(2)}, u32[]{:S(2)}) collective-permute-start(bf16[4,4,256,128]{3,2,1,0:T(8,128)(2,1)S(1)} %order.2.refs_5_), channel_id=1, source_target_pairs={{8,0},{24,16},{0,8},{16,24},{9,1},{25,17},{1,9},{17,25},{10,2},{26... | collective-permute-start | bytes 3145736 | tf_op jit(solution)/shard_map/ppermute | solution.py:509
  23.6 1.2 %collective-permute-start.3 = (bf16[2,256,128]{2,1,0:T(8,128)(2,1)}, bf16[2,256,128]{2,1,0:T(8,128)(2,1)}, u32[]{:S(2)}, u32[]{:S(2)}) collective-permute-start(bf16[2,256,128]{2,1,0:T(8,128)(2,1)} %get-tuple-element.65), channel_id=1, source_target_pairs={{0,2},{2,0},{4,6},{6,4},{1,3},{3,1},{5,7},{7,5},{8,10},{10,8},{12,... | collective-permute-start | bytes 393224 | tf_op jit(solution)/shard_map/ppermute | solution.py:500
  24.8 0.8 collective-permute-start.4
  25.7 1.4 %collective-permute-start.5 = (bf16[2,256,128]{2,1,0:T(8,128)(2,1)}, bf16[2,256,128]{2,1,0:T(8,128)(2,1)}, u32[]{:S(2)}, u32[]{:S(2)}) collective-permute-start(bf16[2,256,128]{2,1,0:T(8,128)(2,1)} %get-tuple-element.69), channel_id=1, source_target_pairs={{0,6},{2,4},{4,2},{6,0},{1,7},{3,5},{5,3},{7,1},{8,14},{10,12},{12... | collective-permute-start | bytes 393224 | tf_op jit(solution)/shard_map/ppermute | solution.py:500
  27.1 0.1 reshape.30
  27.2 1.7 %copy.8 = bf16[2,128,2,1536]{3,1,0,2:T(8,128)(2,1)S(1)} copy(bf16[2,128,2,1536]{3,2,1,0:T(2,128)(2,1)} %param.8) | data formatting | bytes 3145728 | tf_op jit(solution)/shard_map/optimization_barrier | solution.py:528
  28.9 0.0 copy-start.6
  28.9 1.8 %pack_qr.2 = (bf16[1552,128]{1,0:T(8,128)(2,1)S(1)}, bf16[1552,128]{1,0:T(8,128)(2,1)}, bf16[1552,128]{1,0:T(8,128)(2,1)}, bf16[1552,128]{1,0:T(8,128)(2,1)}) custom-call(s32[1]{0:T(128)} %bitcast.me_ref, bf16[256,1536]{1,0:T(8,128)(2,1)S(1)} %bitcast.24, bf16[2,256,1536]{2,1,0:T(8,128)(2,1)S(1)} %bitcast.22, bf16[16,128]{1,0:T(8,128)(2,1)S(1)} %pad.5.f_ref), custom_call_target="tpu_custom_call" | custom-call | tf_op jit(solution)/shard_map/pack_qr/pallas_call | solution.py:384
  30.7 0.8 copy-done.3
  31.4 0.0 collective-permute-done.3.refs_1_
  31.4 0.0 collective-permute-done.4.refs_2_
  31.4 0.4 collective-permute-done.5.refs_3_
  31.9 1.5 %collective-permute-start.6 = (bf16[1552,128]{1,0:T(8,128)(2,1)}, bf16[1552,128]{1,0:T(8,128)(2,1)}, u32[]{:S(2)}, u32[]{:S(2)}) collective-permute-start(bf16[1552,128]{1,0:T(8,128)(2,1)} %get-tuple-element.72), channel_id=1, source_target_pairs={{0,2},{2,0},{4,6},{6,4},{1,3},{3,1},{5,7},{7,5},{8,10},{10,8},{12,... | collective-permute-start | bytes 1191944 | tf_op jit(solution)/shard_map/ppermute | solution.py:500
  33.3 1.2 %collective-permute-start.8 = (bf16[1552,128]{1,0:T(8,128)(2,1)}, bf16[1552,128]{1,0:T(8,128)(2,1)}, u32[]{:S(2)}, u32[]{:S(2)}) collective-permute-start(bf16[1552,128]{1,0:T(8,128)(2,1)} %get-tuple-element.76), channel_id=1, source_target_pairs={{0,6},{2,4},{4,2},{6,0},{1,7},{3,5},{5,3},{7,1},{8,14},{10,12},{12... | collective-permute-start | bytes 1191944 | tf_op jit(solution)/shard_map/ppermute | solution.py:500
  34.5 0.8 collective-permute-start.7
  35.3 0.1 add_bitcast_fusion
  35.4 0.7 key_features.1.refs_8_
  36.1 0.0 copy-start.1
  36.1 0.9 %copy-done.1 = bf16[4,3,256,128]{3,2,1,0:T(8,128)(2,1)} copy-done((bf16[4,3,256,128]{3,2,1,0:T(8,128)(2,1)}, bf16[4,3,256,128]{3,2,1,0:T(8,128)(2,1)S(1)}, u32[]{:S(2)}) %copy-start.1) | copy-done | bytes 786456
  37.0 2.0 %order.3.refs_5_ = bf16[4,2,256,128]{3,2,1,0:T(8,128)(2,1)} custom-call(s32[1]{0:T(128)} %bitcast.me_ref, bf16[2,256,128]{2,1,0:T(8,128)(2,1)S(1)} %get-tuple-element.98.refs_0_, bf16[2,256,128]{2,1,0:T(8,128)(2,1)} %collective-permute-done.3.refs_1_, bf16[2,256,128]{2,1,0:T(8,128)(2,1)} %collective-permute-done.4.refs_2_, ...), custom_call_target="tpu_custom_call" | custom-call | tf_op jit(solution)/shard_map/order/pallas_call | solution.py:345
  39.0 0.0 collective-permute-done.10.refs_7_
  39.0 6.5 %collective-permute-done.9.refs_6_ = bf16[4,4,256,128]{3,2,1,0:T(8,128)(2,1)} collective-permute-done((bf16[4,4,256,128]{3,2,1,0:T(8,128)(2,1)S(1)}, bf16[4,4,256,128]{3,2,1,0:T(8,128)(2,1)}, u32[]{:S(2)}, u32[]{:S(2)}) %collective-permute-start.9) | collective-permute-done | bytes 1048608 | tf_op jit(solution)/shard_map/ppermute | solution.py:509
  45.5 1.4 %collective-permute-start.18 = (bf16[4,2,256,128]{3,2,1,0:T(8,128)(2,1)}, bf16[4,2,256,128]{3,2,1,0:T(8,128)(2,1)}, u32[]{:S(2)}, u32[]{:S(2)}) collective-permute-start(bf16[4,2,256,128]{3,2,1,0:T(8,128)(2,1)} %order.3.refs_5_), channel_id=1, source_target_pairs={{16,8},{8,16},{17,9},{9,17},{18,10},{10,18},{19,11},{11,19},{20,12... | collective-permute-start | bytes 1572872 | tf_op jit(solution)/shard_map/ppermute | solution.py:509
  47.0 2.9 %collective-permute-start.17 = (bf16[4,2,256,128]{3,2,1,0:T(8,128)(2,1)}, bf16[4,2,256,128]{3,2,1,0:T(8,128)(2,1)}, u32[]{:S(2)}, u32[]{:S(2)}) collective-permute-start(bf16[4,2,256,128]{3,2,1,0:T(8,128)(2,1)} %order.3.refs_5_), channel_id=1, source_target_pairs={{8,0},{24,16},{0,8},{16,24},{9,1},{25,17},{1,9},{17,25},{10,2},{26... | collective-permute-start | bytes 1572872 | tf_op jit(solution)/shard_map/ppermute | solution.py:509
  49.9 0.1 copy.9.ids_ref
  50.0 0.5 pack_qr.3
  50.5 0.0 collective-permute-done.6.refs_1_
  50.5 0.0 collective-permute-done.8.refs_3_
  50.5 1.1 %collective-permute-done.7.refs_2_ = bf16[1552,128]{1,0:T(8,128)(2,1)} collective-permute-done((bf16[1552,128]{1,0:T(8,128)(2,1)}, bf16[1552,128]{1,0:T(8,128)(2,1)}, u32[]{:S(2)}, u32[]{:S(2)}) %collective-permute-start.7) | collective-permute-done | bytes 397344 | tf_op jit(solution)/shard_map/ppermute | solution.py:500
  51.6 0.4 collective-permute-start.14
  52.0 1.9 %collective-permute-start.15 = (bf16[768,128]{1,0:T(8,128)(2,1)S(1)}, bf16[768,128]{1,0:T(8,128)(2,1)S(1)}, u32[]{:S(2)}, u32[]{:S(2)}) collective-permute-start(bf16[768,128]{1,0:T(8,128)(2,1)S(1)} %get-tuple-element.94), channel_id=1, source_target_pairs={{0,4},{2,6},{4,0},{6,2},{1,5},{3,7},{5,1},{7,3},{8,12},{10,14},{12... | collective-permute-start | bytes 589832 | tf_op jit(solution)/shard_map/ppermute | solution.py:500
  54.0 1.2 %collective-permute-start.16 = (bf16[768,128]{1,0:T(8,128)(2,1)S(1)}, bf16[768,128]{1,0:T(8,128)(2,1)S(1)}, u32[]{:S(2)}, u32[]{:S(2)}) collective-permute-start(bf16[768,128]{1,0:T(8,128)(2,1)S(1)} %get-tuple-element.96), channel_id=1, source_target_pairs={{0,6},{2,4},{4,2},{6,0},{1,7},{3,5},{5,3},{7,1},{8,14},{10,12},{12... | collective-permute-start | bytes 589832 | tf_op jit(solution)/shard_map/ppermute | solution.py:500
  55.1 0.9 %query_features.1.refs_4_ = bf16[4,256,128]{2,1,0:T(8,128)(2,1)S(1)} custom-call(s32[1]{0:T(128)} %bitcast.me_ref, bf16[1552,128]{1,0:T(8,128)(2,1)S(1)} %copy-done.4, bf16[1552,128]{1,0:T(8,128)(2,1)} %collective-permute-done.6.refs_1_, bf16[1552,128]{1,0:T(8,128)(2,1)} %collective-permute-done.7.refs_2_, bf16[1552,128]{1,0:T(8,128)(2,1)} %collective-permute-done.8.refs_3_), custom_call_target="tpu_custom_call" | custom-call | tf_op jit(solution)/shard_map/query_features/pallas_call | solution.py:272
  56.1 8.6 %attend.2 = (bf16[512,128]{1,0:T(8,128)(2,1)S(1)}, bf16[512,128]{1,0:T(8,128)(2,1)S(1)}, bf16[512,128]{1,0:T(8,128)(2,1)S(1)}, bf16[512,128]{1,0:T(8,128)(2,1)S(1)}) custom-call(s32[1]{0:T(128)} %bitcast.me_ref, s32[4,2]{1,0:T(4,128)S(1)} %copy.9.ids_ref, bf16[1552,128]{1,0:T(8,128)(2,1)S(1)} %copy-done.4, bf16[1552,128]{1,0:T(8,128)(2,1)} %collective-permute-done.6.refs_1_, ...), custom_call_target="tpu_custom_call" | custom-call | flops 2952790016 | bytes 3145728 | tf_op jit(solution)/shard_map/attend/pallas_call | solution.py:224
  64.7 0.0 collective-permute-done.14.refs_1_
  64.7 0.4 collective-permute-start.11
  65.2 1.9 %collective-permute-start.12 = (bf16[512,128]{1,0:T(8,128)(2,1)S(1)}, bf16[512,128]{1,0:T(8,128)(2,1)S(1)}, u32[]{:S(2)}, u32[]{:S(2)}) collective-permute-start(bf16[512,128]{1,0:T(8,128)(2,1)S(1)} %get-tuple-element.84), channel_id=1, source_target_pairs={{0,4},{2,6},{4,0},{6,2},{1,5},{3,7},{5,1},{7,3},{8,12},{10,14},{12... | collective-permute-start | bytes 393224 | tf_op jit(solution)/shard_map/ppermute | solution.py:500
  67.1 1.2 %collective-permute-start.13 = (bf16[512,128]{1,0:T(8,128)(2,1)S(1)}, bf16[512,128]{1,0:T(8,128)(2,1)S(1)}, u32[]{:S(2)}, u32[]{:S(2)}) collective-permute-start(bf16[512,128]{1,0:T(8,128)(2,1)S(1)} %get-tuple-element.85), channel_id=1, source_target_pairs={{0,6},{2,4},{4,2},{6,0},{1,7},{3,5},{5,3},{7,1},{8,14},{10,12},{12... | collective-permute-start | bytes 393224 | tf_op jit(solution)/shard_map/ppermute | solution.py:500
  68.3 0.0 collective-permute-done.18.refs_7_
  68.3 0.0 collective-permute-done.17.refs_6_
  68.3 4.9 %attend.3 = (bf16[256,128]{1,0:T(8,128)(2,1)S(1)}, bf16[256,128]{1,0:T(8,128)(2,1)S(1)}, bf16[256,128]{1,0:T(8,128)(2,1)S(1)}, bf16[256,128]{1,0:T(8,128)(2,1)S(1)}) custom-call(s32[1]{0:T(128)} %bitcast.me_ref, s32[4,2]{1,0:T(4,128)S(1)} %copy.9.ids_ref, bf16[768,128]{1,0:T(8,128)(2,1)S(1)} %get-tuple-element.90.refs_0_, ...), custom_call_target="tpu_custom_call" | custom-call | flops 1476395008 | bytes 1572864 | tf_op jit(solution)/shard_map/attend/pallas_call | solution.py:224
  73.2 0.4 collective-permute-start.19
  73.7 1.9 %collective-permute-start.20 = (bf16[256,128]{1,0:T(8,128)(2,1)S(1)}, bf16[256,128]{1,0:T(8,128)(2,1)S(1)}, u32[]{:S(2)}, u32[]{:S(2)}) collective-permute-start(bf16[256,128]{1,0:T(8,128)(2,1)S(1)} %get-tuple-element.105), channel_id=1, source_target_pairs={{0,4},{2,6},{4,0},{6,2},{1,5},{3,7},{5,1},{7,3},{8,12},{10,14},{12... | collective-permute-start | bytes 196616 | tf_op jit(solution)/shard_map/ppermute | solution.py:500
  75.6 0.0 collective-permute-done.11.refs_1_
  75.6 1.2 %collective-permute-start.21 = (bf16[256,128]{1,0:T(8,128)(2,1)S(1)}, bf16[256,128]{1,0:T(8,128)(2,1)S(1)}, u32[]{:S(2)}, u32[]{:S(2)}) collective-permute-start(bf16[256,128]{1,0:T(8,128)(2,1)S(1)} %get-tuple-element.106), channel_id=1, source_target_pairs={{0,6},{2,4},{4,2},{6,0},{1,7},{3,5},{5,3},{7,1},{8,14},{10,12},{12... | collective-permute-start | bytes 196616 | tf_op jit(solution)/shard_map/ppermute | solution.py:500
  76.8 3.8 %project_early.1.early_ref = f32[2,256,1536]{2,1,0:T(8,128)S(1)} custom-call(s32[1]{0:T(128)} %bitcast.me_ref, bf16[1536,3072]{1,0:T(8,128)(2,1)} %w_hbm.5, bf16[512,128]{1,0:T(8,128)(2,1)S(1)} %get-tuple-element.82.refs_0_, bf16[512,128]{1,0:T(8,128)(2,1)S(1)} %collective-permute-done.11.refs_1_, bf16[512,128]{1,0:T(8,128)(2,1)S(1)} %collective-permute-done.12.refs_2_, ...), custom_call_target="tpu_custom_call" | custom-call | tf_op jit(solution)/shard_map/project_early/pallas_call | solution.py:435
  80.7 0.0 collective-permute-done.20.refs_2_
  80.7 0.1 collective-permute-done.21.refs_3_
  80.8 2.4 %project.3 = bf16[256,1536]{1,0:T(8,128)(2,1)S(1)} custom-call(s32[1]{0:T(128)} %bitcast.me_ref, s32[1]{0:T(128)} %bitcast.16.which_ref, bf16[1536,3072]{1,0:T(8,128)(2,1)} %w_hbm.5, f32[2,256,1536]{2,1,0:T(8,128)S(1)} %project_early.1.early_ref, bf16[256,128]{1,0:T(8,128)(2,1)S(1)} %get-tuple-element.103.refs_0_, ...), custom_call_target="tpu_custom_call" | custom-call | tf_op jit(solution)/shard_map/project/pallas_call | solution.py:466
  83.2 0.1 collective-permute-start.22
  83.3 2.4 %project.2 = bf16[256,1536]{1,0:T(8,128)(2,1)S(1)} custom-call(s32[1]{0:T(128)} %bitcast.me_ref, s32[1]{0:T(128)} %bitcast.1.which_ref, bf16[1536,3072]{1,0:T(8,128)(2,1)} %w_hbm.5, f32[2,256,1536]{2,1,0:T(8,128)S(1)} %project_early.1.early_ref, bf16[256,128]{1,0:T(8,128)(2,1)S(1)} %get-tuple-element.103.refs_0_, ...), custom_call_target="tpu_custom_call" | custom-call | tf_op jit(solution)/shard_map/project/pallas_call | solution.py:466
  85.7 0.0 collective-permute-done.22
  85.7 1.1 %add_convert_fusion = bf16[256,1536]{1,0:T(8,128)(2,1)} fusion(bf16[256,1536]{1,0:T(8,128)(2,1)S(1)} %collective-permute-done.22, bf16[256,1536]{1,0:T(8,128)(2,1)S(1)} %project.2), kind=kLoop, calls=%fused_computation | loop fusion | flops 1572864 | bytes 2359296 | tf_op jit(solution)/shard_map/convert_element_type | solution.py:559
  (18 shorter events, 0.1 us)
Async XLA Ops:
  2.0 10.1 %collective-permute-start = (bf16[4,256,128]{2,1,0:T(8,128)(2,1)S(1)}, bf16[4,256,128]{2,1,0:T(8,128)(2,1)S(1)}, u32[]{:S(2)}, u32[]{:S(2)}) collective-permute-start(bf16[4,256,128]{2,1,0:T(8,128)(2,1)S(1)} %get-tuple-element.57), channel_id=1, source_target_pairs={{0,2},{2,0},{4,6},{6,4},{1,3},{3,1},{5,7},{7,5},{8,10},{10,8},{12,... | collective-permute-start | bytes 786440 | tf_op jit(solution)/shard_map/ppermute | solution.py:500
  5.0 13.4 %collective-permute-start.1 = (bf16[4,256,128]{2,1,0:T(8,128)(2,1)S(1)}, bf16[4,256,128]{2,1,0:T(8,128)(2,1)S(1)}, u32[]{:S(2)}, u32[]{:S(2)}) collective-permute-start(bf16[4,256,128]{2,1,0:T(8,128)(2,1)S(1)} %get-tuple-element.58), channel_id=1, source_target_pairs={{0,4},{2,6},{4,0},{6,2},{1,5},{3,7},{5,1},{7,3},{8,12},{10,14},{12... | collective-permute-start | bytes 786440 | tf_op jit(solution)/shard_map/ppermute | solution.py:500
  6.5 11.9 %collective-permute-start.2 = (bf16[4,256,128]{2,1,0:T(8,128)(2,1)S(1)}, bf16[4,256,128]{2,1,0:T(8,128)(2,1)S(1)}, u32[]{:S(2)}, u32[]{:S(2)}) collective-permute-start(bf16[4,256,128]{2,1,0:T(8,128)(2,1)S(1)} %get-tuple-element.59), channel_id=1, source_target_pairs={{0,6},{2,4},{4,2},{6,0},{1,7},{3,5},{5,3},{7,1},{8,14},{10,12},{12... | collective-permute-start | bytes 786440 | tf_op jit(solution)/shard_map/ppermute | solution.py:500
  6.5 20.6 %copy-start.5 = (s32[16,16]{1,0:T(8,128)S(1)}, s32[16,16]{1,0:T(8,128)}, u32[]{:S(2)}) copy-start(s32[16,16]{1,0:T(8,128)} %param.10) | copy-start | bytes 3076
  18.5 20.6 %collective-permute-start.10 = (bf16[4,4,256,128]{3,2,1,0:T(8,128)(2,1)S(1)}, bf16[4,4,256,128]{3,2,1,0:T(8,128)(2,1)}, u32[]{:S(2)}, u32[]{:S(2)}) collective-permute-start(bf16[4,4,256,128]{3,2,1,0:T(8,128)(2,1)S(1)} %order.2.refs_5_), channel_id=1, source_target_pairs={{16,8},{8,16},{17,9},{9,17},{18,10},{10,18},{19,11},{11,19},{20,12... | collective-permute-start | bytes 3145736 | tf_op jit(solution)/shard_map/ppermute | solution.py:509
  20.1 25.4 %collective-permute-start.9 = (bf16[4,4,256,128]{3,2,1,0:T(8,128)(2,1)S(1)}, bf16[4,4,256,128]{3,2,1,0:T(8,128)(2,1)}, u32[]{:S(2)}, u32[]{:S(2)}) collective-permute-start(bf16[4,4,256,128]{3,2,1,0:T(8,128)(2,1)S(1)} %order.2.refs_5_), channel_id=1, source_target_pairs={{8,0},{24,16},{0,8},{16,24},{9,1},{25,17},{1,9},{17,25},{10,2},{26... | collective-permute-start | bytes 3145736 | tf_op jit(solution)/shard_map/ppermute | solution.py:509
  23.6 7.8 %collective-permute-start.3 = (bf16[2,256,128]{2,1,0:T(8,128)(2,1)}, bf16[2,256,128]{2,1,0:T(8,128)(2,1)}, u32[]{:S(2)}, u32[]{:S(2)}) collective-permute-start(bf16[2,256,128]{2,1,0:T(8,128)(2,1)} %get-tuple-element.65), channel_id=1, source_target_pairs={{0,2},{2,0},{4,6},{6,4},{1,3},{3,1},{5,7},{7,5},{8,10},{10,8},{12,... | collective-permute-start | bytes 393224 | tf_op jit(solution)/shard_map/ppermute | solution.py:500
  24.8 6.6 %collective-permute-start.4 = (bf16[2,256,128]{2,1,0:T(8,128)(2,1)}, bf16[2,256,128]{2,1,0:T(8,128)(2,1)}, u32[]{:S(2)}, u32[]{:S(2)}) collective-permute-start(bf16[2,256,128]{2,1,0:T(8,128)(2,1)} %get-tuple-element.67), channel_id=1, source_target_pairs={{0,4},{2,6},{4,0},{6,2},{1,5},{3,7},{5,1},{7,3},{8,12},{10,14},{12... | collective-permute-start | bytes 393224 | tf_op jit(solution)/shard_map/ppermute | solution.py:500
  25.7 6.2 %collective-permute-start.5 = (bf16[2,256,128]{2,1,0:T(8,128)(2,1)}, bf16[2,256,128]{2,1,0:T(8,128)(2,1)}, u32[]{:S(2)}, u32[]{:S(2)}) collective-permute-start(bf16[2,256,128]{2,1,0:T(8,128)(2,1)} %get-tuple-element.69), channel_id=1, source_target_pairs={{0,6},{2,4},{4,2},{6,0},{1,7},{3,5},{5,3},{7,1},{8,14},{10,12},{12... | collective-permute-start | bytes 393224 | tf_op jit(solution)/shard_map/ppermute | solution.py:500
  27.2 1.7 %copy-start = (bf16[16,16,1536]{2,1,0:T(8,128)(2,1)S(1)}, bf16[16,16,1536]{2,1,0:T(8,128)(2,1)}, u32[]{:S(2)}) copy-start(bf16[16,16,1536]{2,1,0:T(8,128)(2,1)} %param.6) | copy-start | bytes 2359300
  28.9 21.0 %copy-start.6 = (s32[1,4,2]{1,2,0:T(2,128)S(1)}, s32[1,4,2]{1,2,0:T(2,128)}, u32[]{:S(2)}) copy-start(s32[1,4,2]{1,2,0:T(2,128)} %param.9) | copy-start | bytes 100
  30.7 0.8 copy-start.3
  31.9 18.6 %collective-permute-start.6 = (bf16[1552,128]{1,0:T(8,128)(2,1)}, bf16[1552,128]{1,0:T(8,128)(2,1)}, u32[]{:S(2)}, u32[]{:S(2)}) collective-permute-start(bf16[1552,128]{1,0:T(8,128)(2,1)} %get-tuple-element.72), channel_id=1, source_target_pairs={{0,2},{2,0},{4,6},{6,4},{1,3},{3,1},{5,7},{7,5},{8,10},{10,8},{12,... | collective-permute-start | bytes 1191944 | tf_op jit(solution)/shard_map/ppermute | solution.py:500
  33.3 17.2 %collective-permute-start.8 = (bf16[1552,128]{1,0:T(8,128)(2,1)}, bf16[1552,128]{1,0:T(8,128)(2,1)}, u32[]{:S(2)}, u32[]{:S(2)}) collective-permute-start(bf16[1552,128]{1,0:T(8,128)(2,1)} %get-tuple-element.76), channel_id=1, source_target_pairs={{0,6},{2,4},{4,2},{6,0},{1,7},{3,5},{5,3},{7,1},{8,14},{10,12},{12... | collective-permute-start | bytes 1191944 | tf_op jit(solution)/shard_map/ppermute | solution.py:500
  34.5 17.1 %collective-permute-start.7 = (bf16[1552,128]{1,0:T(8,128)(2,1)}, bf16[1552,128]{1,0:T(8,128)(2,1)}, u32[]{:S(2)}, u32[]{:S(2)}) collective-permute-start(bf16[1552,128]{1,0:T(8,128)(2,1)} %get-tuple-element.74), channel_id=1, source_target_pairs={{0,4},{2,6},{4,0},{6,2},{1,5},{3,7},{5,1},{7,3},{8,12},{10,14},{12... | collective-permute-start | bytes 1191944 | tf_op jit(solution)/shard_map/ppermute | solution.py:500
  36.1 0.9 %copy-start.1 = (bf16[4,3,256,128]{3,2,1,0:T(8,128)(2,1)}, bf16[4,3,256,128]{3,2,1,0:T(8,128)(2,1)S(1)}, u32[]{:S(2)}) copy-start(bf16[4,3,256,128]{3,2,1,0:T(8,128)(2,1)S(1)} %key_features.1.refs_8_) | copy-start | bytes 2359300
  45.5 22.8 %collective-permute-start.18 = (bf16[4,2,256,128]{3,2,1,0:T(8,128)(2,1)}, bf16[4,2,256,128]{3,2,1,0:T(8,128)(2,1)}, u32[]{:S(2)}, u32[]{:S(2)}) collective-permute-start(bf16[4,2,256,128]{3,2,1,0:T(8,128)(2,1)} %order.3.refs_5_), channel_id=1, source_target_pairs={{16,8},{8,16},{17,9},{9,17},{18,10},{10,18},{19,11},{11,19},{20,12... | collective-permute-start | bytes 1572872 | tf_op jit(solution)/shard_map/ppermute | solution.py:509
  47.0 21.3 %collective-permute-start.17 = (bf16[4,2,256,128]{3,2,1,0:T(8,128)(2,1)}, bf16[4,2,256,128]{3,2,1,0:T(8,128)(2,1)}, u32[]{:S(2)}, u32[]{:S(2)}) collective-permute-start(bf16[4,2,256,128]{3,2,1,0:T(8,128)(2,1)} %order.3.refs_5_), channel_id=1, source_target_pairs={{8,0},{24,16},{0,8},{16,24},{9,1},{25,17},{1,9},{17,25},{10,2},{26... | collective-permute-start | bytes 1572872 | tf_op jit(solution)/shard_map/ppermute | solution.py:509
  50.0 5.2 %copy-start.4 = (bf16[1552,128]{1,0:T(8,128)(2,1)S(1)}, bf16[1552,128]{1,0:T(8,128)(2,1)}, u32[]{:S(2)}) copy-start(bf16[1552,128]{1,0:T(8,128)(2,1)} %copy-done.3) | copy-start | bytes 1191940
  50.0 6.1 %copy-start.2 = (bf16[4,3,256,128]{3,2,1,0:T(8,128)(2,1)S(1)}, bf16[4,3,256,128]{3,2,1,0:T(8,128)(2,1)}, u32[]{:S(2)}) copy-start(bf16[4,3,256,128]{3,2,1,0:T(8,128)(2,1)} %copy-done.1) | copy-start | bytes 2359300
  51.6 13.1 %collective-permute-start.14 = (bf16[768,128]{1,0:T(8,128)(2,1)S(1)}, bf16[768,128]{1,0:T(8,128)(2,1)S(1)}, u32[]{:S(2)}, u32[]{:S(2)}) collective-permute-start(bf16[768,128]{1,0:T(8,128)(2,1)S(1)} %get-tuple-element.92), channel_id=1, source_target_pairs={{0,2},{2,0},{4,6},{6,4},{1,3},{3,1},{5,7},{7,5},{8,10},{10,8},{12,... | collective-permute-start | bytes 589832 | tf_op jit(solution)/shard_map/ppermute | solution.py:500
  52.0 13.1 %collective-permute-start.15 = (bf16[768,128]{1,0:T(8,128)(2,1)S(1)}, bf16[768,128]{1,0:T(8,128)(2,1)S(1)}, u32[]{:S(2)}, u32[]{:S(2)}) collective-permute-start(bf16[768,128]{1,0:T(8,128)(2,1)S(1)} %get-tuple-element.94), channel_id=1, source_target_pairs={{0,4},{2,6},{4,0},{6,2},{1,5},{3,7},{5,1},{7,3},{8,12},{10,14},{12... | collective-permute-start | bytes 589832 | tf_op jit(solution)/shard_map/ppermute | solution.py:500
  54.0 13.2 %collective-permute-start.16 = (bf16[768,128]{1,0:T(8,128)(2,1)S(1)}, bf16[768,128]{1,0:T(8,128)(2,1)S(1)}, u32[]{:S(2)}, u32[]{:S(2)}) collective-permute-start(bf16[768,128]{1,0:T(8,128)(2,1)S(1)} %get-tuple-element.96), channel_id=1, source_target_pairs={{0,6},{2,4},{4,2},{6,0},{1,7},{3,5},{5,3},{7,1},{8,14},{10,12},{12... | collective-permute-start | bytes 589832 | tf_op jit(solution)/shard_map/ppermute | solution.py:500
  64.7 10.9 %collective-permute-start.11 = (bf16[512,128]{1,0:T(8,128)(2,1)S(1)}, bf16[512,128]{1,0:T(8,128)(2,1)S(1)}, u32[]{:S(2)}, u32[]{:S(2)}) collective-permute-start(bf16[512,128]{1,0:T(8,128)(2,1)S(1)} %get-tuple-element.83), channel_id=1, source_target_pairs={{0,2},{2,0},{4,6},{6,4},{1,3},{3,1},{5,7},{7,5},{8,10},{10,8},{12,... | collective-permute-start | bytes 393224 | tf_op jit(solution)/shard_map/ppermute | solution.py:500
  65.2 11.6 %collective-permute-start.12 = (bf16[512,128]{1,0:T(8,128)(2,1)S(1)}, bf16[512,128]{1,0:T(8,128)(2,1)S(1)}, u32[]{:S(2)}, u32[]{:S(2)}) collective-permute-start(bf16[512,128]{1,0:T(8,128)(2,1)S(1)} %get-tuple-element.84), channel_id=1, source_target_pairs={{0,4},{2,6},{4,0},{6,2},{1,5},{3,7},{5,1},{7,3},{8,12},{10,14},{12... | collective-permute-start | bytes 393224 | tf_op jit(solution)/shard_map/ppermute | solution.py:500
  67.1 9.7 %collective-permute-start.13 = (bf16[512,128]{1,0:T(8,128)(2,1)S(1)}, bf16[512,128]{1,0:T(8,128)(2,1)S(1)}, u32[]{:S(2)}, u32[]{:S(2)}) collective-permute-start(bf16[512,128]{1,0:T(8,128)(2,1)S(1)} %get-tuple-element.85), channel_id=1, source_target_pairs={{0,6},{2,4},{4,2},{6,0},{1,7},{3,5},{5,3},{7,1},{8,14},{10,12},{12... | collective-permute-start | bytes 393224 | tf_op jit(solution)/shard_map/ppermute | solution.py:500
  73.2 7.4 %collective-permute-start.19 = (bf16[256,128]{1,0:T(8,128)(2,1)S(1)}, bf16[256,128]{1,0:T(8,128)(2,1)S(1)}, u32[]{:S(2)}, u32[]{:S(2)}) collective-permute-start(bf16[256,128]{1,0:T(8,128)(2,1)S(1)} %get-tuple-element.104), channel_id=1, source_target_pairs={{0,2},{2,0},{4,6},{6,4},{1,3},{3,1},{5,7},{7,5},{8,10},{10,8},{12,... | collective-permute-start | bytes 196616 | tf_op jit(solution)/shard_map/ppermute | solution.py:500
  73.7 7.0 %collective-permute-start.20 = (bf16[256,128]{1,0:T(8,128)(2,1)S(1)}, bf16[256,128]{1,0:T(8,128)(2,1)S(1)}, u32[]{:S(2)}, u32[]{:S(2)}) collective-permute-start(bf16[256,128]{1,0:T(8,128)(2,1)S(1)} %get-tuple-element.105), channel_id=1, source_target_pairs={{0,4},{2,6},{4,0},{6,2},{1,5},{3,7},{5,1},{7,3},{8,12},{10,14},{12... | collective-permute-start | bytes 196616 | tf_op jit(solution)/shard_map/ppermute | solution.py:500
  75.6 5.2 %collective-permute-start.21 = (bf16[256,128]{1,0:T(8,128)(2,1)S(1)}, bf16[256,128]{1,0:T(8,128)(2,1)S(1)}, u32[]{:S(2)}, u32[]{:S(2)}) collective-permute-start(bf16[256,128]{1,0:T(8,128)(2,1)S(1)} %get-tuple-element.106), channel_id=1, source_target_pairs={{0,6},{2,4},{4,2},{6,0},{1,7},{3,5},{5,3},{7,1},{8,14},{10,12},{12... | collective-permute-start | bytes 196616 | tf_op jit(solution)/shard_map/ppermute | solution.py:500
  83.2 2.5 %collective-permute-start.22 = (bf16[256,1536]{1,0:T(8,128)(2,1)S(1)}, bf16[256,1536]{1,0:T(8,128)(2,1)S(1)}, u32[]{:S(2)}, u32[]{:S(2)}) collective-permute-start(bf16[256,1536]{1,0:T(8,128)(2,1)S(1)} %project.3), channel_id=1, source_target_pairs={{0,1},{1,0},{2,3},{3,2},{4,5},{5,4},{6,7},{7,6},{8,9},{9,8},{10,11... | collective-permute-start | bytes 2359304 | tf_op jit(solution)/shard_map/ppermute | solution.py:556

commit v3 on v2

--- a/solution.py
+++ b/solution.py
@@ -151,67 +151,78 @@
     ones_block = jnp.ones((block_tokens, HD), jnp.bfloat16)
     for k in range(tiles):
         qr_ref[me_ref[0] ^ k] = come[k][: qr_ref.shape[1]]
-    for head in range(count):
+
+    def pieces(head, w):
+        key_at = head * head_rows + token_count
+        value_at = key_at + per_owner * block_tokens
+        for other in range(max(w - 1, 0), min(w + 2, tiles)):
+            for r, source in enumerate((a_ref, own_ref, b_ref)):
+                yield (
+                    functools.partial(lambda s, o: s[o, 2 * head], source, other),
+                    functools.partial(lambda r, c: kf_ref[r, c], r, other - w + 1),
+                    functools.partial(lambda s, o: s[o, 2 * head + 1], source, other),
+                )
+        for n in range(chosen_count):
+            chosen = ids_ref[w, n]
+            owner = lax.div(chosen, per_owner)
+            start = pl.multiple_of(lax.rem(chosen, per_owner) * block_tokens, block_tokens)
+            yield (
+                functools.partial(lambda o, s: qr_ref[o, pl.ds(key_at + s, block_tokens)], owner, start),
+                lambda: kf_ref[3, 0, :block_tokens],
+                functools.partial(lambda o, s: qr_ref[o, pl.ds(value_at + s, block_tokens)], owner, start),
+            )
+
+    def score(head, w, slot):
         query_at = head * head_rows
-        key_at = query_at + token_count
-        value_at = key_at + per_owner * block_tokens
-        for w in range(tiles):
-            queries = qr_ref[w, query_at : query_at + token_count]
-            q_wide = jnp.concatenate([queries, qf_ref[w]], axis=1)
-            window = []
-            for other in range(max(w - 1, 0), min(w + 2, tiles)):
-                for r, source in enumerate((a_ref, own_ref, b_ref)):
-                    window.append((source, other, r, other - w + 1))
-            at = 0
-            best = None
-
-            def scored(keys, features, at, best):
-                wide = jnp.concatenate([keys, features], axis=1)
-                s = lax.dot_general(
-                    q_wide, wide, (((1,), (1,)), ((), ())), preferred_element_type=jnp.float32
-                )
-                width = s.shape[1]
-                s_ref[:, at : at + width] = s
-                for part in range(0, width, HD):
-                    piece = s[:, part : part + HD]
-                    best = piece if best is None else jnp.maximum(best, piece)
-                return at + width, best
-
-            for source, other, r, c in window:
-                at, best = scored(source[other, 2 * head], kf_ref[r, c], at, best)
-            picks = []
-            for n in range(chosen_count):
-                chosen = ids_ref[w, n]
-                owner = lax.div(chosen, per_owner)
-                start = pl.multiple_of(lax.rem(chosen, per_owner) * block_tokens, block_tokens)
-                picks.append((owner, start))
-                at, best = scored(
-                    qr_ref[owner, pl.ds(key_at + start, block_tokens)],
-                    kf_ref[3, 0, :block_tokens],
-                    at,
-                    best,
-                )
-            row_max = jnp.max(best, axis=1, keepdims=True)
-            at = 0
-            total = jnp.zeros((token_count, 2 * HD), jnp.float32)
-
-            def weighed(values, at, total):
-                width = values.shape[0]
-                probs = jnp.exp2((s_ref[:, at : at + width] - row_max) * factor)
-                total = total + jnp.dot(
-                    probs.astype(jnp.bfloat16), values, preferred_element_type=jnp.float32
-                )
-                return at + width, total
-
-            for source, other, r, c in window:
-                values = source[other, 2 * head + 1]
-                at, total = weighed(jnp.concatenate([values, ones], axis=1), at, total)
-            for owner, start in picks:
-                values = qr_ref[owner, pl.ds(value_at + start, block_tokens)]
-                at, total = weighed(jnp.concatenate([values, ones_block], axis=1), at, total)
-            out_ref[w, head * token_count : (head + 1) * token_count] = (
-                total[:, :HD] / total[:, HD:]
-            ).astype(jnp.bfloat16)
+        q_wide = jnp.concatenate(
+            [qr_ref[w, query_at : query_at + token_count], qf_ref[w]], axis=1
+        )
+        at, best = 0, None
+        for keys, features, _ in pieces(head, w):
+            wide = jnp.concatenate([keys(), features()], axis=1)
+            s = lax.dot_general(
+                q_wide, wide, (((1,), (1,)), ((), ())), preferred_element_type=jnp.float32
+            )
+            s_ref[slot, :, at : at + s.shape[1]] = s
+            at += s.shape[1]
+            for part in range(0, s.shape[1], HD):
+                piece = s[:, part : part + HD]
+                best = piece if best is None else jnp.maximum(best, piece)
+            yield None
+        yield jnp.max(best, axis=1, keepdims=True)
+
+    def weigh(head, w, slot, row_max):
+        at = 0
+        total = jnp.zeros((token_count, 2 * HD), jnp.float32)
+        for _, _, values in pieces(head, w):
+            v = values()
+            width = v.shape[0]
+            probs = jnp.exp2((s_ref[slot, :, at : at + width] - row_max) * factor)
+            total = total + jnp.dot(
+                probs.astype(jnp.bfloat16),
+                jnp.concatenate([v, jnp.ones((width, HD), jnp.bfloat16)], axis=1),
+                preferred_element_type=jnp.float32,
+            )
+            at += width
+            yield None
+        out_ref[w, head * token_count : (head + 1) * token_count] = (
+            total[:, :HD] / total[:, HD:]
+        ).astype(jnp.bfloat16)
+
+    items = [(head, w) for head in range(count) for w in range(tiles)]
+    row_max = None
+    for n in range(len(items) + 1):
+        first = score(*items[n], n % 2) if n < len(items) else iter(())
+        second = weigh(*items[n - 1], 1 - n % 2, row_max) if n else iter(())
+        running = [first, second]
+        while running:
+            for one in list(running):
+                try:
+                    got = next(one)
+                    if got is not None:
+                        row_max = got
+                except StopIteration:
+                    running.remove(one)
     for k in range(tiles):
         o_refs[k][...] = out_ref[me_ref[0] ^ k]
 
@@ -227,11 +238,11 @@
         in_specs=[SMEM] * 2 + [VMEM] * (tiles + 5),
         out_specs=[VMEM] * tiles,
         scratch_shapes=[
-            pltpu.VMEM((token_count, key_count), jnp.float32),
+            pltpu.VMEM((2, token_count, key_count), jnp.float32),
             pltpu.VMEM((tiles, rows, HD), jnp.bfloat16),
             pltpu.VMEM((tiles, count * token_count, HD), jnp.bfloat16),
         ],
-        compiler_params=pltpu.CompilerParams(vmem_limit_bytes=10 << 20),
+        compiler_params=pltpu.CompilerParams(vmem_limit_bytes=12 << 20),
         cost_estimate=pl.CostEstimate(
             flops=count * tiles * 4 * token_count * key_count * HD,
             transcendentals=count * tiles * token_count * key_count,
@@ -393,14 +404,14 @@
     return [flat[n * tiles : (n + 1) * tiles] for n in range(len(chunks))]
 
 
-def fetch_rows(tiles, share, chunk, me_ref, w_hbm, w_ref, sem, columns):
+def fetch_rows(tiles, share, chunk, me_ref, w_hbm, w_ref, sem):
     depth = len(chunk) * HD
     copies = []
     for k in range(tiles):
         first = pl.multiple_of(((me_ref[0] ^ k) * share + chunk[0]) * HD, HD)
         copies.append(
             pltpu.make_async_copy(
-                w_hbm.at[pl.ds(first, depth), columns], w_ref.at[k], sem.at[k]
+                w_hbm.at[pl.ds(first, depth)], w_ref.at[k], sem.at[k]
             )
         )
         copies[-1].start()
@@ -414,10 +425,12 @@
     )
 
 
-def project_early_kernel(tiles, share, chunk, me_ref, w_hbm, *refs):
-    *heads, o_ref, w_ref, sem = refs
+def project_early_kernel(tiles, share, chunks, me_ref, w_hbm, *refs):
+    *heads, o_ref, late_ref, w_ref, sem, late_sem = refs
     width = o_ref.shape[2]
-    copies = fetch_rows(tiles, share, chunk, me_ref, w_hbm, w_ref, sem, slice(None))
+    chunk = chunks[0]
+    copies = fetch_rows(tiles, share, chunk, me_ref, w_hbm, w_ref, sem)
+    late = fetch_rows(tiles, share, chunks[1], me_ref, w_hbm, late_ref, late_sem)
     for k in range(tiles):
         copies[k].wait()
         x = side_by_side(heads[k], len(chunk))
@@ -426,55 +439,56 @@
                 x, w_ref[k, :, half * width : (half + 1) * width], preferred_element_type=jnp.float32
             )
             o_ref[half] = part if k == 0 else o_ref[half] + part
-
-
-def project_early(me, weight, heads, chunk, share):
+    for copy in late:
+        copy.wait()
+
+
+def project_early(me, weight, heads, chunks, share):
+    chunk = chunks[0]
     tiles = len(heads)
     token_count = heads[0].shape[0] // len(chunk)
     width = weight.shape[1]
     return pl.pallas_call(
-        functools.partial(project_early_kernel, tiles, share, chunk),
-        out_shape=jax.ShapeDtypeStruct((2, token_count, width // 2), jnp.float32),
+        functools.partial(project_early_kernel, tiles, share, chunks),
+        out_shape=[
+            jax.ShapeDtypeStruct((2, token_count, width // 2), jnp.float32),
+            jax.ShapeDtypeStruct((tiles, len(chunks[1]) * HD, width), weight.dtype),
+        ],
         in_specs=[SMEM, ANY] + [VMEM] * tiles,
-        out_specs=VMEM,
+        out_specs=[VMEM] * 2,
         scratch_shapes=[
             pltpu.VMEM((tiles, len(chunk) * HD, width), jnp.bfloat16),
             pltpu.SemaphoreType.DMA((tiles,)),
+            pltpu.SemaphoreType.DMA((tiles,)),
         ],
-        compiler_params=pltpu.CompilerParams(vmem_limit_bytes=14 << 20),
+        compiler_params=pltpu.CompilerParams(vmem_limit_bytes=18 << 20),
         name="project_early",
     )(me, pltpu.with_memory_space_constraint(weight, pltpu.HBM), *heads)
 
 
-def project_kernel(tiles, share, chunk, me_ref, which_ref, w_hbm, early_ref, *refs):
-    *heads, o_ref, w_ref, sem = refs
+def project_kernel(tiles, count, which_ref, w_ref, early_ref, *refs):
+    *heads, o_ref = refs
     width = o_ref.shape[1]
     columns = pl.ds(pl.multiple_of(which_ref[0] * width, HD), width)
-    copies = fetch_rows(tiles, share, chunk, me_ref, w_hbm, w_ref, sem, columns)
     total = early_ref[which_ref[0]]
-    for copy in copies:
-        copy.wait()
     for k in range(tiles):
-        x = side_by_side(heads[k], len(chunk))
-        total = total + jnp.dot(x, w_ref[k], preferred_element_type=jnp.float32)
+        total = total + jnp.dot(
+            side_by_side(heads[k], count), w_ref[k, :, columns], preferred_element_type=jnp.float32
+        )
     o_ref[...] = total.astype(o_ref.dtype)
 
 
-def project(me, which, weight, early, heads, chunk, share):
+def project(which, weight, early, heads, count):
     tiles = len(heads)
     _, token_count, width = early.shape
     return pl.pallas_call(
-        functools.partial(project_kernel, tiles, share, chunk),
+        functools.partial(project_kernel, tiles, count),
         out_shape=jax.ShapeDtypeStruct((token_count, width), jnp.bfloat16),
-        in_specs=[SMEM] * 2 + [ANY] + [VMEM] * (1 + tiles),
+        in_specs=[SMEM] + [VMEM] * (2 + tiles),
         out_specs=VMEM,
-        scratch_shapes=[
-            pltpu.VMEM((tiles, len(chunk) * HD, width), jnp.bfloat16),
-            pltpu.SemaphoreType.DMA((tiles,)),
-        ],
         compiler_params=pltpu.CompilerParams(vmem_limit_bytes=10 << 20),
         name="project",
-    )(me, which.reshape(1), pltpu.with_memory_space_constraint(weight, pltpu.HBM), early, *heads)
+    )(which.reshape(1), weight, early, *heads)
 
 
 def in_vmem(*arrays):
@@ -550,11 +564,11 @@
         )
         for n in range(len(chunks))
     ]
-    early = project_early(me, proj_weight, heads[0], chunks[0], share)
+    early, weight = project_early(me, proj_weight, heads[0], chunks, share)
     mine = lax.axis_index("head")
-    theirs = project(me, 1 - mine, proj_weight, early, heads[1], chunks[1], share)
+    theirs = project(1 - mine, weight, early, heads[1], len(chunks[1]))
     got = lax.ppermute(theirs, "head", [(0, 1), (1, 0)])
-    own_part = project(me, mine, proj_weight, early, heads[1], chunks[1], share)
+    own_part = project(mine, weight, early, heads[1], len(chunks[1]))
     total = own_part.astype(jnp.float32) + got.astype(jnp.float32)
     return total.astype(jnp.bfloat16).reshape(tile_rows, tile_cols, -1)
 

time: 87.1 us -> 85.1 us (0.977)
  Pallas kernels: 29.3 us -> 26.3 us
  waiting for transfers between devices: 19.2 us -> 20.3 us
    pallas_call x2, Pallas kernels: 4.75 us -> 1.94 us  [project(): pl.pallas_call(functools.partial(project_kernel, tiles, count), out_shape...]
    ppermute x1, waiting for transfers between devices: 0.01 us -> 1.3 us  [by_head(): got = lax.ppermute(theirs, 'head', [(0, 1), (1, 0)])]
  transfers between devices with their start and end apart: 23 -> 23, of which waited for: 6 -> 6; matrix products, arithmetic and copies ran while one was open for 2% -> 2% of each run, Pallas kernels for 31% -> 29%
where the time goes in v3:
time: 85.1 us; the launch traced here: 84.8 us
  starting transfers between devices  31.7 us (37%)
  Pallas kernels  26.3 us (31%)
  waiting for transfers between devices  20.3 us (24%)
  local copies, waits for them, and re-layouts  5.19 us (6%)
  other arithmetic  1.16 us (1%)
    ppermute x18, starting transfers between devices, swap(): lax.ppermute(x, 'wa', [(i, i ^ k) for i in range(tiles)])  22.1 us
    pallas_call x2, Pallas kernels, attend(): pl.pallas_call(functools.partial(attend_kernel, per_owner, tiles, count),...  13 us
    ppermute x18, waiting for transfers between devices, swap(): lax.ppermute(x, 'wa', [(i, i ^ k) for i in range(tiles)])  12.5 us
    ppermute x4, starting transfers between devices, neighbours(): return [lax.ppermute(x, 'ha', pairs) for pairs in both_ways]  9.47 us
    ppermute x4, waiting for transfers between devices, neighbours(): return [lax.ppermute(x, 'ha', pairs) for pairs in both_ways]  6.48 us
    pallas_call x1, Pallas kernels, project_early(): pl.pallas_call(functools.partial(project_early_kernel, tiles, share, chun...  4.17 us
    unnamed x15, local copies, waits for them, and re-layouts  3.34 us
    pallas_call x2, Pallas kernels, pack_qr(): pl.pallas_call(functools.partial(pack_qr_kernel, tiles, share, chunks), o...  2.27 us
  transfers between devices with their start and end apart: 23, of which 6 were waited for; matrix products, arithmetic and copies ran while one was open for 2% of the time, Pallas kernels for 29%

profile of v3, /device:TPU:0, one launch (start us, length us, event | category | flops | bytes accessed | tf_op | source)
XLA Modules:
  0.0 84.8 jit_solution(1664823584839300290)
XLA Ops:
  0.0 1.7 %copy.7 = bf16[16,16,2,1536]{3,1,0,2:T(8,128)(2,1)S(1)} copy(bf16[16,16,2,1536]{3,2,1,0:T(2,128)(2,1)} %param.7) | data formatting | bytes 3145728 | tf_op args[1]
  1.7 0.3 pack_kv.2
  2.0 3.0 %collective-permute-start = (bf16[4,256,128]{2,1,0:T(8,128)(2,1)S(1)}, bf16[4,256,128]{2,1,0:T(8,128)(2,1)S(1)}, u32[]{:S(2)}, u32[]{:S(2)}) collective-permute-start(bf16[4,256,128]{2,1,0:T(8,128)(2,1)S(1)} %get-tuple-element.59), channel_id=1, source_target_pairs={{0,2},{2,0},{4,6},{6,4},{1,3},{3,1},{5,7},{7,5},{8,10},{10,8},{12,... | collective-permute-start | bytes 786440 | tf_op jit(solution)/shard_map/ppermute | solution.py:514
  5.0 1.5 %collective-permute-start.1 = (bf16[4,256,128]{2,1,0:T(8,128)(2,1)S(1)}, bf16[4,256,128]{2,1,0:T(8,128)(2,1)S(1)}, u32[]{:S(2)}, u32[]{:S(2)}) collective-permute-start(bf16[4,256,128]{2,1,0:T(8,128)(2,1)S(1)} %get-tuple-element.60), channel_id=1, source_target_pairs={{0,4},{2,6},{4,0},{6,2},{1,5},{3,7},{5,1},{7,3},{8,12},{10,14},{12... | collective-permute-start | bytes 786440 | tf_op jit(solution)/shard_map/ppermute | solution.py:514
  6.5 0.0 collective-permute-start.2
  6.5 0.9 %pack_kv.3 = (bf16[2,256,128]{2,1,0:T(8,128)(2,1)S(1)}, bf16[2,256,128]{2,1,0:T(8,128)(2,1)}, bf16[2,256,128]{2,1,0:T(8,128)(2,1)}, bf16[2,256,128]{2,1,0:T(8,128)(2,1)}) custom-call(s32[1]{0:T(128)} %bitcast.1.me_ref, bf16[2,256,1536]{2,1,0:T(8,128)(2,1)S(1)} %bitcast.21), custom_call_target="tpu_custom_call" | custom-call | tf_op jit(solution)/shard_map/pack_kv/pallas_call | solution.py:338
  7.4 4.7 %collective-permute-done.refs_1_ = bf16[4,256,128]{2,1,0:T(8,128)(2,1)S(1)} collective-permute-done((bf16[4,256,128]{2,1,0:T(8,128)(2,1)S(1)}, bf16[4,256,128]{2,1,0:T(8,128)(2,1)S(1)}, u32[]{:S(2)}, u32[]{:S(2)}) %collective-permute-start) | collective-permute-done | bytes 262176 | tf_op jit(solution)/shard_map/ppermute | solution.py:514
  12.1 6.2 %collective-permute-done.1.refs_2_ = bf16[4,256,128]{2,1,0:T(8,128)(2,1)S(1)} collective-permute-done((bf16[4,256,128]{2,1,0:T(8,128)(2,1)S(1)}, bf16[4,256,128]{2,1,0:T(8,128)(2,1)S(1)}, u32[]{:S(2)}, u32[]{:S(2)}) %collective-permute-start.1) | collective-permute-done | bytes 262176 | tf_op jit(solution)/shard_map/ppermute | solution.py:514
  18.4 0.0 collective-permute-done.2.refs_3_
  18.4 0.1 order.2.refs_5_
  18.5 1.6 %collective-permute-start.10 = (bf16[4,4,256,128]{3,2,1,0:T(8,128)(2,1)S(1)}, bf16[4,4,256,128]{3,2,1,0:T(8,128)(2,1)}, u32[]{:S(2)}, u32[]{:S(2)}) collective-permute-start(bf16[4,4,256,128]{3,2,1,0:T(8,128)(2,1)S(1)} %order.2.refs_5_), channel_id=1, source_target_pairs={{16,8},{8,16},{17,9},{9,17},{18,10},{10,18},{19,11},{11,19},{20,12... | collective-permute-start | bytes 3145736 | tf_op jit(solution)/shard_map/ppermute | solution.py:523
  20.1 3.5 %collective-permute-start.9 = (bf16[4,4,256,128]{3,2,1,0:T(8,128)(2,1)S(1)}, bf16[4,4,256,128]{3,2,1,0:T(8,128)(2,1)}, u32[]{:S(2)}, u32[]{:S(2)}) collective-permute-start(bf16[4,4,256,128]{3,2,1,0:T(8,128)(2,1)S(1)} %order.2.refs_5_), channel_id=1, source_target_pairs={{8,0},{24,16},{0,8},{16,24},{9,1},{25,17},{1,9},{17,25},{10,2},{26... | collective-permute-start | bytes 3145736 | tf_op jit(solution)/shard_map/ppermute | solution.py:523
  23.6 1.2 %collective-permute-start.3 = (bf16[2,256,128]{2,1,0:T(8,128)(2,1)}, bf16[2,256,128]{2,1,0:T(8,128)(2,1)}, u32[]{:S(2)}, u32[]{:S(2)}) collective-permute-start(bf16[2,256,128]{2,1,0:T(8,128)(2,1)} %get-tuple-element.67), channel_id=1, source_target_pairs={{0,2},{2,0},{4,6},{6,4},{1,3},{3,1},{5,7},{7,5},{8,10},{10,8},{12,... | collective-permute-start | bytes 393224 | tf_op jit(solution)/shard_map/ppermute | solution.py:514
  24.8 0.8 collective-permute-start.4
  25.7 1.4 %collective-permute-start.5 = (bf16[2,256,128]{2,1,0:T(8,128)(2,1)}, bf16[2,256,128]{2,1,0:T(8,128)(2,1)}, u32[]{:S(2)}, u32[]{:S(2)}) collective-permute-start(bf16[2,256,128]{2,1,0:T(8,128)(2,1)} %get-tuple-element.71), channel_id=1, source_target_pairs={{0,6},{2,4},{4,2},{6,0},{1,7},{3,5},{5,3},{7,1},{8,14},{10,12},{12... | collective-permute-start | bytes 393224 | tf_op jit(solution)/shard_map/ppermute | solution.py:514
  27.1 0.1 reshape.30
  27.2 1.7 %copy.8 = bf16[2,128,2,1536]{3,1,0,2:T(8,128)(2,1)S(1)} copy(bf16[2,128,2,1536]{3,2,1,0:T(2,128)(2,1)} %param.8) | data formatting | bytes 3145728 | tf_op jit(solution)/shard_map/optimization_barrier | solution.py:542
  28.9 0.0 copy-start.6
  28.9 1.7 %pack_qr.2 = (bf16[1552,128]{1,0:T(8,128)(2,1)S(1)}, bf16[1552,128]{1,0:T(8,128)(2,1)}, bf16[1552,128]{1,0:T(8,128)(2,1)}, bf16[1552,128]{1,0:T(8,128)(2,1)}) custom-call(s32[1]{0:T(128)} %bitcast.1.me_ref, bf16[256,1536]{1,0:T(8,128)(2,1)S(1)} %bitcast.24, bf16[2,256,1536]{2,1,0:T(8,128)(2,1)S(1)} %bitcast.22, bf16[16,128]{1,0:T(8,128)(2,1)S(1)} %pad.5.f_ref), custom_call_target="tpu_custom_call" | custom-call | tf_op jit(solution)/shard_map/pack_qr/pallas_call | solution.py:395
  30.7 0.8 copy-done.3
  31.5 0.0 collective-permute-done.3.refs_1_
  31.5 0.0 collective-permute-done.4.refs_2_
  31.5 0.4 collective-permute-done.5.refs_3_
  31.9 1.5 %collective-permute-start.6 = (bf16[1552,128]{1,0:T(8,128)(2,1)}, bf16[1552,128]{1,0:T(8,128)(2,1)}, u32[]{:S(2)}, u32[]{:S(2)}) collective-permute-start(bf16[1552,128]{1,0:T(8,128)(2,1)} %get-tuple-element.74), channel_id=1, source_target_pairs={{0,2},{2,0},{4,6},{6,4},{1,3},{3,1},{5,7},{7,5},{8,10},{10,8},{12,... | collective-permute-start | bytes 1191944 | tf_op jit(solution)/shard_map/ppermute | solution.py:514
  33.3 1.2 %collective-permute-start.8 = (bf16[1552,128]{1,0:T(8,128)(2,1)}, bf16[1552,128]{1,0:T(8,128)(2,1)}, u32[]{:S(2)}, u32[]{:S(2)}) collective-permute-start(bf16[1552,128]{1,0:T(8,128)(2,1)} %get-tuple-element.78), channel_id=1, source_target_pairs={{0,6},{2,4},{4,2},{6,0},{1,7},{3,5},{5,3},{7,1},{8,14},{10,12},{12... | collective-permute-start | bytes 1191944 | tf_op jit(solution)/shard_map/ppermute | solution.py:514
  34.5 0.8 collective-permute-start.7
  35.3 0.1 add_bitcast_fusion
  35.4 0.7 key_features.1.refs_8_
  36.1 0.0 copy-start.1
  36.1 0.9 %copy-done.1 = bf16[4,3,256,128]{3,2,1,0:T(8,128)(2,1)} copy-done((bf16[4,3,256,128]{3,2,1,0:T(8,128)(2,1)}, bf16[4,3,256,128]{3,2,1,0:T(8,128)(2,1)S(1)}, u32[]{:S(2)}) %copy-start.1) | copy-done | bytes 786456
  37.0 2.0 %order.3.refs_5_ = bf16[4,2,256,128]{3,2,1,0:T(8,128)(2,1)} custom-call(s32[1]{0:T(128)} %bitcast.1.me_ref, bf16[2,256,128]{2,1,0:T(8,128)(2,1)S(1)} %get-tuple-element.102.refs_0_, bf16[2,256,128]{2,1,0:T(8,128)(2,1)} %collective-permute-done.3.refs_1_, bf16[2,256,128]{2,1,0:T(8,128)(2,1)} %collective-permute-done.4.refs_2_, ...), custom_call_target="tpu_custom_call" | custom-call | tf_op jit(solution)/shard_map/order/pallas_call | solution.py:356
  39.0 0.0 collective-permute-done.10.refs_7_
  39.0 6.5 %collective-permute-done.9.refs_6_ = bf16[4,4,256,128]{3,2,1,0:T(8,128)(2,1)} collective-permute-done((bf16[4,4,256,128]{3,2,1,0:T(8,128)(2,1)S(1)}, bf16[4,4,256,128]{3,2,1,0:T(8,128)(2,1)}, u32[]{:S(2)}, u32[]{:S(2)}) %collective-permute-start.9) | collective-permute-done | bytes 1048608 | tf_op jit(solution)/shard_map/ppermute | solution.py:523
  45.5 1.5 %collective-permute-start.18 = (bf16[4,2,256,128]{3,2,1,0:T(8,128)(2,1)}, bf16[4,2,256,128]{3,2,1,0:T(8,128)(2,1)}, u32[]{:S(2)}, u32[]{:S(2)}) collective-permute-start(bf16[4,2,256,128]{3,2,1,0:T(8,128)(2,1)} %order.3.refs_5_), channel_id=1, source_target_pairs={{16,8},{8,16},{17,9},{9,17},{18,10},{10,18},{19,11},{11,19},{20,12... | collective-permute-start | bytes 1572872 | tf_op jit(solution)/shard_map/ppermute | solution.py:523
  47.0 2.9 %collective-permute-start.17 = (bf16[4,2,256,128]{3,2,1,0:T(8,128)(2,1)}, bf16[4,2,256,128]{3,2,1,0:T(8,128)(2,1)}, u32[]{:S(2)}, u32[]{:S(2)}) collective-permute-start(bf16[4,2,256,128]{3,2,1,0:T(8,128)(2,1)} %order.3.refs_5_), channel_id=1, source_target_pairs={{8,0},{24,16},{0,8},{16,24},{9,1},{25,17},{1,9},{17,25},{10,2},{26... | collective-permute-start | bytes 1572872 | tf_op jit(solution)/shard_map/ppermute | solution.py:523
  49.9 0.1 copy.9.ids_ref
  50.0 0.5 pack_qr.3
  50.5 0.0 collective-permute-done.6.refs_1_
  50.5 1.1 %collective-permute-done.7.refs_2_ = bf16[1552,128]{1,0:T(8,128)(2,1)} collective-permute-done((bf16[1552,128]{1,0:T(8,128)(2,1)}, bf16[1552,128]{1,0:T(8,128)(2,1)}, u32[]{:S(2)}, u32[]{:S(2)}) %collective-permute-start.7) | collective-permute-done | bytes 397344 | tf_op jit(solution)/shard_map/ppermute | solution.py:514
  51.6 0.4 collective-permute-start.14
  52.0 2.0 %collective-permute-start.15 = (bf16[768,128]{1,0:T(8,128)(2,1)S(1)}, bf16[768,128]{1,0:T(8,128)(2,1)S(1)}, u32[]{:S(2)}, u32[]{:S(2)}) collective-permute-start(bf16[768,128]{1,0:T(8,128)(2,1)S(1)} %get-tuple-element.98), channel_id=1, source_target_pairs={{0,4},{2,6},{4,0},{6,2},{1,5},{3,7},{5,1},{7,3},{8,12},{10,14},{12... | collective-permute-start | bytes 589832 | tf_op jit(solution)/shard_map/ppermute | solution.py:514
  54.0 1.1 %collective-permute-start.16 = (bf16[768,128]{1,0:T(8,128)(2,1)S(1)}, bf16[768,128]{1,0:T(8,128)(2,1)S(1)}, u32[]{:S(2)}, u32[]{:S(2)}) collective-permute-start(bf16[768,128]{1,0:T(8,128)(2,1)S(1)} %get-tuple-element.100), channel_id=1, source_target_pairs={{0,6},{2,4},{4,2},{6,0},{1,7},{3,5},{5,3},{7,1},{8,14},{10,12},{12... | collective-permute-start | bytes 589832 | tf_op jit(solution)/shard_map/ppermute | solution.py:514
  55.1 0.9 %query_features.1.refs_4_ = bf16[4,256,128]{2,1,0:T(8,128)(2,1)S(1)} custom-call(s32[1]{0:T(128)} %bitcast.1.me_ref, bf16[1552,128]{1,0:T(8,128)(2,1)S(1)} %copy-done.4, bf16[1552,128]{1,0:T(8,128)(2,1)} %collective-permute-done.6.refs_1_, bf16[1552,128]{1,0:T(8,128)(2,1)} %collective-permute-done.7.refs_2_, bf16[1552,128]{1,0:T(8,128)(2,1)} %collective-permute-done.8.refs_3_), custom_call_target="tpu_custom_call" | custom-call | tf_op jit(solution)/shard_map/query_features/pallas_call | solution.py:283
  56.1 8.2 %attend.2 = (bf16[512,128]{1,0:T(8,128)(2,1)S(1)}, bf16[512,128]{1,0:T(8,128)(2,1)S(1)}, bf16[512,128]{1,0:T(8,128)(2,1)S(1)}, bf16[512,128]{1,0:T(8,128)(2,1)S(1)}) custom-call(s32[1]{0:T(128)} %bitcast.1.me_ref, s32[4,2]{1,0:T(4,128)S(1)} %copy.9.ids_ref, bf16[1552,128]{1,0:T(8,128)(2,1)S(1)} %copy-done.4, ...), custom_call_target="tpu_custom_call" | custom-call | flops 2952790016 | bytes 3145728 | tf_op jit(solution)/shard_map/attend/pallas_call | solution.py:235
  64.3 0.0 collective-permute-done.14.refs_1_
  64.3 0.4 collective-permute-start.11
  64.8 0.0 collective-permute-done.15.refs_2_
  64.8 2.0 %collective-permute-start.12 = (bf16[512,128]{1,0:T(8,128)(2,1)S(1)}, bf16[512,128]{1,0:T(8,128)(2,1)S(1)}, u32[]{:S(2)}, u32[]{:S(2)}) collective-permute-start(bf16[512,128]{1,0:T(8,128)(2,1)S(1)} %get-tuple-element.86), channel_id=1, source_target_pairs={{0,4},{2,6},{4,0},{6,2},{1,5},{3,7},{5,1},{7,3},{8,12},{10,14},{12... | collective-permute-start | bytes 393224 | tf_op jit(solution)/shard_map/ppermute | solution.py:514
  66.7 1.1 %collective-permute-start.13 = (bf16[512,128]{1,0:T(8,128)(2,1)S(1)}, bf16[512,128]{1,0:T(8,128)(2,1)S(1)}, u32[]{:S(2)}, u32[]{:S(2)}) collective-permute-start(bf16[512,128]{1,0:T(8,128)(2,1)S(1)} %get-tuple-element.87), channel_id=1, source_target_pairs={{0,6},{2,4},{4,2},{6,0},{1,7},{3,5},{5,3},{7,1},{8,14},{10,12},{12... | collective-permute-start | bytes 393224 | tf_op jit(solution)/shard_map/ppermute | solution.py:514
  67.9 0.0 collective-permute-done.17.refs_6_
  67.9 4.8 %attend.3 = (bf16[256,128]{1,0:T(8,128)(2,1)S(1)}, bf16[256,128]{1,0:T(8,128)(2,1)S(1)}, bf16[256,128]{1,0:T(8,128)(2,1)S(1)}, bf16[256,128]{1,0:T(8,128)(2,1)S(1)}) custom-call(s32[1]{0:T(128)} %bitcast.1.me_ref, s32[4,2]{1,0:T(4,128)S(1)} %copy.9.ids_ref, bf16[768,128]{1,0:T(8,128)(2,1)S(1)} %get-tuple-element.94.refs_0_, ...), custom_call_target="tpu_custom_call" | custom-call | flops 1476395008 | bytes 1572864 | tf_op jit(solution)/shard_map/attend/pallas_call | solution.py:235
  72.7 0.5 collective-permute-start.19
  73.1 2.0 %collective-permute-start.20 = (bf16[256,128]{1,0:T(8,128)(2,1)S(1)}, bf16[256,128]{1,0:T(8,128)(2,1)S(1)}, u32[]{:S(2)}, u32[]{:S(2)}) collective-permute-start(bf16[256,128]{1,0:T(8,128)(2,1)S(1)} %get-tuple-element.109), channel_id=1, source_target_pairs={{0,4},{2,6},{4,0},{6,2},{1,5},{3,7},{5,1},{7,3},{8,12},{10,14},{12... | collective-permute-start | bytes 196616 | tf_op jit(solution)/shard_map/ppermute | solution.py:514
  75.1 1.1 %collective-permute-start.21 = (bf16[256,128]{1,0:T(8,128)(2,1)S(1)}, bf16[256,128]{1,0:T(8,128)(2,1)S(1)}, u32[]{:S(2)}, u32[]{:S(2)}) collective-permute-start(bf16[256,128]{1,0:T(8,128)(2,1)S(1)} %get-tuple-element.110), channel_id=1, source_target_pairs={{0,6},{2,4},{4,2},{6,0},{1,7},{3,5},{5,3},{7,1},{8,14},{10,12},{12... | collective-permute-start | bytes 196616 | tf_op jit(solution)/shard_map/ppermute | solution.py:514
  76.2 0.0 collective-permute-done.12.refs_2_
  76.2 0.0 collective-permute-done.13.refs_3_
  76.2 4.2 %project_early.1 = (f32[2,256,1536]{2,1,0:T(8,128)S(1)}, bf16[4,128,3072]{2,1,0:T(8,128)(2,1)S(1)}) custom-call(s32[1]{0:T(128)} %bitcast.1.me_ref, bf16[1536,3072]{1,0:T(8,128)(2,1)} %w_hbm.1, bf16[512,128]{1,0:T(8,128)(2,1)S(1)} %get-tuple-element.84.refs_0_, bf16[512,128]{1,0:T(8,128)(2,1)S(1)} %collective-permute-done.11.refs_1_, ...), custom_call_target="tpu_custom_call" | custom-call | tf_op jit(solution)/shard_map/project_early/pallas_call | solution.py:451
  80.4 0.0 collective-permute-done.19.refs_1_
  80.4 0.0 collective-permute-done.21.refs_3_
  80.4 1.0 %project.3 = bf16[256,1536]{1,0:T(8,128)(2,1)S(1)} custom-call(s32[1]{0:T(128)} %bitcast.16.which_ref, bf16[4,128,3072]{2,1,0:T(8,128)(2,1)S(1)} %get-tuple-element.88.w_ref, f32[2,256,1536]{2,1,0:T(8,128)S(1)} %get-tuple-element.89.early_ref, bf16[256,128]{1,0:T(8,128)(2,1)S(1)} %get-tuple-element.107.refs_0_, ...), custom_call_target="tpu_custom_call" | custom-call | tf_op jit(solution)/shard_map/project/pallas_call | solution.py:484
  81.4 0.1 collective-permute-start.22
  81.5 1.0 %project.2 = bf16[256,1536]{1,0:T(8,128)(2,1)S(1)} custom-call(s32[1]{0:T(128)} %bitcast.which_ref, bf16[4,128,3072]{2,1,0:T(8,128)(2,1)S(1)} %get-tuple-element.88.w_ref, f32[2,256,1536]{2,1,0:T(8,128)S(1)} %get-tuple-element.89.early_ref, bf16[256,128]{1,0:T(8,128)(2,1)S(1)} %get-tuple-element.107.refs_0_, ...), custom_call_target="tpu_custom_call" | custom-call | tf_op jit(solution)/shard_map/project/pallas_call | solution.py:484
  82.5 1.3 %collective-permute-done.22 = bf16[256,1536]{1,0:T(8,128)(2,1)S(1)} collective-permute-done((bf16[256,1536]{1,0:T(8,128)(2,1)S(1)}, bf16[256,1536]{1,0:T(8,128)(2,1)S(1)}, u32[]{:S(2)}, u32[]{:S(2)}) %collective-permute-start.22) | collective-permute-done | bytes 786464 | tf_op jit(solution)/shard_map/ppermute | solution.py:570
  83.8 1.1 %add_convert_fusion = bf16[256,1536]{1,0:T(8,128)(2,1)} fusion(bf16[256,1536]{1,0:T(8,128)(2,1)S(1)} %collective-permute-done.22, bf16[256,1536]{1,0:T(8,128)(2,1)S(1)} %project.2), kind=kLoop, calls=%fused_computation | loop fusion | flops 1572864 | bytes 2359296 | tf_op jit(solution)/shard_map/convert_element_type | solution.py:573
  (18 shorter events, 0.1 us)
Async XLA Ops:
  2.0 10.1 %collective-permute-start = (bf16[4,256,128]{2,1,0:T(8,128)(2,1)S(1)}, bf16[4,256,128]{2,1,0:T(8,128)(2,1)S(1)}, u32[]{:S(2)}, u32[]{:S(2)}) collective-permute-start(bf16[4,256,128]{2,1,0:T(8,128)(2,1)S(1)} %get-tuple-element.59), channel_id=1, source_target_pairs={{0,2},{2,0},{4,6},{6,4},{1,3},{3,1},{5,7},{7,5},{8,10},{10,8},{12,... | collective-permute-start | bytes 786440 | tf_op jit(solution)/shard_map/ppermute | solution.py:514
  5.0 13.4 %collective-permute-start.1 = (bf16[4,256,128]{2,1,0:T(8,128)(2,1)S(1)}, bf16[4,256,128]{2,1,0:T(8,128)(2,1)S(1)}, u32[]{:S(2)}, u32[]{:S(2)}) collective-permute-start(bf16[4,256,128]{2,1,0:T(8,128)(2,1)S(1)} %get-tuple-element.60), channel_id=1, source_target_pairs={{0,4},{2,6},{4,0},{6,2},{1,5},{3,7},{5,1},{7,3},{8,12},{10,14},{12... | collective-permute-start | bytes 786440 | tf_op jit(solution)/shard_map/ppermute | solution.py:514
  6.5 11.9 %collective-permute-start.2 = (bf16[4,256,128]{2,1,0:T(8,128)(2,1)S(1)}, bf16[4,256,128]{2,1,0:T(8,128)(2,1)S(1)}, u32[]{:S(2)}, u32[]{:S(2)}) collective-permute-start(bf16[4,256,128]{2,1,0:T(8,128)(2,1)S(1)} %get-tuple-element.61), channel_id=1, source_target_pairs={{0,6},{2,4},{4,2},{6,0},{1,7},{3,5},{5,3},{7,1},{8,14},{10,12},{12... | collective-permute-start | bytes 786440 | tf_op jit(solution)/shard_map/ppermute | solution.py:514
  6.5 20.6 %copy-start.5 = (s32[16,16]{1,0:T(8,128)S(1)}, s32[16,16]{1,0:T(8,128)}, u32[]{:S(2)}) copy-start(s32[16,16]{1,0:T(8,128)} %param.10) | copy-start | bytes 3076
  18.5 20.6 %collective-permute-start.10 = (bf16[4,4,256,128]{3,2,1,0:T(8,128)(2,1)S(1)}, bf16[4,4,256,128]{3,2,1,0:T(8,128)(2,1)}, u32[]{:S(2)}, u32[]{:S(2)}) collective-permute-start(bf16[4,4,256,128]{3,2,1,0:T(8,128)(2,1)S(1)} %order.2.refs_5_), channel_id=1, source_target_pairs={{16,8},{8,16},{17,9},{9,17},{18,10},{10,18},{19,11},{11,19},{20,12... | collective-permute-start | bytes 3145736 | tf_op jit(solution)/shard_map/ppermute | solution.py:523
  20.1 25.4 %collective-permute-start.9 = (bf16[4,4,256,128]{3,2,1,0:T(8,128)(2,1)S(1)}, bf16[4,4,256,128]{3,2,1,0:T(8,128)(2,1)}, u32[]{:S(2)}, u32[]{:S(2)}) collective-permute-start(bf16[4,4,256,128]{3,2,1,0:T(8,128)(2,1)S(1)} %order.2.refs_5_), channel_id=1, source_target_pairs={{8,0},{24,16},{0,8},{16,24},{9,1},{25,17},{1,9},{17,25},{10,2},{26... | collective-permute-start | bytes 3145736 | tf_op jit(solution)/shard_map/ppermute | solution.py:523
  23.6 7.8 %collective-permute-start.3 = (bf16[2,256,128]{2,1,0:T(8,128)(2,1)}, bf16[2,256,128]{2,1,0:T(8,128)(2,1)}, u32[]{:S(2)}, u32[]{:S(2)}) collective-permute-start(bf16[2,256,128]{2,1,0:T(8,128)(2,1)} %get-tuple-element.67), channel_id=1, source_target_pairs={{0,2},{2,0},{4,6},{6,4},{1,3},{3,1},{5,7},{7,5},{8,10},{10,8},{12,... | collective-permute-start | bytes 393224 | tf_op jit(solution)/shard_map/ppermute | solution.py:514
  24.8 6.6 %collective-permute-start.4 = (bf16[2,256,128]{2,1,0:T(8,128)(2,1)}, bf16[2,256,128]{2,1,0:T(8,128)(2,1)}, u32[]{:S(2)}, u32[]{:S(2)}) collective-permute-start(bf16[2,256,128]{2,1,0:T(8,128)(2,1)} %get-tuple-element.69), channel_id=1, source_target_pairs={{0,4},{2,6},{4,0},{6,2},{1,5},{3,7},{5,1},{7,3},{8,12},{10,14},{12... | collective-permute-start | bytes 393224 | tf_op jit(solution)/shard_map/ppermute | solution.py:514
  25.7 6.2 %collective-permute-start.5 = (bf16[2,256,128]{2,1,0:T(8,128)(2,1)}, bf16[2,256,128]{2,1,0:T(8,128)(2,1)}, u32[]{:S(2)}, u32[]{:S(2)}) collective-permute-start(bf16[2,256,128]{2,1,0:T(8,128)(2,1)} %get-tuple-element.71), channel_id=1, source_target_pairs={{0,6},{2,4},{4,2},{6,0},{1,7},{3,5},{5,3},{7,1},{8,14},{10,12},{12... | collective-permute-start | bytes 393224 | tf_op jit(solution)/shard_map/ppermute | solution.py:514
  27.2 1.7 %copy-start = (bf16[16,16,1536]{2,1,0:T(8,128)(2,1)S(1)}, bf16[16,16,1536]{2,1,0:T(8,128)(2,1)}, u32[]{:S(2)}) copy-start(bf16[16,16,1536]{2,1,0:T(8,128)(2,1)} %param.6) | copy-start | bytes 2359300
  28.9 21.0 %copy-start.6 = (s32[1,4,2]{1,2,0:T(2,128)S(1)}, s32[1,4,2]{1,2,0:T(2,128)}, u32[]{:S(2)}) copy-start(s32[1,4,2]{1,2,0:T(2,128)} %param.9) | copy-start | bytes 100
  30.7 0.8 copy-start.3
  31.9 18.6 %collective-permute-start.6 = (bf16[1552,128]{1,0:T(8,128)(2,1)}, bf16[1552,128]{1,0:T(8,128)(2,1)}, u32[]{:S(2)}, u32[]{:S(2)}) collective-permute-start(bf16[1552,128]{1,0:T(8,128)(2,1)} %get-tuple-element.74), channel_id=1, source_target_pairs={{0,2},{2,0},{4,6},{6,4},{1,3},{3,1},{5,7},{7,5},{8,10},{10,8},{12,... | collective-permute-start | bytes 1191944 | tf_op jit(solution)/shard_map/ppermute | solution.py:514
  33.3 17.2 %collective-permute-start.8 = (bf16[1552,128]{1,0:T(8,128)(2,1)}, bf16[1552,128]{1,0:T(8,128)(2,1)}, u32[]{:S(2)}, u32[]{:S(2)}) collective-permute-start(bf16[1552,128]{1,0:T(8,128)(2,1)} %get-tuple-element.78), channel_id=1, source_target_pairs={{0,6},{2,4},{4,2},{6,0},{1,7},{3,5},{5,3},{7,1},{8,14},{10,12},{12... | collective-permute-start | bytes 1191944 | tf_op jit(solution)/shard_map/ppermute | solution.py:514
  34.5 17.1 %collective-permute-start.7 = (bf16[1552,128]{1,0:T(8,128)(2,1)}, bf16[1552,128]{1,0:T(8,128)(2,1)}, u32[]{:S(2)}, u32[]{:S(2)}) collective-permute-start(bf16[1552,128]{1,0:T(8,128)(2,1)} %get-tuple-element.76), channel_id=1, source_target_pairs={{0,4},{2,6},{4,0},{6,2},{1,5},{3,7},{5,1},{7,3},{8,12},{10,14},{12... | collective-permute-start | bytes 1191944 | tf_op jit(solution)/shard_map/ppermute | solution.py:514
  36.1 0.9 %copy-start.1 = (bf16[4,3,256,128]{3,2,1,0:T(8,128)(2,1)}, bf16[4,3,256,128]{3,2,1,0:T(8,128)(2,1)S(1)}, u32[]{:S(2)}) copy-start(bf16[4,3,256,128]{3,2,1,0:T(8,128)(2,1)S(1)} %key_features.1.refs_8_) | copy-start | bytes 2359300
  45.5 22.4 %collective-permute-start.18 = (bf16[4,2,256,128]{3,2,1,0:T(8,128)(2,1)}, bf16[4,2,256,128]{3,2,1,0:T(8,128)(2,1)}, u32[]{:S(2)}, u32[]{:S(2)}) collective-permute-start(bf16[4,2,256,128]{3,2,1,0:T(8,128)(2,1)} %order.3.refs_5_), channel_id=1, source_target_pairs={{16,8},{8,16},{17,9},{9,17},{18,10},{10,18},{19,11},{11,19},{20,12... | collective-permute-start | bytes 1572872 | tf_op jit(solution)/shard_map/ppermute | solution.py:523
  47.0 20.9 %collective-permute-start.17 = (bf16[4,2,256,128]{3,2,1,0:T(8,128)(2,1)}, bf16[4,2,256,128]{3,2,1,0:T(8,128)(2,1)}, u32[]{:S(2)}, u32[]{:S(2)}) collective-permute-start(bf16[4,2,256,128]{3,2,1,0:T(8,128)(2,1)} %order.3.refs_5_), channel_id=1, source_target_pairs={{8,0},{24,16},{0,8},{16,24},{9,1},{25,17},{1,9},{17,25},{10,2},{26... | collective-permute-start | bytes 1572872 | tf_op jit(solution)/shard_map/ppermute | solution.py:523
  50.0 5.2 %copy-start.4 = (bf16[1552,128]{1,0:T(8,128)(2,1)S(1)}, bf16[1552,128]{1,0:T(8,128)(2,1)}, u32[]{:S(2)}) copy-start(bf16[1552,128]{1,0:T(8,128)(2,1)} %copy-done.3) | copy-start | bytes 1191940
  50.0 6.1 %copy-start.2 = (bf16[4,3,256,128]{3,2,1,0:T(8,128)(2,1)S(1)}, bf16[4,3,256,128]{3,2,1,0:T(8,128)(2,1)}, u32[]{:S(2)}) copy-start(bf16[4,3,256,128]{3,2,1,0:T(8,128)(2,1)} %copy-done.1) | copy-start | bytes 2359300
  51.6 12.7 %collective-permute-start.14 = (bf16[768,128]{1,0:T(8,128)(2,1)S(1)}, bf16[768,128]{1,0:T(8,128)(2,1)S(1)}, u32[]{:S(2)}, u32[]{:S(2)}) collective-permute-start(bf16[768,128]{1,0:T(8,128)(2,1)S(1)} %get-tuple-element.96), channel_id=1, source_target_pairs={{0,2},{2,0},{4,6},{6,4},{1,3},{3,1},{5,7},{7,5},{8,10},{10,8},{12,... | collective-permute-start | bytes 589832 | tf_op jit(solution)/shard_map/ppermute | solution.py:514
  52.0 12.7 %collective-permute-start.15 = (bf16[768,128]{1,0:T(8,128)(2,1)S(1)}, bf16[768,128]{1,0:T(8,128)(2,1)S(1)}, u32[]{:S(2)}, u32[]{:S(2)}) collective-permute-start(bf16[768,128]{1,0:T(8,128)(2,1)S(1)} %get-tuple-element.98), channel_id=1, source_target_pairs={{0,4},{2,6},{4,0},{6,2},{1,5},{3,7},{5,1},{7,3},{8,12},{10,14},{12... | collective-permute-start | bytes 589832 | tf_op jit(solution)/shard_map/ppermute | solution.py:514
  54.0 12.7 %collective-permute-start.16 = (bf16[768,128]{1,0:T(8,128)(2,1)S(1)}, bf16[768,128]{1,0:T(8,128)(2,1)S(1)}, u32[]{:S(2)}, u32[]{:S(2)}) collective-permute-start(bf16[768,128]{1,0:T(8,128)(2,1)S(1)} %get-tuple-element.100), channel_id=1, source_target_pairs={{0,6},{2,4},{4,2},{6,0},{1,7},{3,5},{5,3},{7,1},{8,14},{10,12},{12... | collective-permute-start | bytes 589832 | tf_op jit(solution)/shard_map/ppermute | solution.py:514
  64.3 10.8 %collective-permute-start.11 = (bf16[512,128]{1,0:T(8,128)(2,1)S(1)}, bf16[512,128]{1,0:T(8,128)(2,1)S(1)}, u32[]{:S(2)}, u32[]{:S(2)}) collective-permute-start(bf16[512,128]{1,0:T(8,128)(2,1)S(1)} %get-tuple-element.85), channel_id=1, source_target_pairs={{0,2},{2,0},{4,6},{6,4},{1,3},{3,1},{5,7},{7,5},{8,10},{10,8},{12,... | collective-permute-start | bytes 393224 | tf_op jit(solution)/shard_map/ppermute | solution.py:514
  64.8 11.5 %collective-permute-start.12 = (bf16[512,128]{1,0:T(8,128)(2,1)S(1)}, bf16[512,128]{1,0:T(8,128)(2,1)S(1)}, u32[]{:S(2)}, u32[]{:S(2)}) collective-permute-start(bf16[512,128]{1,0:T(8,128)(2,1)S(1)} %get-tuple-element.86), channel_id=1, source_target_pairs={{0,4},{2,6},{4,0},{6,2},{1,5},{3,7},{5,1},{7,3},{8,12},{10,14},{12... | collective-permute-start | bytes 393224 | tf_op jit(solution)/shard_map/ppermute | solution.py:514
  66.7 9.5 %collective-permute-start.13 = (bf16[512,128]{1,0:T(8,128)(2,1)S(1)}, bf16[512,128]{1,0:T(8,128)(2,1)S(1)}, u32[]{:S(2)}, u32[]{:S(2)}) collective-permute-start(bf16[512,128]{1,0:T(8,128)(2,1)S(1)} %get-tuple-element.87), channel_id=1, source_target_pairs={{0,6},{2,4},{4,2},{6,0},{1,7},{3,5},{5,3},{7,1},{8,14},{10,12},{12... | collective-permute-start | bytes 393224 | tf_op jit(solution)/shard_map/ppermute | solution.py:514
  72.7 7.7 %collective-permute-start.19 = (bf16[256,128]{1,0:T(8,128)(2,1)S(1)}, bf16[256,128]{1,0:T(8,128)(2,1)S(1)}, u32[]{:S(2)}, u32[]{:S(2)}) collective-permute-start(bf16[256,128]{1,0:T(8,128)(2,1)S(1)} %get-tuple-element.108), channel_id=1, source_target_pairs={{0,2},{2,0},{4,6},{6,4},{1,3},{3,1},{5,7},{7,5},{8,10},{10,8},{12,... | collective-permute-start | bytes 196616 | tf_op jit(solution)/shard_map/ppermute | solution.py:514
  73.1 7.3 %collective-permute-start.20 = (bf16[256,128]{1,0:T(8,128)(2,1)S(1)}, bf16[256,128]{1,0:T(8,128)(2,1)S(1)}, u32[]{:S(2)}, u32[]{:S(2)}) collective-permute-start(bf16[256,128]{1,0:T(8,128)(2,1)S(1)} %get-tuple-element.109), channel_id=1, source_target_pairs={{0,4},{2,6},{4,0},{6,2},{1,5},{3,7},{5,1},{7,3},{8,12},{10,14},{12... | collective-permute-start | bytes 196616 | tf_op jit(solution)/shard_map/ppermute | solution.py:514
  75.1 5.3 %collective-permute-start.21 = (bf16[256,128]{1,0:T(8,128)(2,1)S(1)}, bf16[256,128]{1,0:T(8,128)(2,1)S(1)}, u32[]{:S(2)}, u32[]{:S(2)}) collective-permute-start(bf16[256,128]{1,0:T(8,128)(2,1)S(1)} %get-tuple-element.110), channel_id=1, source_target_pairs={{0,6},{2,4},{4,2},{6,0},{1,7},{3,5},{5,3},{7,1},{8,14},{10,12},{12... | collective-permute-start | bytes 196616 | tf_op jit(solution)/shard_map/ppermute | solution.py:514
  81.4 2.4 %collective-permute-start.22 = (bf16[256,1536]{1,0:T(8,128)(2,1)S(1)}, bf16[256,1536]{1,0:T(8,128)(2,1)S(1)}, u32[]{:S(2)}, u32[]{:S(2)}) collective-permute-start(bf16[256,1536]{1,0:T(8,128)(2,1)S(1)} %project.3), channel_id=1, source_target_pairs={{0,1},{1,0},{2,3},{3,2},{4,5},{5,4},{6,7},{7,6},{8,9},{9,8},{10,11... | collective-permute-start | bytes 2359304 | tf_op jit(solution)/shard_map/ppermute | solution.py:570

commit v4 on v3

--- a/solution.py
+++ b/solution.py
@@ -553,8 +553,8 @@
         around.append(neighbours(after(own[-1], *around[-1])))
     arrived = []
     for n, pieces in enumerate(qr):
-        gates = come[-1][1:] if n == 0 else arrived[-1][1:]
-        arrived.append(swap([after(x, *gates) for x in pieces]))
+        gates = come[-1] if n == 0 else arrived[-1]
+        arrived.append(swap([after(x, gates[max(k, 1)]) for k, x in enumerate(pieces)]))
     q_features = query_features(tile_rows, tile_cols, me, arrived[0])
     heads = [
         swap(

time: 85.1 us -> 84 us (0.987)
  waiting for transfers between devices: 20.3 us -> 18.8 us
    ppermute x18, waiting for transfers between devices: 12.5 us -> 11.3 us  [swap(): lax.ppermute(x, 'wa', [(i, i ^ k) for i in range(tiles)])]
  transfers between devices with their start and end apart: 23 -> 23, of which waited for: 6 -> 5; matrix products, arithmetic and copies ran while one was open for 2% -> 2% of each run, Pallas kernels for 29% -> 30%
where the time goes in v4:
time: 84 us; the launch traced here: 83.7 us
  starting transfers between devices  32.1 us (38%)
  Pallas kernels  26.2 us (31%)
  waiting for transfers between devices  18.8 us (22%)
  local copies, waits for them, and re-layouts  5.19 us (6%)
  other arithmetic  1.16 us (1%)
    ppermute x18, starting transfers between devices, swap(): lax.ppermute(x, 'wa', [(i, i ^ k) for i in range(tiles)])  22.6 us
    pallas_call x2, Pallas kernels, attend(): pl.pallas_call(functools.partial(attend_kernel, per_owner, tiles, count),...  13 us
    ppermute x18, waiting for transfers between devices, swap(): lax.ppermute(x, 'wa', [(i, i ^ k) for i in range(tiles)])  11.3 us
    ppermute x4, starting transfers between devices, neighbours(): return [lax.ppermute(x, 'ha', pairs) for pairs in both_ways]  9.47 us
    ppermute x4, waiting for transfers between devices, neighbours(): return [lax.ppermute(x, 'ha', pairs) for pairs in both_ways]  6.15 us
    pallas_call x1, Pallas kernels, project_early(): pl.pallas_call(functools.partial(project_early_kernel, tiles, share, chun...  4.17 us
    unnamed x15, local copies, waits for them, and re-layouts  3.34 us
    pallas_call x2, Pallas kernels, pack_qr(): pl.pallas_call(functools.partial(pack_qr_kernel, tiles, share, chunks), o...  2.27 us
  transfers between devices with their start and end apart: 23, of which 5 were waited for; matrix products, arithmetic and copies ran while one was open for 2% of the time, Pallas kernels for 30%

profile of v4, /device:TPU:0, one launch (start us, length us, event | category | flops | bytes accessed | tf_op | source)
XLA Modules:
  0.0 83.7 jit_solution(6650765278711807123)
XLA Ops:
  0.0 1.7 %copy.7 = bf16[16,16,2,1536]{3,1,0,2:T(8,128)(2,1)S(1)} copy(bf16[16,16,2,1536]{3,2,1,0:T(2,128)(2,1)} %param.7) | data formatting | bytes 3145728 | tf_op args[1]
  1.7 0.3 pack_kv.2
  2.0 3.0 %collective-permute-start = (bf16[4,256,128]{2,1,0:T(8,128)(2,1)S(1)}, bf16[4,256,128]{2,1,0:T(8,128)(2,1)S(1)}, u32[]{:S(2)}, u32[]{:S(2)}) collective-permute-start(bf16[4,256,128]{2,1,0:T(8,128)(2,1)S(1)} %get-tuple-element.59), channel_id=1, source_target_pairs={{0,2},{2,0},{4,6},{6,4},{1,3},{3,1},{5,7},{7,5},{8,10},{10,8},{12,... | collective-permute-start | bytes 786440 | tf_op jit(solution)/shard_map/ppermute | solution.py:514
  5.0 1.5 %collective-permute-start.1 = (bf16[4,256,128]{2,1,0:T(8,128)(2,1)S(1)}, bf16[4,256,128]{2,1,0:T(8,128)(2,1)S(1)}, u32[]{:S(2)}, u32[]{:S(2)}) collective-permute-start(bf16[4,256,128]{2,1,0:T(8,128)(2,1)S(1)} %get-tuple-element.60), channel_id=1, source_target_pairs={{0,4},{2,6},{4,0},{6,2},{1,5},{3,7},{5,1},{7,3},{8,12},{10,14},{12... | collective-permute-start | bytes 786440 | tf_op jit(solution)/shard_map/ppermute | solution.py:514
  6.5 0.0 collective-permute-start.2
  6.5 0.9 %pack_kv.3 = (bf16[2,256,128]{2,1,0:T(8,128)(2,1)S(1)}, bf16[2,256,128]{2,1,0:T(8,128)(2,1)}, bf16[2,256,128]{2,1,0:T(8,128)(2,1)}, bf16[2,256,128]{2,1,0:T(8,128)(2,1)}) custom-call(s32[1]{0:T(128)} %bitcast.1.me_ref, bf16[2,256,1536]{2,1,0:T(8,128)(2,1)S(1)} %bitcast.21), custom_call_target="tpu_custom_call" | custom-call | tf_op jit(solution)/shard_map/pack_kv/pallas_call | solution.py:338
  7.4 4.7 %collective-permute-done.refs_1_ = bf16[4,256,128]{2,1,0:T(8,128)(2,1)S(1)} collective-permute-done((bf16[4,256,128]{2,1,0:T(8,128)(2,1)S(1)}, bf16[4,256,128]{2,1,0:T(8,128)(2,1)S(1)}, u32[]{:S(2)}, u32[]{:S(2)}) %collective-permute-start) | collective-permute-done | bytes 262176 | tf_op jit(solution)/shard_map/ppermute | solution.py:514
  12.1 6.2 %collective-permute-done.1.refs_2_ = bf16[4,256,128]{2,1,0:T(8,128)(2,1)S(1)} collective-permute-done((bf16[4,256,128]{2,1,0:T(8,128)(2,1)S(1)}, bf16[4,256,128]{2,1,0:T(8,128)(2,1)S(1)}, u32[]{:S(2)}, u32[]{:S(2)}) %collective-permute-start.1) | collective-permute-done | bytes 262176 | tf_op jit(solution)/shard_map/ppermute | solution.py:514
  18.4 0.0 collective-permute-done.2.refs_3_
  18.4 0.1 order.2.refs_5_
  18.5 1.6 %collective-permute-start.10 = (bf16[4,4,256,128]{3,2,1,0:T(8,128)(2,1)S(1)}, bf16[4,4,256,128]{3,2,1,0:T(8,128)(2,1)}, u32[]{:S(2)}, u32[]{:S(2)}) collective-permute-start(bf16[4,4,256,128]{3,2,1,0:T(8,128)(2,1)S(1)} %order.2.refs_5_), channel_id=1, source_target_pairs={{16,8},{8,16},{17,9},{9,17},{18,10},{10,18},{19,11},{11,19},{20,12... | collective-permute-start | bytes 3145736 | tf_op jit(solution)/shard_map/ppermute | solution.py:523
  20.1 3.5 %collective-permute-start.9 = (bf16[4,4,256,128]{3,2,1,0:T(8,128)(2,1)S(1)}, bf16[4,4,256,128]{3,2,1,0:T(8,128)(2,1)}, u32[]{:S(2)}, u32[]{:S(2)}) collective-permute-start(bf16[4,4,256,128]{3,2,1,0:T(8,128)(2,1)S(1)} %order.2.refs_5_), channel_id=1, source_target_pairs={{8,0},{24,16},{0,8},{16,24},{9,1},{25,17},{1,9},{17,25},{10,2},{26... | collective-permute-start | bytes 3145736 | tf_op jit(solution)/shard_map/ppermute | solution.py:523
  23.6 1.5 %collective-permute-start.5 = (bf16[2,256,128]{2,1,0:T(8,128)(2,1)}, bf16[2,256,128]{2,1,0:T(8,128)(2,1)}, u32[]{:S(2)}, u32[]{:S(2)}) collective-permute-start(bf16[2,256,128]{2,1,0:T(8,128)(2,1)} %get-tuple-element.73), channel_id=1, source_target_pairs={{0,4},{2,6},{4,0},{6,2},{1,5},{3,7},{5,1},{7,3},{8,12},{10,14},{12... | collective-permute-start | bytes 393224 | tf_op jit(solution)/shard_map/ppermute | solution.py:514
  25.1 1.2 %collective-permute-start.7 = (bf16[2,256,128]{2,1,0:T(8,128)(2,1)}, bf16[2,256,128]{2,1,0:T(8,128)(2,1)}, u32[]{:S(2)}, u32[]{:S(2)}) collective-permute-start(bf16[2,256,128]{2,1,0:T(8,128)(2,1)} %get-tuple-element.77), channel_id=1, source_target_pairs={{0,6},{2,4},{4,2},{6,0},{1,7},{3,5},{5,3},{7,1},{8,14},{10,12},{12... | collective-permute-start | bytes 393224 | tf_op jit(solution)/shard_map/ppermute | solution.py:514
  26.3 0.8 collective-permute-start.3
  27.1 0.1 reshape.30
  27.2 1.7 %copy.8 = bf16[2,128,2,1536]{3,1,0,2:T(8,128)(2,1)S(1)} copy(bf16[2,128,2,1536]{3,2,1,0:T(2,128)(2,1)} %param.8) | data formatting | bytes 3145728 | tf_op jit(solution)/shard_map/optimization_barrier | solution.py:542
  28.9 0.0 copy-start.6
  28.9 1.7 %pack_qr.2 = (bf16[1552,128]{1,0:T(8,128)(2,1)S(1)}, bf16[1552,128]{1,0:T(8,128)(2,1)}, bf16[1552,128]{1,0:T(8,128)(2,1)}, bf16[1552,128]{1,0:T(8,128)(2,1)}) custom-call(s32[1]{0:T(128)} %bitcast.1.me_ref, bf16[256,1536]{1,0:T(8,128)(2,1)S(1)} %bitcast.24, bf16[2,256,1536]{2,1,0:T(8,128)(2,1)S(1)} %bitcast.22, bf16[16,128]{1,0:T(8,128)(2,1)S(1)} %pad.5.f_ref), custom_call_target="tpu_custom_call" | custom-call | tf_op jit(solution)/shard_map/pack_qr/pallas_call | solution.py:395
  30.7 0.8 copy-done.3
  31.5 0.0 collective-permute-done.5.refs_2_
  31.5 0.0 collective-permute-done.7.refs_3_
  31.5 0.3 collective-permute-done.3.refs_1_
  31.8 1.2 %collective-permute-start.4 = (bf16[1552,128]{1,0:T(8,128)(2,1)}, bf16[1552,128]{1,0:T(8,128)(2,1)}, u32[]{:S(2)}, u32[]{:S(2)}) collective-permute-start(bf16[1552,128]{1,0:T(8,128)(2,1)} %get-tuple-element.70), channel_id=1, source_target_pairs={{0,2},{2,0},{4,6},{6,4},{1,3},{3,1},{5,7},{7,5},{8,10},{10,8},{12,... | collective-permute-start | bytes 1191944 | tf_op jit(solution)/shard_map/ppermute | solution.py:514
  33.0 2.7 %collective-permute-start.8 = (bf16[1552,128]{1,0:T(8,128)(2,1)}, bf16[1552,128]{1,0:T(8,128)(2,1)}, u32[]{:S(2)}, u32[]{:S(2)}) collective-permute-start(bf16[1552,128]{1,0:T(8,128)(2,1)} %get-tuple-element.78), channel_id=1, source_target_pairs={{0,6},{2,4},{4,2},{6,0},{1,7},{3,5},{5,3},{7,1},{8,14},{10,12},{12... | collective-permute-start | bytes 1191944 | tf_op jit(solution)/shard_map/ppermute | solution.py:514
  35.7 0.1 add_bitcast_fusion
  35.8 0.7 key_features.1.refs_8_
  36.5 0.0 copy-start.1
  36.5 0.9 %copy-done.1 = bf16[4,3,256,128]{3,2,1,0:T(8,128)(2,1)} copy-done((bf16[4,3,256,128]{3,2,1,0:T(8,128)(2,1)}, bf16[4,3,256,128]{3,2,1,0:T(8,128)(2,1)S(1)}, u32[]{:S(2)}) %copy-start.1) | copy-done | bytes 786456
  37.4 2.0 %order.3.refs_5_ = bf16[4,2,256,128]{3,2,1,0:T(8,128)(2,1)} custom-call(s32[1]{0:T(128)} %bitcast.1.me_ref, bf16[2,256,128]{2,1,0:T(8,128)(2,1)S(1)} %get-tuple-element.102.refs_0_, bf16[2,256,128]{2,1,0:T(8,128)(2,1)} %collective-permute-done.3.refs_1_, bf16[2,256,128]{2,1,0:T(8,128)(2,1)} %collective-permute-done.5.refs_2_, ...), custom_call_target="tpu_custom_call" | custom-call | tf_op jit(solution)/shard_map/order/pallas_call | solution.py:356
  39.4 0.0 collective-permute-done.10.refs_7_
  39.4 6.1 %collective-permute-done.9.refs_6_ = bf16[4,4,256,128]{3,2,1,0:T(8,128)(2,1)} collective-permute-done((bf16[4,4,256,128]{3,2,1,0:T(8,128)(2,1)S(1)}, bf16[4,4,256,128]{3,2,1,0:T(8,128)(2,1)}, u32[]{:S(2)}, u32[]{:S(2)}) %collective-permute-start.9) | collective-permute-done | bytes 1048608 | tf_op jit(solution)/shard_map/ppermute | solution.py:523
  45.5 1.5 %collective-permute-start.18 = (bf16[4,2,256,128]{3,2,1,0:T(8,128)(2,1)}, bf16[4,2,256,128]{3,2,1,0:T(8,128)(2,1)}, u32[]{:S(2)}, u32[]{:S(2)}) collective-permute-start(bf16[4,2,256,128]{3,2,1,0:T(8,128)(2,1)} %order.3.refs_5_), channel_id=1, source_target_pairs={{16,8},{8,16},{17,9},{9,17},{18,10},{10,18},{19,11},{11,19},{20,12... | collective-permute-start | bytes 1572872 | tf_op jit(solution)/shard_map/ppermute | solution.py:523
  47.0 2.9 %collective-permute-start.17 = (bf16[4,2,256,128]{3,2,1,0:T(8,128)(2,1)}, bf16[4,2,256,128]{3,2,1,0:T(8,128)(2,1)}, u32[]{:S(2)}, u32[]{:S(2)}) collective-permute-start(bf16[4,2,256,128]{3,2,1,0:T(8,128)(2,1)} %order.3.refs_5_), channel_id=1, source_target_pairs={{8,0},{24,16},{0,8},{16,24},{9,1},{25,17},{1,9},{17,25},{10,2},{26... | collective-permute-start | bytes 1572872 | tf_op jit(solution)/shard_map/ppermute | solution.py:523
  49.9 0.1 copy.9.ids_ref
  50.0 0.5 pack_qr.3
  50.5 0.0 collective-permute-done.4.refs_1_
  50.5 1.5 %collective-permute-start.14 = (bf16[768,128]{1,0:T(8,128)(2,1)S(1)}, bf16[768,128]{1,0:T(8,128)(2,1)S(1)}, u32[]{:S(2)}, u32[]{:S(2)}) collective-permute-start(bf16[768,128]{1,0:T(8,128)(2,1)S(1)} %get-tuple-element.96), channel_id=1, source_target_pairs={{0,2},{2,0},{4,6},{6,4},{1,3},{3,1},{5,7},{7,5},{8,10},{10,8},{12,... | collective-permute-start | bytes 589832 | tf_op jit(solution)/shard_map/ppermute | solution.py:514
  52.0 0.0 collective-permute-done.8.refs_3_
  52.0 0.5 collective-permute-start.16
  52.5 1.5 %collective-permute-start.15 = (bf16[768,128]{1,0:T(8,128)(2,1)S(1)}, bf16[768,128]{1,0:T(8,128)(2,1)S(1)}, u32[]{:S(2)}, u32[]{:S(2)}) collective-permute-start(bf16[768,128]{1,0:T(8,128)(2,1)S(1)} %get-tuple-element.98), channel_id=1, source_target_pairs={{0,4},{2,6},{4,0},{6,2},{1,5},{3,7},{5,1},{7,3},{8,12},{10,14},{12... | collective-permute-start | bytes 589832 | tf_op jit(solution)/shard_map/ppermute | solution.py:514
  54.1 0.9 %query_features.1.refs_4_ = bf16[4,256,128]{2,1,0:T(8,128)(2,1)S(1)} custom-call(s32[1]{0:T(128)} %bitcast.1.me_ref, bf16[1552,128]{1,0:T(8,128)(2,1)S(1)} %copy-done.4, bf16[1552,128]{1,0:T(8,128)(2,1)} %collective-permute-done.4.refs_1_, bf16[1552,128]{1,0:T(8,128)(2,1)} %collective-permute-done.6.refs_2_, bf16[1552,128]{1,0:T(8,128)(2,1)} %collective-permute-done.8.refs_3_), custom_call_target="tpu_custom_call" | custom-call | tf_op jit(solution)/shard_map/query_features/pallas_call | solution.py:283
  55.0 8.2 %attend.2 = (bf16[512,128]{1,0:T(8,128)(2,1)S(1)}, bf16[512,128]{1,0:T(8,128)(2,1)S(1)}, bf16[512,128]{1,0:T(8,128)(2,1)S(1)}, bf16[512,128]{1,0:T(8,128)(2,1)S(1)}) custom-call(s32[1]{0:T(128)} %bitcast.1.me_ref, s32[4,2]{1,0:T(4,128)S(1)} %copy.9.ids_ref, bf16[1552,128]{1,0:T(8,128)(2,1)S(1)} %copy-done.4, ...), custom_call_target="tpu_custom_call" | custom-call | flops 2952790016 | bytes 3145728 | tf_op jit(solution)/shard_map/attend/pallas_call | solution.py:235
  63.2 1.5 %collective-permute-start.11 = (bf16[512,128]{1,0:T(8,128)(2,1)S(1)}, bf16[512,128]{1,0:T(8,128)(2,1)S(1)}, u32[]{:S(2)}, u32[]{:S(2)}) collective-permute-start(bf16[512,128]{1,0:T(8,128)(2,1)S(1)} %get-tuple-element.85), channel_id=1, source_target_pairs={{0,2},{2,0},{4,6},{6,4},{1,3},{3,1},{5,7},{7,5},{8,10},{10,8},{12,... | collective-permute-start | bytes 393224 | tf_op jit(solution)/shard_map/ppermute | solution.py:514
  64.7 0.0 collective-permute-done.16.refs_3_
  64.8 0.6 collective-permute-start.12
  65.3 0.0 collective-permute-done.15.refs_2_
  65.3 1.5 %collective-permute-start.13 = (bf16[512,128]{1,0:T(8,128)(2,1)S(1)}, bf16[512,128]{1,0:T(8,128)(2,1)S(1)}, u32[]{:S(2)}, u32[]{:S(2)}) collective-permute-start(bf16[512,128]{1,0:T(8,128)(2,1)S(1)} %get-tuple-element.87), channel_id=1, source_target_pairs={{0,6},{2,4},{4,2},{6,0},{1,7},{3,5},{5,3},{7,1},{8,14},{10,12},{12... | collective-permute-start | bytes 393224 | tf_op jit(solution)/shard_map/ppermute | solution.py:514
  66.8 0.0 collective-permute-done.18.refs_7_
  66.8 0.0 collective-permute-done.17.refs_6_
  66.8 4.8 %attend.3 = (bf16[256,128]{1,0:T(8,128)(2,1)S(1)}, bf16[256,128]{1,0:T(8,128)(2,1)S(1)}, bf16[256,128]{1,0:T(8,128)(2,1)S(1)}, bf16[256,128]{1,0:T(8,128)(2,1)S(1)}) custom-call(s32[1]{0:T(128)} %bitcast.1.me_ref, s32[4,2]{1,0:T(4,128)S(1)} %copy.9.ids_ref, bf16[768,128]{1,0:T(8,128)(2,1)S(1)} %get-tuple-element.94.refs_0_, ...), custom_call_target="tpu_custom_call" | custom-call | flops 1476395008 | bytes 1572864 | tf_op jit(solution)/shard_map/attend/pallas_call | solution.py:235
  71.6 1.5 %collective-permute-start.19 = (bf16[256,128]{1,0:T(8,128)(2,1)S(1)}, bf16[256,128]{1,0:T(8,128)(2,1)S(1)}, u32[]{:S(2)}, u32[]{:S(2)}) collective-permute-start(bf16[256,128]{1,0:T(8,128)(2,1)S(1)} %get-tuple-element.108), channel_id=1, source_target_pairs={{0,2},{2,0},{4,6},{6,4},{1,3},{3,1},{5,7},{7,5},{8,10},{10,8},{12,... | collective-permute-start | bytes 196616 | tf_op jit(solution)/shard_map/ppermute | solution.py:514
  73.1 0.5 collective-permute-start.20
  73.7 0.0 collective-permute-done.11.refs_1_
  73.7 1.5 %collective-permute-start.21 = (bf16[256,128]{1,0:T(8,128)(2,1)S(1)}, bf16[256,128]{1,0:T(8,128)(2,1)S(1)}, u32[]{:S(2)}, u32[]{:S(2)}) collective-permute-start(bf16[256,128]{1,0:T(8,128)(2,1)S(1)} %get-tuple-element.110), channel_id=1, source_target_pairs={{0,6},{2,4},{4,2},{6,0},{1,7},{3,5},{5,3},{7,1},{8,14},{10,12},{12... | collective-permute-start | bytes 196616 | tf_op jit(solution)/shard_map/ppermute | solution.py:514
  75.1 0.0 collective-permute-done.12.refs_2_
  75.2 4.2 %project_early.1 = (f32[2,256,1536]{2,1,0:T(8,128)S(1)}, bf16[4,128,3072]{2,1,0:T(8,128)(2,1)S(1)}) custom-call(s32[1]{0:T(128)} %bitcast.1.me_ref, bf16[1536,3072]{1,0:T(8,128)(2,1)} %w_hbm.1, bf16[512,128]{1,0:T(8,128)(2,1)S(1)} %get-tuple-element.84.refs_0_, bf16[512,128]{1,0:T(8,128)(2,1)S(1)} %collective-permute-done.11.refs_1_, ...), custom_call_target="tpu_custom_call" | custom-call | tf_op jit(solution)/shard_map/project_early/pallas_call | solution.py:451
  79.3 0.0 collective-permute-done.19.refs_1_
  79.3 0.0 collective-permute-done.20.refs_2_
  79.4 1.0 %project.3 = bf16[256,1536]{1,0:T(8,128)(2,1)S(1)} custom-call(s32[1]{0:T(128)} %bitcast.16.which_ref, bf16[4,128,3072]{2,1,0:T(8,128)(2,1)S(1)} %get-tuple-element.88.w_ref, f32[2,256,1536]{2,1,0:T(8,128)S(1)} %get-tuple-element.89.early_ref, bf16[256,128]{1,0:T(8,128)(2,1)S(1)} %get-tuple-element.107.refs_0_, ...), custom_call_target="tpu_custom_call" | custom-call | tf_op jit(solution)/shard_map/project/pallas_call | solution.py:484
  80.3 0.1 collective-permute-start.22
  80.4 1.0 %project.2 = bf16[256,1536]{1,0:T(8,128)(2,1)S(1)} custom-call(s32[1]{0:T(128)} %bitcast.which_ref, bf16[4,128,3072]{2,1,0:T(8,128)(2,1)S(1)} %get-tuple-element.88.w_ref, f32[2,256,1536]{2,1,0:T(8,128)S(1)} %get-tuple-element.89.early_ref, bf16[256,128]{1,0:T(8,128)(2,1)S(1)} %get-tuple-element.107.refs_0_, ...), custom_call_target="tpu_custom_call" | custom-call | tf_op jit(solution)/shard_map/project/pallas_call | solution.py:484
  81.4 1.3 %collective-permute-done.22 = bf16[256,1536]{1,0:T(8,128)(2,1)S(1)} collective-permute-done((bf16[256,1536]{1,0:T(8,128)(2,1)S(1)}, bf16[256,1536]{1,0:T(8,128)(2,1)S(1)}, u32[]{:S(2)}, u32[]{:S(2)}) %collective-permute-start.22) | collective-permute-done | bytes 786464 | tf_op jit(solution)/shard_map/ppermute | solution.py:570
  82.7 1.1 %add_convert_fusion = bf16[256,1536]{1,0:T(8,128)(2,1)} fusion(bf16[256,1536]{1,0:T(8,128)(2,1)S(1)} %collective-permute-done.22, bf16[256,1536]{1,0:T(8,128)(2,1)S(1)} %project.2), kind=kLoop, calls=%fused_computation | loop fusion | flops 1572864 | bytes 2359296 | tf_op jit(solution)/shard_map/convert_element_type | solution.py:573
  (18 shorter events, 0.1 us)
Async XLA Ops:
  2.0 10.1 %collective-permute-start = (bf16[4,256,128]{2,1,0:T(8,128)(2,1)S(1)}, bf16[4,256,128]{2,1,0:T(8,128)(2,1)S(1)}, u32[]{:S(2)}, u32[]{:S(2)}) collective-permute-start(bf16[4,256,128]{2,1,0:T(8,128)(2,1)S(1)} %get-tuple-element.59), channel_id=1, source_target_pairs={{0,2},{2,0},{4,6},{6,4},{1,3},{3,1},{5,7},{7,5},{8,10},{10,8},{12,... | collective-permute-start | bytes 786440 | tf_op jit(solution)/shard_map/ppermute | solution.py:514
  5.0 13.4 %collective-permute-start.1 = (bf16[4,256,128]{2,1,0:T(8,128)(2,1)S(1)}, bf16[4,256,128]{2,1,0:T(8,128)(2,1)S(1)}, u32[]{:S(2)}, u32[]{:S(2)}) collective-permute-start(bf16[4,256,128]{2,1,0:T(8,128)(2,1)S(1)} %get-tuple-element.60), channel_id=1, source_target_pairs={{0,4},{2,6},{4,0},{6,2},{1,5},{3,7},{5,1},{7,3},{8,12},{10,14},{12... | collective-permute-start | bytes 786440 | tf_op jit(solution)/shard_map/ppermute | solution.py:514
  6.5 11.9 %collective-permute-start.2 = (bf16[4,256,128]{2,1,0:T(8,128)(2,1)S(1)}, bf16[4,256,128]{2,1,0:T(8,128)(2,1)S(1)}, u32[]{:S(2)}, u32[]{:S(2)}) collective-permute-start(bf16[4,256,128]{2,1,0:T(8,128)(2,1)S(1)} %get-tuple-element.61), channel_id=1, source_target_pairs={{0,6},{2,4},{4,2},{6,0},{1,7},{3,5},{5,3},{7,1},{8,14},{10,12},{12... | collective-permute-start | bytes 786440 | tf_op jit(solution)/shard_map/ppermute | solution.py:514
  6.5 20.6 %copy-start.5 = (s32[16,16]{1,0:T(8,128)S(1)}, s32[16,16]{1,0:T(8,128)}, u32[]{:S(2)}) copy-start(s32[16,16]{1,0:T(8,128)} %param.10) | copy-start | bytes 3076
  18.5 20.9 %collective-permute-start.10 = (bf16[4,4,256,128]{3,2,1,0:T(8,128)(2,1)S(1)}, bf16[4,4,256,128]{3,2,1,0:T(8,128)(2,1)}, u32[]{:S(2)}, u32[]{:S(2)}) collective-permute-start(bf16[4,4,256,128]{3,2,1,0:T(8,128)(2,1)S(1)} %order.2.refs_5_), channel_id=1, source_target_pairs={{16,8},{8,16},{17,9},{9,17},{18,10},{10,18},{19,11},{11,19},{20,12... | collective-permute-start | bytes 3145736 | tf_op jit(solution)/shard_map/ppermute | solution.py:523
  20.1 25.4 %collective-permute-start.9 = (bf16[4,4,256,128]{3,2,1,0:T(8,128)(2,1)S(1)}, bf16[4,4,256,128]{3,2,1,0:T(8,128)(2,1)}, u32[]{:S(2)}, u32[]{:S(2)}) collective-permute-start(bf16[4,4,256,128]{3,2,1,0:T(8,128)(2,1)S(1)} %order.2.refs_5_), channel_id=1, source_target_pairs={{8,0},{24,16},{0,8},{16,24},{9,1},{25,17},{1,9},{17,25},{10,2},{26... | collective-permute-start | bytes 3145736 | tf_op jit(solution)/shard_map/ppermute | solution.py:523
  23.6 7.8 %collective-permute-start.5 = (bf16[2,256,128]{2,1,0:T(8,128)(2,1)}, bf16[2,256,128]{2,1,0:T(8,128)(2,1)}, u32[]{:S(2)}, u32[]{:S(2)}) collective-permute-start(bf16[2,256,128]{2,1,0:T(8,128)(2,1)} %get-tuple-element.73), channel_id=1, source_target_pairs={{0,4},{2,6},{4,0},{6,2},{1,5},{3,7},{5,1},{7,3},{8,12},{10,14},{12... | collective-permute-start | bytes 393224 | tf_op jit(solution)/shard_map/ppermute | solution.py:514
  25.1 6.3 %collective-permute-start.7 = (bf16[2,256,128]{2,1,0:T(8,128)(2,1)}, bf16[2,256,128]{2,1,0:T(8,128)(2,1)}, u32[]{:S(2)}, u32[]{:S(2)}) collective-permute-start(bf16[2,256,128]{2,1,0:T(8,128)(2,1)} %get-tuple-element.77), channel_id=1, source_target_pairs={{0,6},{2,4},{4,2},{6,0},{1,7},{3,5},{5,3},{7,1},{8,14},{10,12},{12... | collective-permute-start | bytes 393224 | tf_op jit(solution)/shard_map/ppermute | solution.py:514
  26.3 5.5 %collective-permute-start.3 = (bf16[2,256,128]{2,1,0:T(8,128)(2,1)}, bf16[2,256,128]{2,1,0:T(8,128)(2,1)}, u32[]{:S(2)}, u32[]{:S(2)}) collective-permute-start(bf16[2,256,128]{2,1,0:T(8,128)(2,1)} %get-tuple-element.67), channel_id=1, source_target_pairs={{0,2},{2,0},{4,6},{6,4},{1,3},{3,1},{5,7},{7,5},{8,10},{10,8},{12,... | collective-permute-start | bytes 393224 | tf_op jit(solution)/shard_map/ppermute | solution.py:514
  27.2 1.7 %copy-start = (bf16[16,16,1536]{2,1,0:T(8,128)(2,1)S(1)}, bf16[16,16,1536]{2,1,0:T(8,128)(2,1)}, u32[]{:S(2)}) copy-start(bf16[16,16,1536]{2,1,0:T(8,128)(2,1)} %param.6) | copy-start | bytes 2359300
  28.9 21.0 %copy-start.6 = (s32[1,4,2]{1,2,0:T(2,128)S(1)}, s32[1,4,2]{1,2,0:T(2,128)}, u32[]{:S(2)}) copy-start(s32[1,4,2]{1,2,0:T(2,128)} %param.9) | copy-start | bytes 100
  30.7 0.8 copy-start.3
  31.8 18.7 %collective-permute-start.4 = (bf16[1552,128]{1,0:T(8,128)(2,1)}, bf16[1552,128]{1,0:T(8,128)(2,1)}, u32[]{:S(2)}, u32[]{:S(2)}) collective-permute-start(bf16[1552,128]{1,0:T(8,128)(2,1)} %get-tuple-element.70), channel_id=1, source_target_pairs={{0,2},{2,0},{4,6},{6,4},{1,3},{3,1},{5,7},{7,5},{8,10},{10,8},{12,... | collective-permute-start | bytes 1191944 | tf_op jit(solution)/shard_map/ppermute | solution.py:514
  33.0 19.0 %collective-permute-start.8 = (bf16[1552,128]{1,0:T(8,128)(2,1)}, bf16[1552,128]{1,0:T(8,128)(2,1)}, u32[]{:S(2)}, u32[]{:S(2)}) collective-permute-start(bf16[1552,128]{1,0:T(8,128)(2,1)} %get-tuple-element.78), channel_id=1, source_target_pairs={{0,6},{2,4},{4,2},{6,0},{1,7},{3,5},{5,3},{7,1},{8,14},{10,12},{12... | collective-permute-start | bytes 1191944 | tf_op jit(solution)/shard_map/ppermute | solution.py:514
  35.7 16.9 %collective-permute-start.6 = (bf16[1552,128]{1,0:T(8,128)(2,1)}, bf16[1552,128]{1,0:T(8,128)(2,1)}, u32[]{:S(2)}, u32[]{:S(2)}) collective-permute-start(bf16[1552,128]{1,0:T(8,128)(2,1)} %get-tuple-element.74), channel_id=1, source_target_pairs={{0,4},{2,6},{4,0},{6,2},{1,5},{3,7},{5,1},{7,3},{8,12},{10,14},{12... | collective-permute-start | bytes 1191944 | tf_op jit(solution)/shard_map/ppermute | solution.py:514
  36.5 0.9 %copy-start.1 = (bf16[4,3,256,128]{3,2,1,0:T(8,128)(2,1)}, bf16[4,3,256,128]{3,2,1,0:T(8,128)(2,1)S(1)}, u32[]{:S(2)}) copy-start(bf16[4,3,256,128]{3,2,1,0:T(8,128)(2,1)S(1)} %key_features.1.refs_8_) | copy-start | bytes 2359300
  45.5 21.3 %collective-permute-start.18 = (bf16[4,2,256,128]{3,2,1,0:T(8,128)(2,1)}, bf16[4,2,256,128]{3,2,1,0:T(8,128)(2,1)}, u32[]{:S(2)}, u32[]{:S(2)}) collective-permute-start(bf16[4,2,256,128]{3,2,1,0:T(8,128)(2,1)} %order.3.refs_5_), channel_id=1, source_target_pairs={{16,8},{8,16},{17,9},{9,17},{18,10},{10,18},{19,11},{11,19},{20,12... | collective-permute-start | bytes 1572872 | tf_op jit(solution)/shard_map/ppermute | solution.py:523
  47.0 19.8 %collective-permute-start.17 = (bf16[4,2,256,128]{3,2,1,0:T(8,128)(2,1)}, bf16[4,2,256,128]{3,2,1,0:T(8,128)(2,1)}, u32[]{:S(2)}, u32[]{:S(2)}) collective-permute-start(bf16[4,2,256,128]{3,2,1,0:T(8,128)(2,1)} %order.3.refs_5_), channel_id=1, source_target_pairs={{8,0},{24,16},{0,8},{16,24},{9,1},{25,17},{1,9},{17,25},{10,2},{26... | collective-permute-start | bytes 1572872 | tf_op jit(solution)/shard_map/ppermute | solution.py:523
  50.0 4.1 %copy-start.4 = (bf16[1552,128]{1,0:T(8,128)(2,1)S(1)}, bf16[1552,128]{1,0:T(8,128)(2,1)}, u32[]{:S(2)}) copy-start(bf16[1552,128]{1,0:T(8,128)(2,1)} %copy-done.3) | copy-start | bytes 1191940
  50.0 5.1 %copy-start.2 = (bf16[4,3,256,128]{3,2,1,0:T(8,128)(2,1)S(1)}, bf16[4,3,256,128]{3,2,1,0:T(8,128)(2,1)}, u32[]{:S(2)}) copy-start(bf16[4,3,256,128]{3,2,1,0:T(8,128)(2,1)} %copy-done.1) | copy-start | bytes 2359300
  50.5 12.7 %collective-permute-start.14 = (bf16[768,128]{1,0:T(8,128)(2,1)S(1)}, bf16[768,128]{1,0:T(8,128)(2,1)S(1)}, u32[]{:S(2)}, u32[]{:S(2)}) collective-permute-start(bf16[768,128]{1,0:T(8,128)(2,1)S(1)} %get-tuple-element.96), channel_id=1, source_target_pairs={{0,2},{2,0},{4,6},{6,4},{1,3},{3,1},{5,7},{7,5},{8,10},{10,8},{12,... | collective-permute-start | bytes 589832 | tf_op jit(solution)/shard_map/ppermute | solution.py:514
  52.0 12.7 %collective-permute-start.16 = (bf16[768,128]{1,0:T(8,128)(2,1)S(1)}, bf16[768,128]{1,0:T(8,128)(2,1)S(1)}, u32[]{:S(2)}, u32[]{:S(2)}) collective-permute-start(bf16[768,128]{1,0:T(8,128)(2,1)S(1)} %get-tuple-element.100), channel_id=1, source_target_pairs={{0,6},{2,4},{4,2},{6,0},{1,7},{3,5},{5,3},{7,1},{8,14},{10,12},{12... | collective-permute-start | bytes 589832 | tf_op jit(solution)/shard_map/ppermute | solution.py:514
  52.5 12.8 %collective-permute-start.15 = (bf16[768,128]{1,0:T(8,128)(2,1)S(1)}, bf16[768,128]{1,0:T(8,128)(2,1)S(1)}, u32[]{:S(2)}, u32[]{:S(2)}) collective-permute-start(bf16[768,128]{1,0:T(8,128)(2,1)S(1)} %get-tuple-element.98), channel_id=1, source_target_pairs={{0,4},{2,6},{4,0},{6,2},{1,5},{3,7},{5,1},{7,3},{8,12},{10,14},{12... | collective-permute-start | bytes 589832 | tf_op jit(solution)/shard_map/ppermute | solution.py:514
  63.2 10.4 %collective-permute-start.11 = (bf16[512,128]{1,0:T(8,128)(2,1)S(1)}, bf16[512,128]{1,0:T(8,128)(2,1)S(1)}, u32[]{:S(2)}, u32[]{:S(2)}) collective-permute-start(bf16[512,128]{1,0:T(8,128)(2,1)S(1)} %get-tuple-element.85), channel_id=1, source_target_pairs={{0,2},{2,0},{4,6},{6,4},{1,3},{3,1},{5,7},{7,5},{8,10},{10,8},{12,... | collective-permute-start | bytes 393224 | tf_op jit(solution)/shard_map/ppermute | solution.py:514
  64.8 10.4 %collective-permute-start.12 = (bf16[512,128]{1,0:T(8,128)(2,1)S(1)}, bf16[512,128]{1,0:T(8,128)(2,1)S(1)}, u32[]{:S(2)}, u32[]{:S(2)}) collective-permute-start(bf16[512,128]{1,0:T(8,128)(2,1)S(1)} %get-tuple-element.86), channel_id=1, source_target_pairs={{0,4},{2,6},{4,0},{6,2},{1,5},{3,7},{5,1},{7,3},{8,12},{10,14},{12... | collective-permute-start | bytes 393224 | tf_op jit(solution)/shard_map/ppermute | solution.py:514
  65.3 9.8 %collective-permute-start.13 = (bf16[512,128]{1,0:T(8,128)(2,1)S(1)}, bf16[512,128]{1,0:T(8,128)(2,1)S(1)}, u32[]{:S(2)}, u32[]{:S(2)}) collective-permute-start(bf16[512,128]{1,0:T(8,128)(2,1)S(1)} %get-tuple-element.87), channel_id=1, source_target_pairs={{0,6},{2,4},{4,2},{6,0},{1,7},{3,5},{5,3},{7,1},{8,14},{10,12},{12... | collective-permute-start | bytes 393224 | tf_op jit(solution)/shard_map/ppermute | solution.py:514
  71.6 7.7 %collective-permute-start.19 = (bf16[256,128]{1,0:T(8,128)(2,1)S(1)}, bf16[256,128]{1,0:T(8,128)(2,1)S(1)}, u32[]{:S(2)}, u32[]{:S(2)}) collective-permute-start(bf16[256,128]{1,0:T(8,128)(2,1)S(1)} %get-tuple-element.108), channel_id=1, source_target_pairs={{0,2},{2,0},{4,6},{6,4},{1,3},{3,1},{5,7},{7,5},{8,10},{10,8},{12,... | collective-permute-start | bytes 196616 | tf_op jit(solution)/shard_map/ppermute | solution.py:514
  73.1 6.2 %collective-permute-start.20 = (bf16[256,128]{1,0:T(8,128)(2,1)S(1)}, bf16[256,128]{1,0:T(8,128)(2,1)S(1)}, u32[]{:S(2)}, u32[]{:S(2)}) collective-permute-start(bf16[256,128]{1,0:T(8,128)(2,1)S(1)} %get-tuple-element.109), channel_id=1, source_target_pairs={{0,4},{2,6},{4,0},{6,2},{1,5},{3,7},{5,1},{7,3},{8,12},{10,14},{12... | collective-permute-start | bytes 196616 | tf_op jit(solution)/shard_map/ppermute | solution.py:514
  73.7 5.7 %collective-permute-start.21 = (bf16[256,128]{1,0:T(8,128)(2,1)S(1)}, bf16[256,128]{1,0:T(8,128)(2,1)S(1)}, u32[]{:S(2)}, u32[]{:S(2)}) collective-permute-start(bf16[256,128]{1,0:T(8,128)(2,1)S(1)} %get-tuple-element.110), channel_id=1, source_target_pairs={{0,6},{2,4},{4,2},{6,0},{1,7},{3,5},{5,3},{7,1},{8,14},{10,12},{12... | collective-permute-start | bytes 196616 | tf_op jit(solution)/shard_map/ppermute | solution.py:514
  80.3 2.4 %collective-permute-start.22 = (bf16[256,1536]{1,0:T(8,128)(2,1)S(1)}, bf16[256,1536]{1,0:T(8,128)(2,1)S(1)}, u32[]{:S(2)}, u32[]{:S(2)}) collective-permute-start(bf16[256,1536]{1,0:T(8,128)(2,1)S(1)} %project.3), channel_id=1, source_target_pairs={{0,1},{1,0},{2,3},{3,2},{4,5},{5,4},{6,7},{7,6},{8,9},{9,8},{10,11... | collective-permute-start | bytes 2359304 | tf_op jit(solution)/shard_map/ppermute | solution.py:570

commit v5 on v4

--- a/solution.py
+++ b/solution.py
@@ -554,7 +554,7 @@
     arrived = []
     for n, pieces in enumerate(qr):
         gates = come[-1] if n == 0 else arrived[-1]
-        arrived.append(swap([after(x, gates[max(k, 1)]) for k, x in enumerate(pieces)]))
+        arrived.append(swap([after(x, gates[max(k, 1)]) if k else x for k, x in enumerate(pieces)]))
     q_features = query_features(tile_rows, tile_cols, me, arrived[0])
     heads = [
         swap(

time: 84 us -> 84 us (level)
  no operation moved by 1% of the time
where the time goes in v5:
time: 84 us; the launch traced here: 83.7 us
  starting transfers between devices  32.1 us (38%)
  Pallas kernels  26.2 us (31%)
  waiting for transfers between devices  18.8 us (22%)
  local copies, waits for them, and re-layouts  5.19 us (6%)
  other arithmetic  1.16 us (1%)
    ppermute x18, starting transfers between devices, swap(): lax.ppermute(x, 'wa', [(i, i ^ k) for i in range(tiles)])  22.6 us
    pallas_call x2, Pallas kernels, attend(): pl.pallas_call(functools.partial(attend_kernel, per_owner, tiles, count),...  13 us
    ppermute x18, waiting for transfers between devices, swap(): lax.ppermute(x, 'wa', [(i, i ^ k) for i in range(tiles)])  11.3 us
    ppermute x4, starting transfers between devices, neighbours(): return [lax.ppermute(x, 'ha', pairs) for pairs in both_ways]  9.47 us
    ppermute x4, waiting for transfers between devices, neighbours(): return [lax.ppermute(x, 'ha', pairs) for pairs in both_ways]  6.15 us
    pallas_call x1, Pallas kernels, project_early(): pl.pallas_call(functools.partial(project_early_kernel, tiles, share, chun...  4.17 us
    unnamed x15, local copies, waits for them, and re-layouts  3.34 us
    pallas_call x2, Pallas kernels, pack_qr(): pl.pallas_call(functools.partial(pack_qr_kernel, tiles, share, chunks), o...  2.27 us
  transfers between devices with their start and end apart: 23, of which 5 were waited for; matrix products, arithmetic and copies ran while one was open for 2% of the time, Pallas kernels for 30%

profile of v5, /device:TPU:0, one launch (start us, length us, event | category | flops | bytes accessed | tf_op | source)
XLA Modules:
  0.0 83.7 jit_solution(155064116552692606)
XLA Ops:
  0.0 1.7 %copy.7 = bf16[16,16,2,1536]{3,1,0,2:T(8,128)(2,1)S(1)} copy(bf16[16,16,2,1536]{3,2,1,0:T(2,128)(2,1)} %param.7) | data formatting | bytes 3145728 | tf_op args[1]
  1.7 0.3 pack_kv.2
  2.0 3.0 %collective-permute-start = (bf16[4,256,128]{2,1,0:T(8,128)(2,1)S(1)}, bf16[4,256,128]{2,1,0:T(8,128)(2,1)S(1)}, u32[]{:S(2)}, u32[]{:S(2)}) collective-permute-start(bf16[4,256,128]{2,1,0:T(8,128)(2,1)S(1)} %get-tuple-element.57), channel_id=1, source_target_pairs={{0,2},{2,0},{4,6},{6,4},{1,3},{3,1},{5,7},{7,5},{8,10},{10,8},{12,... | collective-permute-start | bytes 786440 | tf_op jit(solution)/shard_map/ppermute | solution.py:514
  5.0 1.5 %collective-permute-start.1 = (bf16[4,256,128]{2,1,0:T(8,128)(2,1)S(1)}, bf16[4,256,128]{2,1,0:T(8,128)(2,1)S(1)}, u32[]{:S(2)}, u32[]{:S(2)}) collective-permute-start(bf16[4,256,128]{2,1,0:T(8,128)(2,1)S(1)} %get-tuple-element.58), channel_id=1, source_target_pairs={{0,4},{2,6},{4,0},{6,2},{1,5},{3,7},{5,1},{7,3},{8,12},{10,14},{12... | collective-permute-start | bytes 786440 | tf_op jit(solution)/shard_map/ppermute | solution.py:514
  6.5 0.0 collective-permute-start.2
  6.5 0.9 %pack_kv.3 = (bf16[2,256,128]{2,1,0:T(8,128)(2,1)S(1)}, bf16[2,256,128]{2,1,0:T(8,128)(2,1)}, bf16[2,256,128]{2,1,0:T(8,128)(2,1)}, bf16[2,256,128]{2,1,0:T(8,128)(2,1)}) custom-call(s32[1]{0:T(128)} %bitcast.1.me_ref, bf16[2,256,1536]{2,1,0:T(8,128)(2,1)S(1)} %bitcast.21), custom_call_target="tpu_custom_call" | custom-call | tf_op jit(solution)/shard_map/pack_kv/pallas_call | solution.py:338
  7.4 4.7 %collective-permute-done.refs_1_ = bf16[4,256,128]{2,1,0:T(8,128)(2,1)S(1)} collective-permute-done((bf16[4,256,128]{2,1,0:T(8,128)(2,1)S(1)}, bf16[4,256,128]{2,1,0:T(8,128)(2,1)S(1)}, u32[]{:S(2)}, u32[]{:S(2)}) %collective-permute-start) | collective-permute-done | bytes 262176 | tf_op jit(solution)/shard_map/ppermute | solution.py:514
  12.1 6.2 %collective-permute-done.1.refs_2_ = bf16[4,256,128]{2,1,0:T(8,128)(2,1)S(1)} collective-permute-done((bf16[4,256,128]{2,1,0:T(8,128)(2,1)S(1)}, bf16[4,256,128]{2,1,0:T(8,128)(2,1)S(1)}, u32[]{:S(2)}, u32[]{:S(2)}) %collective-permute-start.1) | collective-permute-done | bytes 262176 | tf_op jit(solution)/shard_map/ppermute | solution.py:514
  18.4 0.0 collective-permute-done.2.refs_3_
  18.4 0.1 order.2.refs_5_
  18.5 1.6 %collective-permute-start.10 = (bf16[4,4,256,128]{3,2,1,0:T(8,128)(2,1)S(1)}, bf16[4,4,256,128]{3,2,1,0:T(8,128)(2,1)}, u32[]{:S(2)}, u32[]{:S(2)}) collective-permute-start(bf16[4,4,256,128]{3,2,1,0:T(8,128)(2,1)S(1)} %order.2.refs_5_), channel_id=1, source_target_pairs={{16,8},{8,16},{17,9},{9,17},{18,10},{10,18},{19,11},{11,19},{20,12... | collective-permute-start | bytes 3145736 | tf_op jit(solution)/shard_map/ppermute | solution.py:523
  20.1 3.5 %collective-permute-start.9 = (bf16[4,4,256,128]{3,2,1,0:T(8,128)(2,1)S(1)}, bf16[4,4,256,128]{3,2,1,0:T(8,128)(2,1)}, u32[]{:S(2)}, u32[]{:S(2)}) collective-permute-start(bf16[4,4,256,128]{3,2,1,0:T(8,128)(2,1)S(1)} %order.2.refs_5_), channel_id=1, source_target_pairs={{8,0},{24,16},{0,8},{16,24},{9,1},{25,17},{1,9},{17,25},{10,2},{26... | collective-permute-start | bytes 3145736 | tf_op jit(solution)/shard_map/ppermute | solution.py:523
  23.6 1.5 %collective-permute-start.5 = (bf16[2,256,128]{2,1,0:T(8,128)(2,1)}, bf16[2,256,128]{2,1,0:T(8,128)(2,1)}, u32[]{:S(2)}, u32[]{:S(2)}) collective-permute-start(bf16[2,256,128]{2,1,0:T(8,128)(2,1)} %get-tuple-element.70), channel_id=1, source_target_pairs={{0,4},{2,6},{4,0},{6,2},{1,5},{3,7},{5,1},{7,3},{8,12},{10,14},{12... | collective-permute-start | bytes 393224 | tf_op jit(solution)/shard_map/ppermute | solution.py:514
  25.1 1.2 %collective-permute-start.7 = (bf16[2,256,128]{2,1,0:T(8,128)(2,1)}, bf16[2,256,128]{2,1,0:T(8,128)(2,1)}, u32[]{:S(2)}, u32[]{:S(2)}) collective-permute-start(bf16[2,256,128]{2,1,0:T(8,128)(2,1)} %get-tuple-element.74), channel_id=1, source_target_pairs={{0,6},{2,4},{4,2},{6,0},{1,7},{3,5},{5,3},{7,1},{8,14},{10,12},{12... | collective-permute-start | bytes 393224 | tf_op jit(solution)/shard_map/ppermute | solution.py:514
  26.3 0.8 collective-permute-start.3
  27.1 0.1 reshape.30
  27.2 1.7 %copy.8 = bf16[2,128,2,1536]{3,1,0,2:T(8,128)(2,1)S(1)} copy(bf16[2,128,2,1536]{3,2,1,0:T(2,128)(2,1)} %param.8) | data formatting | bytes 3145728 | tf_op jit(solution)/shard_map/optimization_barrier | solution.py:542
  28.9 0.0 copy-start.6
  28.9 1.7 %pack_qr.2 = (bf16[1552,128]{1,0:T(8,128)(2,1)S(1)}, bf16[1552,128]{1,0:T(8,128)(2,1)}, bf16[1552,128]{1,0:T(8,128)(2,1)}, bf16[1552,128]{1,0:T(8,128)(2,1)}) custom-call(s32[1]{0:T(128)} %bitcast.1.me_ref, bf16[256,1536]{1,0:T(8,128)(2,1)S(1)} %bitcast.24, bf16[2,256,1536]{2,1,0:T(8,128)(2,1)S(1)} %bitcast.22, bf16[16,128]{1,0:T(8,128)(2,1)S(1)} %pad.5.f_ref), custom_call_target="tpu_custom_call" | custom-call | tf_op jit(solution)/shard_map/pack_qr/pallas_call | solution.py:395
  30.7 0.8 copy-done.3
  31.5 0.0 collective-permute-done.5.refs_2_
  31.5 0.0 collective-permute-done.7.refs_3_
  31.5 0.3 collective-permute-done.3.refs_1_
  31.8 1.2 %collective-permute-start.4 = (bf16[1552,128]{1,0:T(8,128)(2,1)}, bf16[1552,128]{1,0:T(8,128)(2,1)}, u32[]{:S(2)}, u32[]{:S(2)}) collective-permute-start(bf16[1552,128]{1,0:T(8,128)(2,1)} %get-tuple-element.67), channel_id=1, source_target_pairs={{0,2},{2,0},{4,6},{6,4},{1,3},{3,1},{5,7},{7,5},{8,10},{10,8},{12,... | collective-permute-start | bytes 1191944 | tf_op jit(solution)/shard_map/ppermute | solution.py:514
  33.0 2.7 %collective-permute-start.8 = (bf16[1552,128]{1,0:T(8,128)(2,1)}, bf16[1552,128]{1,0:T(8,128)(2,1)}, u32[]{:S(2)}, u32[]{:S(2)}) collective-permute-start(bf16[1552,128]{1,0:T(8,128)(2,1)} %get-tuple-element.75), channel_id=1, source_target_pairs={{0,6},{2,4},{4,2},{6,0},{1,7},{3,5},{5,3},{7,1},{8,14},{10,12},{12... | collective-permute-start | bytes 1191944 | tf_op jit(solution)/shard_map/ppermute | solution.py:514
  35.7 0.1 add_bitcast_fusion
  35.8 0.7 key_features.1.refs_8_
  36.5 0.0 copy-start.1
  36.5 0.9 %copy-done.1 = bf16[4,3,256,128]{3,2,1,0:T(8,128)(2,1)} copy-done((bf16[4,3,256,128]{3,2,1,0:T(8,128)(2,1)}, bf16[4,3,256,128]{3,2,1,0:T(8,128)(2,1)S(1)}, u32[]{:S(2)}) %copy-start.1) | copy-done | bytes 786456
  37.4 2.0 %order.3.refs_5_ = bf16[4,2,256,128]{3,2,1,0:T(8,128)(2,1)} custom-call(s32[1]{0:T(128)} %bitcast.1.me_ref, bf16[2,256,128]{2,1,0:T(8,128)(2,1)S(1)} %get-tuple-element.98.refs_0_, bf16[2,256,128]{2,1,0:T(8,128)(2,1)} %collective-permute-done.3.refs_1_, bf16[2,256,128]{2,1,0:T(8,128)(2,1)} %collective-permute-done.5.refs_2_, ...), custom_call_target="tpu_custom_call" | custom-call | tf_op jit(solution)/shard_map/order/pallas_call | solution.py:356
  39.4 0.0 collective-permute-done.10.refs_7_
  39.4 6.1 %collective-permute-done.9.refs_6_ = bf16[4,4,256,128]{3,2,1,0:T(8,128)(2,1)} collective-permute-done((bf16[4,4,256,128]{3,2,1,0:T(8,128)(2,1)S(1)}, bf16[4,4,256,128]{3,2,1,0:T(8,128)(2,1)}, u32[]{:S(2)}, u32[]{:S(2)}) %collective-permute-start.9) | collective-permute-done | bytes 1048608 | tf_op jit(solution)/shard_map/ppermute | solution.py:523
  45.5 1.5 %collective-permute-start.18 = (bf16[4,2,256,128]{3,2,1,0:T(8,128)(2,1)}, bf16[4,2,256,128]{3,2,1,0:T(8,128)(2,1)}, u32[]{:S(2)}, u32[]{:S(2)}) collective-permute-start(bf16[4,2,256,128]{3,2,1,0:T(8,128)(2,1)} %order.3.refs_5_), channel_id=1, source_target_pairs={{16,8},{8,16},{17,9},{9,17},{18,10},{10,18},{19,11},{11,19},{20,12... | collective-permute-start | bytes 1572872 | tf_op jit(solution)/shard_map/ppermute | solution.py:523
  47.0 2.9 %collective-permute-start.17 = (bf16[4,2,256,128]{3,2,1,0:T(8,128)(2,1)}, bf16[4,2,256,128]{3,2,1,0:T(8,128)(2,1)}, u32[]{:S(2)}, u32[]{:S(2)}) collective-permute-start(bf16[4,2,256,128]{3,2,1,0:T(8,128)(2,1)} %order.3.refs_5_), channel_id=1, source_target_pairs={{8,0},{24,16},{0,8},{16,24},{9,1},{25,17},{1,9},{17,25},{10,2},{26... | collective-permute-start | bytes 1572872 | tf_op jit(solution)/shard_map/ppermute | solution.py:523
  49.9 0.1 copy.9.ids_ref
  50.0 0.5 pack_qr.3
  50.5 0.0 collective-permute-done.4.refs_1_
  50.5 1.5 %collective-permute-start.14 = (bf16[768,128]{1,0:T(8,128)(2,1)S(1)}, bf16[768,128]{1,0:T(8,128)(2,1)S(1)}, u32[]{:S(2)}, u32[]{:S(2)}) collective-permute-start(bf16[768,128]{1,0:T(8,128)(2,1)S(1)} %get-tuple-element.92), channel_id=1, source_target_pairs={{0,2},{2,0},{4,6},{6,4},{1,3},{3,1},{5,7},{7,5},{8,10},{10,8},{12,... | collective-permute-start | bytes 589832 | tf_op jit(solution)/shard_map/ppermute | solution.py:514
  52.0 0.0 collective-permute-done.8.refs_3_
  52.0 0.5 collective-permute-start.16
  52.5 1.5 %collective-permute-start.15 = (bf16[768,128]{1,0:T(8,128)(2,1)S(1)}, bf16[768,128]{1,0:T(8,128)(2,1)S(1)}, u32[]{:S(2)}, u32[]{:S(2)}) collective-permute-start(bf16[768,128]{1,0:T(8,128)(2,1)S(1)} %get-tuple-element.94), channel_id=1, source_target_pairs={{0,4},{2,6},{4,0},{6,2},{1,5},{3,7},{5,1},{7,3},{8,12},{10,14},{12... | collective-permute-start | bytes 589832 | tf_op jit(solution)/shard_map/ppermute | solution.py:514
  54.1 0.9 %query_features.1.refs_4_ = bf16[4,256,128]{2,1,0:T(8,128)(2,1)S(1)} custom-call(s32[1]{0:T(128)} %bitcast.1.me_ref, bf16[1552,128]{1,0:T(8,128)(2,1)S(1)} %copy-done.4, bf16[1552,128]{1,0:T(8,128)(2,1)} %collective-permute-done.4.refs_1_, bf16[1552,128]{1,0:T(8,128)(2,1)} %collective-permute-done.6.refs_2_, bf16[1552,128]{1,0:T(8,128)(2,1)} %collective-permute-done.8.refs_3_), custom_call_target="tpu_custom_call" | custom-call | tf_op jit(solution)/shard_map/query_features/pallas_call | solution.py:283
  55.0 8.2 %attend.2 = (bf16[512,128]{1,0:T(8,128)(2,1)S(1)}, bf16[512,128]{1,0:T(8,128)(2,1)S(1)}, bf16[512,128]{1,0:T(8,128)(2,1)S(1)}, bf16[512,128]{1,0:T(8,128)(2,1)S(1)}) custom-call(s32[1]{0:T(128)} %bitcast.1.me_ref, s32[4,2]{1,0:T(4,128)S(1)} %copy.9.ids_ref, bf16[1552,128]{1,0:T(8,128)(2,1)S(1)} %copy-done.4, ...), custom_call_target="tpu_custom_call" | custom-call | flops 2952790016 | bytes 3145728 | tf_op jit(solution)/shard_map/attend/pallas_call | solution.py:235
  63.2 1.5 %collective-permute-start.11 = (bf16[512,128]{1,0:T(8,128)(2,1)S(1)}, bf16[512,128]{1,0:T(8,128)(2,1)S(1)}, u32[]{:S(2)}, u32[]{:S(2)}) collective-permute-start(bf16[512,128]{1,0:T(8,128)(2,1)S(1)} %get-tuple-element.82), channel_id=1, source_target_pairs={{0,2},{2,0},{4,6},{6,4},{1,3},{3,1},{5,7},{7,5},{8,10},{10,8},{12,... | collective-permute-start | bytes 393224 | tf_op jit(solution)/shard_map/ppermute | solution.py:514
  64.7 0.0 collective-permute-done.16.refs_3_
  64.8 0.6 collective-permute-start.12
  65.3 0.0 collective-permute-done.15.refs_2_
  65.3 1.5 %collective-permute-start.13 = (bf16[512,128]{1,0:T(8,128)(2,1)S(1)}, bf16[512,128]{1,0:T(8,128)(2,1)S(1)}, u32[]{:S(2)}, u32[]{:S(2)}) collective-permute-start(bf16[512,128]{1,0:T(8,128)(2,1)S(1)} %get-tuple-element.84), channel_id=1, source_target_pairs={{0,6},{2,4},{4,2},{6,0},{1,7},{3,5},{5,3},{7,1},{8,14},{10,12},{12... | collective-permute-start | bytes 393224 | tf_op jit(solution)/shard_map/ppermute | solution.py:514
  66.8 0.0 collective-permute-done.18.refs_7_
  66.8 0.0 collective-permute-done.17.refs_6_
  66.8 4.8 %attend.3 = (bf16[256,128]{1,0:T(8,128)(2,1)S(1)}, bf16[256,128]{1,0:T(8,128)(2,1)S(1)}, bf16[256,128]{1,0:T(8,128)(2,1)S(1)}, bf16[256,128]{1,0:T(8,128)(2,1)S(1)}) custom-call(s32[1]{0:T(128)} %bitcast.1.me_ref, s32[4,2]{1,0:T(4,128)S(1)} %copy.9.ids_ref, bf16[768,128]{1,0:T(8,128)(2,1)S(1)} %get-tuple-element.90.refs_0_, ...), custom_call_target="tpu_custom_call" | custom-call | flops 1476395008 | bytes 1572864 | tf_op jit(solution)/shard_map/attend/pallas_call | solution.py:235
  71.6 1.5 %collective-permute-start.19 = (bf16[256,128]{1,0:T(8,128)(2,1)S(1)}, bf16[256,128]{1,0:T(8,128)(2,1)S(1)}, u32[]{:S(2)}, u32[]{:S(2)}) collective-permute-start(bf16[256,128]{1,0:T(8,128)(2,1)S(1)} %get-tuple-element.104), channel_id=1, source_target_pairs={{0,2},{2,0},{4,6},{6,4},{1,3},{3,1},{5,7},{7,5},{8,10},{10,8},{12,... | collective-permute-start | bytes 196616 | tf_op jit(solution)/shard_map/ppermute | solution.py:514
  73.1 0.5 collective-permute-start.20
  73.7 0.0 collective-permute-done.11.refs_1_
  73.7 1.5 %collective-permute-start.21 = (bf16[256,128]{1,0:T(8,128)(2,1)S(1)}, bf16[256,128]{1,0:T(8,128)(2,1)S(1)}, u32[]{:S(2)}, u32[]{:S(2)}) collective-permute-start(bf16[256,128]{1,0:T(8,128)(2,1)S(1)} %get-tuple-element.106), channel_id=1, source_target_pairs={{0,6},{2,4},{4,2},{6,0},{1,7},{3,5},{5,3},{7,1},{8,14},{10,12},{12... | collective-permute-start | bytes 196616 | tf_op jit(solution)/shard_map/ppermute | solution.py:514
  75.1 0.0 collective-permute-done.12.refs_2_
  75.2 4.2 %project_early.1 = (f32[2,256,1536]{2,1,0:T(8,128)S(1)}, bf16[4,128,3072]{2,1,0:T(8,128)(2,1)S(1)}) custom-call(s32[1]{0:T(128)} %bitcast.1.me_ref, bf16[1536,3072]{1,0:T(8,128)(2,1)} %w_hbm.1, bf16[512,128]{1,0:T(8,128)(2,1)S(1)} %get-tuple-element.81.refs_0_, bf16[512,128]{1,0:T(8,128)(2,1)S(1)} %collective-permute-done.11.refs_1_, ...), custom_call_target="tpu_custom_call" | custom-call | tf_op jit(solution)/shard_map/project_early/pallas_call | solution.py:451
  79.3 0.0 collective-permute-done.19.refs_1_
  79.3 0.0 collective-permute-done.20.refs_2_
  79.4 1.0 %project.3 = bf16[256,1536]{1,0:T(8,128)(2,1)S(1)} custom-call(s32[1]{0:T(128)} %bitcast.16.which_ref, bf16[4,128,3072]{2,1,0:T(8,128)(2,1)S(1)} %get-tuple-element.85.w_ref, f32[2,256,1536]{2,1,0:T(8,128)S(1)} %get-tuple-element.86.early_ref, bf16[256,128]{1,0:T(8,128)(2,1)S(1)} %get-tuple-element.103.refs_0_, ...), custom_call_target="tpu_custom_call" | custom-call | tf_op jit(solution)/shard_map/project/pallas_call | solution.py:484
  80.3 0.1 collective-permute-start.22
  80.4 1.0 %project.2 = bf16[256,1536]{1,0:T(8,128)(2,1)S(1)} custom-call(s32[1]{0:T(128)} %bitcast.which_ref, bf16[4,128,3072]{2,1,0:T(8,128)(2,1)S(1)} %get-tuple-element.85.w_ref, f32[2,256,1536]{2,1,0:T(8,128)S(1)} %get-tuple-element.86.early_ref, bf16[256,128]{1,0:T(8,128)(2,1)S(1)} %get-tuple-element.103.refs_0_, ...), custom_call_target="tpu_custom_call" | custom-call | tf_op jit(solution)/shard_map/project/pallas_call | solution.py:484
  81.4 1.3 %collective-permute-done.22 = bf16[256,1536]{1,0:T(8,128)(2,1)S(1)} collective-permute-done((bf16[256,1536]{1,0:T(8,128)(2,1)S(1)}, bf16[256,1536]{1,0:T(8,128)(2,1)S(1)}, u32[]{:S(2)}, u32[]{:S(2)}) %collective-permute-start.22) | collective-permute-done | bytes 786464 | tf_op jit(solution)/shard_map/ppermute | solution.py:570
  82.7 1.1 %add_convert_fusion = bf16[256,1536]{1,0:T(8,128)(2,1)} fusion(bf16[256,1536]{1,0:T(8,128)(2,1)S(1)} %collective-permute-done.22, bf16[256,1536]{1,0:T(8,128)(2,1)S(1)} %project.2), kind=kLoop, calls=%fused_computation | loop fusion | flops 1572864 | bytes 2359296 | tf_op jit(solution)/shard_map/convert_element_type | solution.py:573
  (18 shorter events, 0.1 us)
Async XLA Ops:
  2.0 10.1 %collective-permute-start = (bf16[4,256,128]{2,1,0:T(8,128)(2,1)S(1)}, bf16[4,256,128]{2,1,0:T(8,128)(2,1)S(1)}, u32[]{:S(2)}, u32[]{:S(2)}) collective-permute-start(bf16[4,256,128]{2,1,0:T(8,128)(2,1)S(1)} %get-tuple-element.57), channel_id=1, source_target_pairs={{0,2},{2,0},{4,6},{6,4},{1,3},{3,1},{5,7},{7,5},{8,10},{10,8},{12,... | collective-permute-start | bytes 786440 | tf_op jit(solution)/shard_map/ppermute | solution.py:514
  5.0 13.4 %collective-permute-start.1 = (bf16[4,256,128]{2,1,0:T(8,128)(2,1)S(1)}, bf16[4,256,128]{2,1,0:T(8,128)(2,1)S(1)}, u32[]{:S(2)}, u32[]{:S(2)}) collective-permute-start(bf16[4,256,128]{2,1,0:T(8,128)(2,1)S(1)} %get-tuple-element.58), channel_id=1, source_target_pairs={{0,4},{2,6},{4,0},{6,2},{1,5},{3,7},{5,1},{7,3},{8,12},{10,14},{12... | collective-permute-start | bytes 786440 | tf_op jit(solution)/shard_map/ppermute | solution.py:514
  6.5 11.9 %collective-permute-start.2 = (bf16[4,256,128]{2,1,0:T(8,128)(2,1)S(1)}, bf16[4,256,128]{2,1,0:T(8,128)(2,1)S(1)}, u32[]{:S(2)}, u32[]{:S(2)}) collective-permute-start(bf16[4,256,128]{2,1,0:T(8,128)(2,1)S(1)} %get-tuple-element.59), channel_id=1, source_target_pairs={{0,6},{2,4},{4,2},{6,0},{1,7},{3,5},{5,3},{7,1},{8,14},{10,12},{12... | collective-permute-start | bytes 786440 | tf_op jit(solution)/shard_map/ppermute | solution.py:514
  6.5 20.6 %copy-start.5 = (s32[16,16]{1,0:T(8,128)S(1)}, s32[16,16]{1,0:T(8,128)}, u32[]{:S(2)}) copy-start(s32[16,16]{1,0:T(8,128)} %param.10) | copy-start | bytes 3076
  18.5 20.9 %collective-permute-start.10 = (bf16[4,4,256,128]{3,2,1,0:T(8,128)(2,1)S(1)}, bf16[4,4,256,128]{3,2,1,0:T(8,128)(2,1)}, u32[]{:S(2)}, u32[]{:S(2)}) collective-permute-start(bf16[4,4,256,128]{3,2,1,0:T(8,128)(2,1)S(1)} %order.2.refs_5_), channel_id=1, source_target_pairs={{16,8},{8,16},{17,9},{9,17},{18,10},{10,18},{19,11},{11,19},{20,12... | collective-permute-start | bytes 3145736 | tf_op jit(solution)/shard_map/ppermute | solution.py:523
  20.1 25.4 %collective-permute-start.9 = (bf16[4,4,256,128]{3,2,1,0:T(8,128)(2,1)S(1)}, bf16[4,4,256,128]{3,2,1,0:T(8,128)(2,1)}, u32[]{:S(2)}, u32[]{:S(2)}) collective-permute-start(bf16[4,4,256,128]{3,2,1,0:T(8,128)(2,1)S(1)} %order.2.refs_5_), channel_id=1, source_target_pairs={{8,0},{24,16},{0,8},{16,24},{9,1},{25,17},{1,9},{17,25},{10,2},{26... | collective-permute-start | bytes 3145736 | tf_op jit(solution)/shard_map/ppermute | solution.py:523
  23.6 7.8 %collective-permute-start.5 = (bf16[2,256,128]{2,1,0:T(8,128)(2,1)}, bf16[2,256,128]{2,1,0:T(8,128)(2,1)}, u32[]{:S(2)}, u32[]{:S(2)}) collective-permute-start(bf16[2,256,128]{2,1,0:T(8,128)(2,1)} %get-tuple-element.70), channel_id=1, source_target_pairs={{0,4},{2,6},{4,0},{6,2},{1,5},{3,7},{5,1},{7,3},{8,12},{10,14},{12... | collective-permute-start | bytes 393224 | tf_op jit(solution)/shard_map/ppermute | solution.py:514
  25.1 6.3 %collective-permute-start.7 = (bf16[2,256,128]{2,1,0:T(8,128)(2,1)}, bf16[2,256,128]{2,1,0:T(8,128)(2,1)}, u32[]{:S(2)}, u32[]{:S(2)}) collective-permute-start(bf16[2,256,128]{2,1,0:T(8,128)(2,1)} %get-tuple-element.74), channel_id=1, source_target_pairs={{0,6},{2,4},{4,2},{6,0},{1,7},{3,5},{5,3},{7,1},{8,14},{10,12},{12... | collective-permute-start | bytes 393224 | tf_op jit(solution)/shard_map/ppermute | solution.py:514
  26.3 5.5 %collective-permute-start.3 = (bf16[2,256,128]{2,1,0:T(8,128)(2,1)}, bf16[2,256,128]{2,1,0:T(8,128)(2,1)}, u32[]{:S(2)}, u32[]{:S(2)}) collective-permute-start(bf16[2,256,128]{2,1,0:T(8,128)(2,1)} %get-tuple-element.66), channel_id=1, source_target_pairs={{0,2},{2,0},{4,6},{6,4},{1,3},{3,1},{5,7},{7,5},{8,10},{10,8},{12,... | collective-permute-start | bytes 393224 | tf_op jit(solution)/shard_map/ppermute | solution.py:514
  27.2 1.7 %copy-start = (bf16[16,16,1536]{2,1,0:T(8,128)(2,1)S(1)}, bf16[16,16,1536]{2,1,0:T(8,128)(2,1)}, u32[]{:S(2)}) copy-start(bf16[16,16,1536]{2,1,0:T(8,128)(2,1)} %param.6) | copy-start | bytes 2359300
  28.9 21.0 %copy-start.6 = (s32[1,4,2]{1,2,0:T(2,128)S(1)}, s32[1,4,2]{1,2,0:T(2,128)}, u32[]{:S(2)}) copy-start(s32[1,4,2]{1,2,0:T(2,128)} %param.9) | copy-start | bytes 100
  30.7 0.8 copy-start.3
  31.8 18.7 %collective-permute-start.4 = (bf16[1552,128]{1,0:T(8,128)(2,1)}, bf16[1552,128]{1,0:T(8,128)(2,1)}, u32[]{:S(2)}, u32[]{:S(2)}) collective-permute-start(bf16[1552,128]{1,0:T(8,128)(2,1)} %get-tuple-element.67), channel_id=1, source_target_pairs={{0,2},{2,0},{4,6},{6,4},{1,3},{3,1},{5,7},{7,5},{8,10},{10,8},{12,... | collective-permute-start | bytes 1191944 | tf_op jit(solution)/shard_map/ppermute | solution.py:514
  33.0 19.0 %collective-permute-start.8 = (bf16[1552,128]{1,0:T(8,128)(2,1)}, bf16[1552,128]{1,0:T(8,128)(2,1)}, u32[]{:S(2)}, u32[]{:S(2)}) collective-permute-start(bf16[1552,128]{1,0:T(8,128)(2,1)} %get-tuple-element.75), channel_id=1, source_target_pairs={{0,6},{2,4},{4,2},{6,0},{1,7},{3,5},{5,3},{7,1},{8,14},{10,12},{12... | collective-permute-start | bytes 1191944 | tf_op jit(solution)/shard_map/ppermute | solution.py:514
  35.7 16.9 %collective-permute-start.6 = (bf16[1552,128]{1,0:T(8,128)(2,1)}, bf16[1552,128]{1,0:T(8,128)(2,1)}, u32[]{:S(2)}, u32[]{:S(2)}) collective-permute-start(bf16[1552,128]{1,0:T(8,128)(2,1)} %get-tuple-element.71), channel_id=1, source_target_pairs={{0,4},{2,6},{4,0},{6,2},{1,5},{3,7},{5,1},{7,3},{8,12},{10,14},{12... | collective-permute-start | bytes 1191944 | tf_op jit(solution)/shard_map/ppermute | solution.py:514
  36.5 0.9 %copy-start.1 = (bf16[4,3,256,128]{3,2,1,0:T(8,128)(2,1)}, bf16[4,3,256,128]{3,2,1,0:T(8,128)(2,1)S(1)}, u32[]{:S(2)}) copy-start(bf16[4,3,256,128]{3,2,1,0:T(8,128)(2,1)S(1)} %key_features.1.refs_8_) | copy-start | bytes 2359300
  45.5 21.3 %collective-permute-start.18 = (bf16[4,2,256,128]{3,2,1,0:T(8,128)(2,1)}, bf16[4,2,256,128]{3,2,1,0:T(8,128)(2,1)}, u32[]{:S(2)}, u32[]{:S(2)}) collective-permute-start(bf16[4,2,256,128]{3,2,1,0:T(8,128)(2,1)} %order.3.refs_5_), channel_id=1, source_target_pairs={{16,8},{8,16},{17,9},{9,17},{18,10},{10,18},{19,11},{11,19},{20,12... | collective-permute-start | bytes 1572872 | tf_op jit(solution)/shard_map/ppermute | solution.py:523
  47.0 19.8 %collective-permute-start.17 = (bf16[4,2,256,128]{3,2,1,0:T(8,128)(2,1)}, bf16[4,2,256,128]{3,2,1,0:T(8,128)(2,1)}, u32[]{:S(2)}, u32[]{:S(2)}) collective-permute-start(bf16[4,2,256,128]{3,2,1,0:T(8,128)(2,1)} %order.3.refs_5_), channel_id=1, source_target_pairs={{8,0},{24,16},{0,8},{16,24},{9,1},{25,17},{1,9},{17,25},{10,2},{26... | collective-permute-start | bytes 1572872 | tf_op jit(solution)/shard_map/ppermute | solution.py:523
  50.0 4.1 %copy-start.4 = (bf16[1552,128]{1,0:T(8,128)(2,1)S(1)}, bf16[1552,128]{1,0:T(8,128)(2,1)}, u32[]{:S(2)}) copy-start(bf16[1552,128]{1,0:T(8,128)(2,1)} %copy-done.3) | copy-start | bytes 1191940
  50.0 5.1 %copy-start.2 = (bf16[4,3,256,128]{3,2,1,0:T(8,128)(2,1)S(1)}, bf16[4,3,256,128]{3,2,1,0:T(8,128)(2,1)}, u32[]{:S(2)}) copy-start(bf16[4,3,256,128]{3,2,1,0:T(8,128)(2,1)} %copy-done.1) | copy-start | bytes 2359300
  50.5 12.7 %collective-permute-start.14 = (bf16[768,128]{1,0:T(8,128)(2,1)S(1)}, bf16[768,128]{1,0:T(8,128)(2,1)S(1)}, u32[]{:S(2)}, u32[]{:S(2)}) collective-permute-start(bf16[768,128]{1,0:T(8,128)(2,1)S(1)} %get-tuple-element.92), channel_id=1, source_target_pairs={{0,2},{2,0},{4,6},{6,4},{1,3},{3,1},{5,7},{7,5},{8,10},{10,8},{12,... | collective-permute-start | bytes 589832 | tf_op jit(solution)/shard_map/ppermute | solution.py:514
  52.0 12.7 %collective-permute-start.16 = (bf16[768,128]{1,0:T(8,128)(2,1)S(1)}, bf16[768,128]{1,0:T(8,128)(2,1)S(1)}, u32[]{:S(2)}, u32[]{:S(2)}) collective-permute-start(bf16[768,128]{1,0:T(8,128)(2,1)S(1)} %get-tuple-element.96), channel_id=1, source_target_pairs={{0,6},{2,4},{4,2},{6,0},{1,7},{3,5},{5,3},{7,1},{8,14},{10,12},{12... | collective-permute-start | bytes 589832 | tf_op jit(solution)/shard_map/ppermute | solution.py:514
  52.5 12.8 %collective-permute-start.15 = (bf16[768,128]{1,0:T(8,128)(2,1)S(1)}, bf16[768,128]{1,0:T(8,128)(2,1)S(1)}, u32[]{:S(2)}, u32[]{:S(2)}) collective-permute-start(bf16[768,128]{1,0:T(8,128)(2,1)S(1)} %get-tuple-element.94), channel_id=1, source_target_pairs={{0,4},{2,6},{4,0},{6,2},{1,5},{3,7},{5,1},{7,3},{8,12},{10,14},{12... | collective-permute-start | bytes 589832 | tf_op jit(solution)/shard_map/ppermute | solution.py:514
  63.2 10.4 %collective-permute-start.11 = (bf16[512,128]{1,0:T(8,128)(2,1)S(1)}, bf16[512,128]{1,0:T(8,128)(2,1)S(1)}, u32[]{:S(2)}, u32[]{:S(2)}) collective-permute-start(bf16[512,128]{1,0:T(8,128)(2,1)S(1)} %get-tuple-element.82), channel_id=1, source_target_pairs={{0,2},{2,0},{4,6},{6,4},{1,3},{3,1},{5,7},{7,5},{8,10},{10,8},{12,... | collective-permute-start | bytes 393224 | tf_op jit(solution)/shard_map/ppermute | solution.py:514
  64.8 10.4 %collective-permute-start.12 = (bf16[512,128]{1,0:T(8,128)(2,1)S(1)}, bf16[512,128]{1,0:T(8,128)(2,1)S(1)}, u32[]{:S(2)}, u32[]{:S(2)}) collective-permute-start(bf16[512,128]{1,0:T(8,128)(2,1)S(1)} %get-tuple-element.83), channel_id=1, source_target_pairs={{0,4},{2,6},{4,0},{6,2},{1,5},{3,7},{5,1},{7,3},{8,12},{10,14},{12... | collective-permute-start | bytes 393224 | tf_op jit(solution)/shard_map/ppermute | solution.py:514
  65.3 9.8 %collective-permute-start.13 = (bf16[512,128]{1,0:T(8,128)(2,1)S(1)}, bf16[512,128]{1,0:T(8,128)(2,1)S(1)}, u32[]{:S(2)}, u32[]{:S(2)}) collective-permute-start(bf16[512,128]{1,0:T(8,128)(2,1)S(1)} %get-tuple-element.84), channel_id=1, source_target_pairs={{0,6},{2,4},{4,2},{6,0},{1,7},{3,5},{5,3},{7,1},{8,14},{10,12},{12... | collective-permute-start | bytes 393224 | tf_op jit(solution)/shard_map/ppermute | solution.py:514
  71.6 7.7 %collective-permute-start.19 = (bf16[256,128]{1,0:T(8,128)(2,1)S(1)}, bf16[256,128]{1,0:T(8,128)(2,1)S(1)}, u32[]{:S(2)}, u32[]{:S(2)}) collective-permute-start(bf16[256,128]{1,0:T(8,128)(2,1)S(1)} %get-tuple-element.104), channel_id=1, source_target_pairs={{0,2},{2,0},{4,6},{6,4},{1,3},{3,1},{5,7},{7,5},{8,10},{10,8},{12,... | collective-permute-start | bytes 196616 | tf_op jit(solution)/shard_map/ppermute | solution.py:514
  73.1 6.2 %collective-permute-start.20 = (bf16[256,128]{1,0:T(8,128)(2,1)S(1)}, bf16[256,128]{1,0:T(8,128)(2,1)S(1)}, u32[]{:S(2)}, u32[]{:S(2)}) collective-permute-start(bf16[256,128]{1,0:T(8,128)(2,1)S(1)} %get-tuple-element.105), channel_id=1, source_target_pairs={{0,4},{2,6},{4,0},{6,2},{1,5},{3,7},{5,1},{7,3},{8,12},{10,14},{12... | collective-permute-start | bytes 196616 | tf_op jit(solution)/shard_map/ppermute | solution.py:514
  73.7 5.7 %collective-permute-start.21 = (bf16[256,128]{1,0:T(8,128)(2,1)S(1)}, bf16[256,128]{1,0:T(8,128)(2,1)S(1)}, u32[]{:S(2)}, u32[]{:S(2)}) collective-permute-start(bf16[256,128]{1,0:T(8,128)(2,1)S(1)} %get-tuple-element.106), channel_id=1, source_target_pairs={{0,6},{2,4},{4,2},{6,0},{1,7},{3,5},{5,3},{7,1},{8,14},{10,12},{12... | collective-permute-start | bytes 196616 | tf_op jit(solution)/shard_map/ppermute | solution.py:514
  80.3 2.4 %collective-permute-start.22 = (bf16[256,1536]{1,0:T(8,128)(2,1)S(1)}, bf16[256,1536]{1,0:T(8,128)(2,1)S(1)}, u32[]{:S(2)}, u32[]{:S(2)}) collective-permute-start(bf16[256,1536]{1,0:T(8,128)(2,1)S(1)} %project.3), channel_id=1, source_target_pairs={{0,1},{1,0},{2,3},{3,2},{4,5},{5,4},{6,7},{7,6},{8,9},{9,8},{10,11... | collective-permute-start | bytes 2359304 | tf_op jit(solution)/shard_map/ppermute | solution.py:570
